TPU v7x, 32 devices: a whole 2x2x4 slice. The times are simulated.
32 devices in a mesh: dom: 8 (over z, x), line: 4 (over y, core).
Axes of the slice: x: 2, y: 2, z: 4, core: 2. Of those that a mesh axis runs over, the one named last changes fastest.
Arguments:
- right_side: float32 [64, 4096], P(None, ('dom', 'line')), may hold values from -18 to 18
- diag_blocks: bfloat16 [64, 64, 4096], P(None, None, ('dom', 'line')), may hold values from -0.5 to 3.5
- lower_blocks: bfloat16 [64, 64, 4096], P(None, None, ('dom', 'line')), may hold values from -0.375 to 0.375
- upper_blocks: bfloat16 [64, 64, 4096], P(None, None, ('dom', 'line')), may hold values from -0.375 to 0.375
- face_blocks: bfloat16 [4, 64, 64, 4096], P(None, None, None, ('dom', 'line')), may hold values from -0.75 to 0.75
- face_nbr: int32 [4, 4096], P(None, ('dom', 'line')), may hold values from 0 to 160, as said below
- send_list: int32 [2, 512], P(None, ('dom', 'line')), may hold values from 0 to 127
- inv_blocks: bfloat16 [64, 64, 4096], P(None, None, ('dom', 'line')), may hold values from -0.75 to 0.75
- fwd_blocks: bfloat16 [64, 64, 4096], P(None, None, ('dom', 'line')), may hold values from -0.625 to 0.625
- bwd_blocks: bfloat16 [64, 64, 4096], P(None, None, ('dom', 'line')), may hold values from -0.625 to 0.625
Outputs:
- update: float32 [64, 4096], P(None, ('dom', 'line'))
- hessenberg: float32 [4, 3], replicated
Inputs may be any that keep to these rules, and one draw needn't show every extreme that they name: `face_nbr`: slots 128 to 159 name values received from the neighbouring partitions and slot 160 is the zero slot.
All inputs are finite; a program needn't handle non-finite values.
Results may differ from a plain program's by a relative error of at most 0.015.
Values may be sent and summed in bfloat16 or wider, within the bound.
No kernel may reach another device: no remote copies, remote signals or barrier semaphores. Data moves between devices by JAX's collectives and lax.ppermute only.
A program may use at most 64 MiB of HBM per device.

v0:
```python
import functools

import jax
import jax.numpy as jnp
from jax import lax
from jax.experimental import pallas as pl
from jax.experimental.pallas import tpu as pltpu
from jax.sharding import PartitionSpec as P

ITERS = 3
LINES_DEV = 16
SUB = 8
MIB = 1 << 20
HIGHEST = lax.Precision.HIGHEST
F32 = jnp.float32
BF16 = jnp.bfloat16


def lanes_of(shape):
    return lax.broadcasted_iota(jnp.int32, shape, 1)


def fold_sublanes(parts):
    row = lax.broadcasted_iota(jnp.int32, parts[0].shape, 0)
    step = SUB // 2
    while step:
        mask = (row & step) == 0
        folded = []
        for a in range(step):
            low, high = parts[a], parts[a + step]
            if step == SUB // 2:
                kept = jnp.where(mask, low, high)
                folded.append(kept + pltpu.roll(jnp.where(mask, high, low), step, 0))
            else:
                low = low + pltpu.roll(low, SUB - step, 0)
                high = high + pltpu.roll(high, step, 0)
                folded.append(jnp.where(mask, low, high))
        parts = folded
        step //= 2
    return parts[0]


def spread_groups(packed, width):
    total = packed.shape[1]
    group = lanes_of(packed.shape) // width
    step = total // width // 2
    arrays = [packed]
    while step:
        clear = (group & step) == 0
        grown = []
        for item in arrays:
            moved = pltpu.roll(item, step * width, 1)
            grown.append(jnp.where(clear, item, moved))
            grown.append(jnp.where(clear, moved, item))
        arrays = grown
        step //= 2
    return arrays


def swap_groups(arrays, width):
    count = len(arrays)
    total = arrays[0].shape[1]
    group = lanes_of(arrays[0].shape) // width
    arrays = list(arrays)
    step = count // 2
    while step:
        clear = (group & step) == 0
        for a in range(count):
            if a & step == 0:
                low, high = arrays[a], arrays[a + step]
                arrays[a] = jnp.where(clear, low, pltpu.roll(high, step * width, 1))
                arrays[a + step] = jnp.where(clear, pltpu.roll(low, total - step * width, 1), high)
        step //= 2
    return arrays


def group_zero(arrays, width):
    group = lanes_of(arrays[0].shape) // width
    packed = arrays[0]
    for g in range(1, len(arrays)):
        packed = jnp.where(group == g, pltpu.roll(arrays[g], g * width, 1), packed)
    return packed


def rows_of(array):
    return [array[SUB * g : SUB * (g + 1)] for g in range(array.shape[0] // SUB)]


def packed_product(blocks, packed, width):
    spread = spread_groups(packed, width)
    parts = []
    for il in range(SUB):
        rows = rows_of(blocks(il).astype(F32))
        terms = [rows[g] * spread[g] for g in range(len(rows))]
        while len(terms) > 1:
            terms = [terms[t] + terms[t + 1] for t in range(0, len(terms), 2)]
        parts.append(terms[0])
    return fold_sublanes(parts)


def block_rows(reads, vectors):
    parts = []
    for i in range(SUB):
        total = None
        for read, vector in zip(reads, vectors):
            rows = rows_of(read(i).astype(F32))
            for row, entry in zip(rows, vector):
                term = row * entry
                total = term if total is None else total + term
        parts.append(total)
    return fold_sublanes(parts)


def swap_sublanes(arrays):
    row = lax.broadcasted_iota(jnp.int32, arrays[0].shape, 0)
    arrays = list(arrays)
    step = SUB // 2
    while step:
        clear = (row & step) == 0
        for a in range(SUB):
            if a & step == 0:
                low, high = arrays[a], arrays[a + step]
                arrays[a] = jnp.where(clear, low, pltpu.roll(high, step, 0))
                arrays[a + step] = jnp.where(clear, pltpu.roll(low, SUB - step, 0), high)
        step //= 2
    return arrays


def steps_kernel(width, fwd, bwd, fwd_steps, bwd_steps, last):
    size, _, elements = fwd.shape
    positions = elements // width
    pack = 2 * SUB
    split = size // pack

    @pl.loop(0, SUB * split)
    def _(n):
        il = n // split
        at = pl.multiple_of((n % split) * pack, pack)
        for blocks, steps in ((fwd, fwd_steps), (bwd, bwd_steps)):
            arrays = [
                -blocks[ih * SUB + il, pl.ds(at, pack), :].astype(F32) for ih in range(size // SUB)
            ]
            arrays = swap_groups(arrays, width)
            for q in range(positions):
                steps[q, il, pl.ds(at, pack), :] = arrays[q].astype(BF16)
            if steps is bwd_steps:
                last[il, pl.ds(at, pack), :] = arrays[-1].astype(BF16)


def step_layouts(fwd, bwd, width):
    size, _, elements = fwd.shape
    steps = jax.ShapeDtypeStruct((elements // width, SUB, size, elements), BF16)
    return pl.pallas_call(
        functools.partial(steps_kernel, width),
        out_shape=(steps, steps, jax.ShapeDtypeStruct((SUB, size, elements), BF16)),
        name="step_layouts",
        compiler_params=pltpu.CompilerParams(vmem_limit_bytes=10 * MIB),
        cost_estimate=pl.CostEstimate(flops=4000000, bytes_accessed=8 * MIB, transcendentals=0),
    )(fwd, bwd)


def chain_kernel(width, fwd, bwd, response, ends, tiles, chain):
    size, _, elements = fwd.shape
    positions = elements // width
    half = lanes_of((size, elements)) < size

    @pl.loop(0, size // SUB)
    def _(n):
        turned = []
        for il in range(SUB):
            both = jnp.concatenate(
                [fwd[n * SUB + il].astype(F32), bwd[n * SUB + il].astype(F32)], axis=0
            )
            turned.append(-both.T)
        for g in range(elements // SUB):
            rows = swap_sublanes([t[g * SUB : (g + 1) * SUB] for t in turned])
            for a in range(SUB):
                tiles[pl.ds((g * SUB + a) * size + n * SUB, SUB), :] = rows[a]

    def tile(e):
        return tiles[pl.ds(pl.multiple_of(e * size, size), size), :]

    def split(value):
        high = value.astype(BF16)
        return high, (value - high.astype(F32)).astype(BF16)

    zeros = jnp.zeros((size, 2 * elements), BF16)
    for line in range(width):
        first = tile(line)
        chain[pl.ds(line * size, size), :] = jnp.where(half, first, pltpu.roll(first, size, 1))

    @pl.loop(1, positions)
    def _(q):
        for line in range(width):
            e = q * width + line
            before = chain[pl.ds(pl.multiple_of((e - width) * size, size), size), :]
            high, low = split(before)
            right = jnp.where(half, high, low)
            out = jnp.dot(tile(e)[:, :size].astype(BF16), right, preferred_element_type=F32)
            chain[pl.ds(pl.multiple_of(e * size, size), size), :] = out + pltpu.roll(out, size, 1)

    last = positions - 1
    paired = width // 2
    for line in range(paired):
        e = last * width + line
        one = chain[pl.ds(e * size, size), :]
        two = chain[pl.ds((e + paired) * size, size), :]
        ends[line] = jnp.where(half, one, two)
    for line in range(width):
        e = last * width + line
        chain[pl.ds(e * size, size), :] = jnp.where(half, chain[pl.ds(e * size, size), :], tile(e))

    @pl.loop(0, last)
    def _(n):
        q = last - 1 - n
        for line in range(width):
            e = q * width + line
            after = chain[pl.ds(pl.multiple_of((e + width) * size, size), size), :]
            high, low = split(after)
            right = jnp.concatenate([zeros, jnp.concatenate([high, low], axis=1)], axis=0)
            out = jnp.dot(tile(e).astype(BF16), right, preferred_element_type=F32)
            own = chain[pl.ds(pl.multiple_of(e * size, size), size), :]
            chain[pl.ds(pl.multiple_of(e * size, size), size), :] = (
                jnp.where(half, own, 0.0) + out[:, :elements] + out[:, elements:]
            )

    for line in range(width):
        ends[paired + line] = chain[pl.ds(line * size, size), :]

    @pl.loop(0, size // SUB)
    def _(n):
        groups = []
        for g in range(elements // SUB):
            groups.append(
                swap_sublanes(
                    [chain[pl.ds((g * SUB + a) * size + n * SUB, SUB), :] for a in range(SUB)]
                )
            )
        for il in range(SUB):
            response[n * SUB + il] = jnp.concatenate([rows[il] for rows in groups], axis=0).T


def chain_products(fwd, bwd, width):
    size, _, elements = fwd.shape
    return pl.pallas_call(
        functools.partial(chain_kernel, width),
        out_shape=(
            jax.ShapeDtypeStruct((size, 2 * size, elements), F32),
            jax.ShapeDtypeStruct((width + width // 2, size, elements), F32),
        ),
        scratch_shapes=[
            pltpu.VMEM((elements * size, elements), F32),
            pltpu.VMEM((elements * size, elements), F32),
        ],
        name="chain_products",
        compiler_params=pltpu.CompilerParams(vmem_limit_bytes=20 * MIB),
        cost_estimate=pl.CostEstimate(flops=40000000, bytes_accessed=12 * MIB, transcendentals=0),
    )(fwd, bwd)


def maps_kernel(width, own, other, through_low, through_high, reach_high, back_low, back_high, pair):
    size = own.shape[1]
    elements = own.shape[2]
    is_odd = lax.axis_index("line") % 2 == 1
    half = lanes_of((size, elements)) < size
    paired = width // 2

    def through(line, which):
        both = which(line % paired)
        turned = pltpu.roll(both, size, 1)
        return (both, turned) if line < paired else (turned, both)

    def low(n):
        return jnp.where(is_odd, other[n], own[n])

    def high(n):
        return jnp.where(is_odd, own[n], other[n])

    def pack(tile, outs):
        groups = []
        for ih in range(size // SUB):
            for lh in range(width // SUB):
                groups.append(
                    swap_sublanes(
                        [tile(lh * SUB + a)[ih * SUB : (ih + 1) * SUB] for a in range(SUB)]
                    )
                )
        for il in range(SUB):
            turned = jnp.concatenate([rows[il] for rows in groups], axis=0).T
            for n, out in enumerate(outs):
                out[il] = turned[n * size : (n + 1) * size]

    def joined(line):
        left, right = through(line, low)
        both = jnp.where(half, left, right)
        top, bottom = high(paired + line), low(paired + line)
        step = jnp.dot(top[:, :size], both, precision=HIGHEST, preferred_element_type=F32)
        turned = pltpu.roll(bottom, size, 1)
        step = jnp.dot(turned[:, :size], step, precision=HIGHEST, preferred_element_type=F32)
        return jnp.where(half, pltpu.roll(top, size, 1), turned + step)

    first = [
        jnp.where(half, through(line, low)[0], through(line, high)[1]) for line in range(width)
    ]
    pack(lambda line: first[line], (through_low, through_high))
    second = [jnp.where(half, high(paired + line), low(paired + line)) for line in range(width)]
    pack(lambda line: second[line], (reach_high, back_low))
    third = [joined(line) for line in range(width)]
    pack(lambda line: third[line], (back_high, pair))


def maps(own, other, width):
    size, elements = own.shape[1:]
    shape = jax.ShapeDtypeStruct((SUB, size, elements), F32)
    return pl.pallas_call(
        functools.partial(maps_kernel, width),
        out_shape=(shape,) * 6,
        name="line_maps",
        compiler_params=pltpu.CompilerParams(vmem_limit_bytes=10 * MIB),
    )(own, other)


def line_sweeps(width, entries, inv, fwd_steps, bwd_steps, local, ends, source):
    elements = source.shape[1]
    positions = elements // width

    @pl.loop(0, source.shape[0] // SUB)
    def _(n):
        at = pl.multiple_of(n * SUB, SUB)
        source[pl.ds(at, SUB), :] = block_rows([lambda i: inv[at + i]], [entries])

    values = swap_groups(rows_of(source[...]), width)
    for q in range(1, positions):
        values[q] = values[q] + packed_product(lambda il: fwd_steps[q, il], values[q - 1], width)
    ends[:SUB] = values[-1]
    for q in reversed(range(positions - 1)):
        values[q] = values[q] + packed_product(lambda il: bwd_steps[q, il], values[q + 1], width)
    ends[SUB:] = values[0]
    for n, rows in enumerate(swap_groups(values, width)):
        local[SUB * n : SUB * (n + 1), :] = rows


def sweep_kernel(width, right_side, norm, inv, fwd_steps, bwd_steps, local, ends, vector, source):
    vector[...] = right_side[...] / norm[0:1, :]
    rounded = vector[...].astype(BF16).astype(F32)
    line_sweeps(width, rows_of(rounded), inv, fwd_steps, bwd_steps, local, ends, source)


def sweep_shapes(size, elements):
    return (
        jax.ShapeDtypeStruct((size, elements), F32),
        jax.ShapeDtypeStruct((2 * SUB, elements), F32),
        jax.ShapeDtypeStruct((size, elements), F32),
    )


def sweep(right_side, norm, inv, fwd_steps, bwd_steps, width):
    size, elements = right_side.shape
    return pl.pallas_call(
        functools.partial(sweep_kernel, width),
        out_shape=sweep_shapes(size, elements),
        scratch_shapes=[pltpu.VMEM((size, elements), F32)],
        name="line_sweep",
        compiler_params=pltpu.CompilerParams(vmem_limit_bytes=6 * MIB),
    )(right_side, norm, inv, fwd_steps, bwd_steps)


def low_high(own, other):
    is_odd = lax.axis_index("line") % 2 == 1
    mine, theirs = own[...], other[...]
    return is_odd, jnp.where(is_odd, theirs, mine), jnp.where(is_odd, mine, theirs)


def pair_kernel(width, own, other, through_high, reach_high, back_low, far_pair, ends, crossing):
    _, low, high = low_high(own, other)
    passed = high[:SUB] + packed_product(lambda il: through_high[il], low[:SUB], width)
    reached = high[SUB:] + packed_product(lambda il: reach_high[il], low[:SUB], width)
    ends[:SUB] = passed
    ends[SUB:] = low[SUB:] + packed_product(lambda il: back_low[il], reached, width)
    crossing[...] = packed_product(lambda il: far_pair[il], passed, width)


def pair_ends(own, other, through_high, reach_high, back_low, far_pair, width):
    return pl.pallas_call(
        functools.partial(pair_kernel, width),
        out_shape=(
            jax.ShapeDtypeStruct((2 * SUB, own.shape[1]), F32),
            jax.ShapeDtypeStruct((SUB, own.shape[1]), F32),
        ),
        name="line_pair",
        compiler_params=pltpu.CompilerParams(vmem_limit_bytes=4 * MIB),
    )(own, other, through_high, reach_high, back_low, far_pair)


def correct_kernel(
    width, own, other, crossing, far, local, through_low, reach_high, back_high, before_a, before_b,
    response, send_list, result, edges, sent,
):
    place = lax.axis_index("line")
    is_upper = place // 2 == 1
    is_odd, low, high = low_high(own, other)
    zero = jnp.zeros(low[:SUB].shape, F32)
    enter = jnp.where(is_upper, far[:SUB], zero)
    leave = jnp.where(is_upper, zero, far[SUB:] + crossing[...])
    middle = low[:SUB] + packed_product(lambda il: through_low[il], enter, width)
    meet = (
        high[SUB:]
        + packed_product(lambda il: back_high[il], leave, width)
        + packed_product(lambda il: reach_high[il], middle, width)
    )
    forward = jnp.where(is_odd, middle, enter)
    backward = jnp.where(is_odd, leave, meet)
    entries = spread_groups(forward, width) + spread_groups(backward, width)

    @pl.loop(0, local.shape[0] // SUB)
    def _(n):
        at = pl.multiple_of(n * SUB, SUB)
        result[pl.ds(at, SUB), :] = local[pl.ds(at, SUB), :] + block_rows(
            [lambda i: response[at + i]], [entries]
        )

    first = group_zero(rows_of(result[...]), width)
    back = packed_product(
        lambda il: jnp.where(is_odd, before_a[il].astype(F32), before_b[il].astype(F32)), first, width
    )
    edges[:SUB] = forward + jnp.where(place == 0, zero, back)
    edges[SUB:] = backward
    size, elements = result.shape
    rest = jnp.zeros((1, elements - send_list.shape[0] * send_list.shape[1]), jnp.int32)
    index = jnp.concatenate([send_list[0:1, :], send_list[1:2, :], rest], axis=1)
    index = jnp.broadcast_to(index, result.shape)
    sent[...] = jnp.take_along_axis(result[...], index, axis=1)[:, : sent.shape[1]]


def correct(own, other, crossing, far, local, through_low, reach_high, back_high, before_a, before_b, response, send_list, width):
    size, elements = local.shape
    return pl.pallas_call(
        functools.partial(correct_kernel, width),
        out_shape=(
            jax.ShapeDtypeStruct((size, elements), F32),
            jax.ShapeDtypeStruct((2 * SUB, elements), F32),
            jax.ShapeDtypeStruct((size, send_list.size), F32),
        ),
        name="line_correct",
        compiler_params=pltpu.CompilerParams(vmem_limit_bytes=10 * MIB),
    )(own, other, crossing, far, local, through_low, reach_high, back_high, before_a, before_b, response, send_list)


def near_kernel(width, rounded, vector, edges, diag, lower, upper, out):
    size, elements = vector.shape
    lane = lanes_of((SUB, elements))
    center = rows_of(vector[...])
    before = spread_groups(edges[:SUB], width)
    after = spread_groups(edges[SUB:], width)
    earlier = [
        jnp.where(lane < width, edge, pltpu.roll(rows, width, 1))
        for rows, edge in zip(center, before)
    ]
    later = [
        jnp.where(lane >= elements - width, edge, pltpu.roll(rows, elements - width, 1))
        for rows, edge in zip(center, after)
    ]
    if rounded:
        center, earlier, later = (
            [rows.astype(BF16).astype(F32) for rows in each] for each in (center, earlier, later)
        )

    @pl.loop(0, size // SUB)
    def _(n):
        at = pl.multiple_of(n * SUB, SUB)
        out[pl.ds(at, SUB), :] = block_rows(
            [lambda i: diag[at + i], lambda i: lower[at + i], lambda i: upper[at + i]],
            [center, earlier, later],
        )


def near(vector, edges, diag, lower, upper, width, rounded):
    size, elements = vector.shape
    return pl.pallas_call(
        functools.partial(near_kernel, width, rounded),
        out_shape=jax.ShapeDtypeStruct((size, elements), F32),
        name="near_faces",
        compiler_params=pltpu.CompilerParams(vmem_limit_bytes=6 * MIB),
        cost_estimate=pl.CostEstimate(
            flops=6 * size * size * elements, bytes_accessed=6 * size * size * elements, transcendentals=0
        ),
    )(vector, edges, diag, lower, upper)


def pick_faces(rounded, vector, got_a, got_b, face_nbr, picked):
    count, size, elements = picked.shape
    width = got_a.shape[1]
    halo = width // 2
    place, last = lax.axis_index("dom"), lax.axis_size("dom") - 1
    even = place % 2 == 0
    own = vector[...]
    halos = [got_a[...], got_b[...], jnp.zeros((size, elements - 2 * width), F32)]
    halos = jnp.concatenate(halos, axis=1)
    for f in range(count):
        slot = face_nbr[f : f + 1, :]
        left = jnp.logical_and(slot < elements + halo, place > 0)
        right = jnp.logical_and(slot >= elements + halo, slot < elements + width)
        right = jnp.logical_and(right, place < last)
        at_left = slot - elements + jnp.where(even, width, 0)
        at_right = slot - elements + jnp.where(even, 0, width)
        outside = jnp.where(left, at_left, jnp.where(right, at_right, 2 * width))
        at = jnp.broadcast_to(slot, (size, elements))
        outside = jnp.broadcast_to(jnp.clip(outside, 0, elements - 1), (size, elements))
        inner = jnp.take_along_axis(own, jnp.clip(at, 0, elements - 1), axis=1)
        outer = jnp.take_along_axis(halos, outside, axis=1)
        chosen = jnp.where(at < elements, inner, outer)
        if rounded:
            chosen = chosen.astype(BF16).astype(F32)
        picked[f] = chosen


def add_faces(partial, faces, picked, out):
    count, size, elements = picked.shape
    reads = [functools.partial(lambda f, at, i: faces[f, at + i], f) for f in range(count)]

    @pl.loop(0, size // SUB)
    def _(n):
        at = pl.multiple_of(n * SUB, SUB)
        vectors = [rows_of(picked[f]) for f in range(count)]
        out[pl.ds(at, SUB), :] = partial[pl.ds(at, SUB), :] + block_rows(
            [functools.partial(read, at) for read in reads], vectors
        )


def advance_kernel(
    width, rounded, vector, got_a, got_b, face_nbr, partial, faces, inv, fwd_steps, bwd_steps,
    local, ends, out, picked, source,
):
    pick_faces(rounded, vector, got_a, got_b, face_nbr, picked)
    add_faces(partial, faces, picked, out)
    line_sweeps(width, rows_of(out[...]), inv, fwd_steps, bwd_steps, local, ends, source)


def advance(vector, got_a, got_b, face_nbr, partial, faces, inv, fwd_steps, bwd_steps, width, rounded):
    size, elements = vector.shape
    return pl.pallas_call(
        functools.partial(advance_kernel, width, rounded),
        out_shape=sweep_shapes(size, elements),
        scratch_shapes=[
            pltpu.VMEM((faces.shape[0], size, elements), F32),
            pltpu.VMEM((size, elements), F32),
        ],
        name="faces_and_sweep",
        compiler_params=pltpu.CompilerParams(vmem_limit_bytes=10 * MIB),
    )(vector, got_a, got_b, face_nbr, partial, faces, inv, fwd_steps, bwd_steps)


def closing_kernel(rounded, vector, got_a, got_b, face_nbr, partial, faces, *rest):
    basis, (sums, last, picked) = rest[:-3], rest[-3:]
    pick_faces(rounded, vector, got_a, got_b, face_nbr, picked)
    add_faces(partial, faces, picked, last)
    vectors = [rows_of(each[...]) for each in basis] + [rows_of(last[...])]
    lines = []
    for i in range(len(vectors)):
        for j in range(i, len(vectors)):
            lines.append(sum(a * b for a, b in zip(vectors[i], vectors[j])))
    while len(lines) % SUB:
        lines.append(jnp.zeros_like(lines[0]))
    for n in range(0, len(lines), SUB):
        folded = fold_sublanes(lines[n : n + SUB])
        sums[n : n + SUB, :] = jnp.broadcast_to(jnp.sum(folded, axis=1, keepdims=True), folded.shape)


def closing(vector, got_a, got_b, face_nbr, partial, faces, basis, rounded):
    size, elements = vector.shape
    count = len(basis) + 1
    rows = count * (count + 1) // 2
    rows += -rows % SUB
    return pl.pallas_call(
        functools.partial(closing_kernel, rounded),
        out_shape=jax.ShapeDtypeStruct((rows, elements), F32),
        scratch_shapes=[
            pltpu.VMEM((size, elements), F32),
            pltpu.VMEM((faces.shape[0], size, elements), F32),
        ],
        name="faces_and_sums",
        compiler_params=pltpu.CompilerParams(vmem_limit_bytes=8 * MIB),
    )(vector, got_a, got_b, face_nbr, partial, faces, *basis)


def cholesky(entry, count):
    tri = {}
    for i in range(count):
        pivot = entry[i, i]
        for k in range(i):
            pivot = pivot - tri[k, i] * tri[k, i]
        tri[i, i] = jnp.sqrt(pivot)
        for j in range(i + 1, count):
            value = entry[i, j]
            for k in range(i):
                value = value - tri[k, i] * tri[k, j]
            tri[i, j] = value / tri[i, i]
    return tri


def finish_kernel(iters, norm, sums, *rest):
    search, (update, hessenberg) = rest[:iters], rest[iters:]
    count = iters + 1
    entry = {}
    n = 0
    for i in range(count):
        for j in range(i, count):
            entry[i, j] = sums[n : n + 1, :]
            n += 1
    tri = cholesky(entry, count)
    hess = {}
    for j in range(iters):
        for i in range(j + 2):
            value = tri[i, j + 1]
            for k in range(max(i - 1, 0), j):
                value = value - hess[i, k] * tri[k, j]
            hess[i, j] = value / tri[j, j]
    shape = (count, norm.shape[1])
    row, column = (lax.broadcasted_iota(jnp.int32, shape, axis) for axis in (0, 1))
    table = jnp.zeros(shape, F32)
    for (i, j), value in hess.items():
        table = jnp.where(jnp.logical_and(row == i, column == j), value, table)
    hessenberg[...] = table[:, :iters]
    normal = {}
    for i in range(iters):
        for j in range(i, iters):
            normal[i, j] = sum(hess[k, i] * hess[k, j] for k in range(i + 2))
    factor = cholesky(normal, iters)
    start = norm[0:1, :] * tri[0, 0]
    half = []
    for i in range(iters):
        value = start * hess[0, i]
        for k in range(i):
            value = value - factor[k, i] * half[k]
        half.append(value / factor[i, i])
    coeffs = [None] * iters
    for i in reversed(range(iters)):
        value = half[i]
        for k in range(i + 1, iters):
            value = value - factor[i, k] * coeffs[k]
        coeffs[i] = value / factor[i, i]
    weights = [None] * iters
    for i in reversed(range(iters)):
        value = coeffs[i]
        for k in range(i + 1, iters):
            value = value - tri[i, k] * weights[k]
        weights[i] = value / tri[i, i]
    update[...] = sum(weights[i] * search[i][...] for i in range(iters))


def finish(norm, sums, search):
    iters = len(search)
    size, elements = search[0].shape
    return pl.pallas_call(
        functools.partial(finish_kernel, iters),
        out_shape=(
            jax.ShapeDtypeStruct((size, elements), F32),
            jax.ShapeDtypeStruct((iters + 1, iters), F32),
        ),
        name="solve_and_update",
        compiler_params=pltpu.CompilerParams(vmem_limit_bytes=2 * MIB),
    )(norm, sums, *search)


def flip(count, bit):
    return [(i, i ^ bit) for i in range(count)]


def neighbour_pairs(count):
    pairs = []
    for i in range(count):
        j = i + 1 if i % 2 else i - 1
        pairs.append((i, j if 0 <= j < count else i))
    return pairs


def sum_all(value):
    axes = ("dom", "line")
    doms, lines = lax.axis_size("dom"), lax.axis_size("line")
    total = doms * lines
    bits = []
    bit = 1
    while bit < total:
        bits.append(bit)
        bit *= 2
    groups = [bits[:1]] + [bits[n : n + 2] for n in range(1, len(bits), 2)]
    for group in groups:
        masks = [0]
        for bit in group:
            masks = masks + [m | bit for m in masks]
        value = sum((lax.ppermute(value, axes, flip(total, m)) for m in masks[1:]), value)
    return value


def shards(
    right_side, diag_blocks, lower_blocks, upper_blocks, face_blocks, face_nbr, send_list,
    inv_blocks, fwd_blocks, bwd_blocks,
):
    width = LINES_DEV
    lines, doms = lax.axis_size("line"), lax.axis_size("dom")

    squares = jnp.broadcast_to(jnp.sum(right_side * right_side), (SUB, right_side.shape[1]))
    norm = jnp.sqrt(sum_all(squares))
    fwd_steps, bwd_steps, last_block = step_layouts(fwd_blocks, bwd_blocks, width)
    before_a = lax.ppermute(last_block, "line", flip(lines, 1))
    before_b = lax.ppermute(last_block, "line", neighbour_pairs(lines))
    response, ends = chain_products(fwd_blocks, bwd_blocks, width)
    other_ends = lax.ppermute(ends, "line", flip(lines, 1))
    through_low, through_high, reach_high, back_low, back_high, pair = maps(ends, other_ends, width)
    far_pair = lax.ppermute(pair, "line", flip(lines, 2))

    local, ends_own, first = sweep(right_side, norm, inv_blocks, fwd_steps, bwd_steps, width)
    basis = [first]
    search = []
    for iteration in range(ITERS):
        rounded = iteration == 0
        ends_other = lax.ppermute(ends_own, "line", flip(lines, 1))
        pair_own, crossing = pair_ends(
            ends_own, ends_other, through_high, reach_high, back_low, far_pair, width
        )
        pair_far = lax.ppermute(pair_own, "line", flip(lines, 2))
        direction, edges, sent = correct(
            ends_own, ends_other, crossing, pair_far, local, through_low, reach_high, back_high,
            before_a, before_b, response, send_list, width,
        )
        search.append(direction)
        got_a = lax.ppermute(sent, "dom", flip(doms, 1))
        got_b = lax.ppermute(sent, "dom", neighbour_pairs(doms))
        partial = near(direction, edges, diag_blocks, lower_blocks, upper_blocks, width, rounded)
        given = (direction, got_a, got_b, face_nbr, partial, face_blocks)
        if iteration + 1 < ITERS:
            local, ends_own, following = advance(
                *given, inv_blocks, fwd_steps, bwd_steps, width, rounded
            )
            basis.append(following)
    sums = sum_all(closing(*given, basis, rounded))
    update, hessenberg = finish(norm, sums, search)
    return (update, hessenberg)


def solution(mesh):
    in_specs = (
        P(None, ("dom", "line")),
        P(None, None, ("dom", "line")),
        P(None, None, ("dom", "line")),
        P(None, None, ("dom", "line")),
        P(None, None, None, ("dom", "line")),
        P(None, ("dom", "line")),
        P(None, ("dom", "line")),
        P(None, None, ("dom", "line")),
        P(None, None, ("dom", "line")),
        P(None, None, ("dom", "line")),
    )
    out_specs = (P(None, ("dom", "line")), P())
    return jax.shard_map(shards, mesh=mesh, in_specs=in_specs, out_specs=out_specs, check_vma=False)
```

profile of v0, /device:TPU:0, one launch (start us, length us, event | category | flops | bytes accessed | tf_op | source)
XLA Modules:
  0.0 116.6 jit_solution(2850405348060581001)
XLA Ops:
  3.2 8.9 %chain_products.1 = (f32[64,128,128]{2,1,0:T(8,128)S(1)}, f32[24,64,128]{2,1,0:T(8,128)S(1)}) custom-call(bf16[64,64,128]{2,1,0:T(8,128)(2,1)S(1)} %copy-done.5, bf16[64,64,128]{2,1,0:T(8,128)(2,1)S(1)} %copy-done.6), custom_call_target="tpu_custom_call" | custom-call | flops 40000000 | bytes 12582912 | tf_op jit(solution)/shard_map/chain_products/pallas_call | solution.py:245
  12.7 1.4 %multiply_reduce_fusion = f32[]{:T(128)} fusion(f32[64,128]{1,0:T(8,128)} %right_side.1), kind=kLoop, calls=%fused_computation | loop fusion | flops 16383 | bytes 32772 | tf_op jit(solution)/shard_map/reduce_sum | solution.py:702
  16.6 2.7 %collective-permute-start.1 = (f32[8,128]{1,0:T(8,128)S(1)}, f32[8,128]{1,0:T(8,128)S(1)}, u32[]{:S(2)}, u32[]{:S(2)}) collective-permute-start(f32[8,128]{1,0:T(8,128)S(1)} %broadcast_add_fusion), channel_id=1, source_target_pairs={{0,2},{1,3},{2,0},{3,1},{4,6},{5,7},{6,4},{7,5},{8,10},{9,11},{10,... | collective-permute-start | bytes 12296 | tf_op jit(solution)/shard_map/ppermute | solution.py:691
  19.3 1.4 %collective-permute-start.2 = (f32[8,128]{1,0:T(8,128)S(1)}, f32[8,128]{1,0:T(8,128)S(1)}, u32[]{:S(2)}, u32[]{:S(2)}) collective-permute-start(f32[8,128]{1,0:T(8,128)S(1)} %broadcast_add_fusion), channel_id=1, source_target_pairs={{0,4},{1,5},{2,6},{3,7},{4,0},{5,1},{6,2},{7,3},{8,12},{9,13},{10,... | collective-permute-start | bytes 12296 | tf_op jit(solution)/shard_map/ppermute | solution.py:691
  20.8 1.7 %line_maps.1 = (f32[8,64,128]{2,1,0:T(8,128)S(1)}, f32[8,64,128]{2,1,0:T(8,128)S(1)}, f32[8,64,128]{2,1,0:T(8,128)S(1)}, f32[8,64,128]{2,1,0:T(8,128)S(1)}, f32[...) custom-call(f32[24,64,128]{2,1,0:T(8,128)S(1)} %get-tuple-element.40.own, f32[24,64,128]{2,1,0:T(8,128)S(1)} %collective-permute-done.8.other), custom_call_target="tpu_custom_call" | custom-call | tf_op jit(solution)/shard_map/line_maps/pallas_call | solution.py:315
  22.6 2.0 %collective-permute-start.9 = (f32[8,64,128]{2,1,0:T(8,128)S(1)}, f32[8,64,128]{2,1,0:T(8,128)S(1)}, u32[]{:S(2)}, u32[]{:S(2)}) collective-permute-start(f32[8,64,128]{2,1,0:T(8,128)S(1)} %get-tuple-element.44), channel_id=1, source_target_pairs={{0,2},{1,3},{2,0},{3,1},{4,6},{5,7},{6,4},{7,5},{8,10},{9,11},{10,... | collective-permute-start | bytes 786440 | tf_op jit(solution)/shard_map/ppermute | solution.py:710
  26.0 1.7 %collective-permute-start.4 = (f32[8,128]{1,0:T(8,128)S(1)}, f32[8,128]{1,0:T(8,128)S(1)}, u32[]{:S(2)}, u32[]{:S(2)}) collective-permute-start(f32[8,128]{1,0:T(8,128)S(1)} %add_add_fusion.2), channel_id=1, source_target_pairs={{0,8},{1,9},{2,10},{3,11},{4,12},{5,13},{6,14},{7,15},{8,0},{9,1},... | collective-permute-start | bytes 12296 | tf_op jit(solution)/shard_map/ppermute | solution.py:691
  27.7 2.6 %collective-permute-start.5 = (f32[8,128]{1,0:T(8,128)S(1)}, f32[8,128]{1,0:T(8,128)S(1)}, u32[]{:S(2)}, u32[]{:S(2)}) collective-permute-start(f32[8,128]{1,0:T(8,128)S(1)} %add_add_fusion.2), channel_id=1, source_target_pairs={{0,16},{1,17},{2,18},{3,19},{4,20},{5,21},{6,22},{7,23},{8,24},{9,... | collective-permute-start | bytes 12296 | tf_op jit(solution)/shard_map/ppermute | solution.py:691
  30.5 7.7 %step_layouts.1 = (bf16[8,8,64,128]{3,2,1,0:T(8,128)(2,1)S(1)}, bf16[8,8,64,128]{3,2,1,0:T(8,128)(2,1)S(1)}, bf16[8,64,128]{2,1,0:T(8,128)(2,1)S(1)}) custom-call(bf16[64,64,128]{2,1,0:T(8,128)(2,1)S(1)} %copy-done.5, bf16[64,64,128]{2,1,0:T(8,128)(2,1)S(1)} %copy-done.7), custom_call_target="tpu_custom_call" | custom-call | flops 4000000 | bytes 8388608 | tf_op jit(solution)/shard_map/step_layouts/pallas_call | solution.py:153
  39.0 4.0 %line_sweep.1 = (f32[64,128]{1,0:T(8,128)S(1)}, f32[16,128]{1,0:T(8,128)S(1)}, f32[64,128]{1,0:T(8,128)S(1)}) custom-call(f32[64,128]{1,0:T(8,128)S(1)} %copy-done.8, f32[8,128]{1,0:T(8,128)S(1)} %add_sqrt_fusion.norm, bf16[64,64,128]{2,1,0:T(8,128)(2,1)S(1)} %copy-done.4, bf16[8,8,64,128]{3,2,1,0:T(8,128)(2,1)S(1)} %get-tuple-element.37.fwd_steps, ...), custom_call_target="tpu_custom_call" | custom-call | tf_op jit(solution)/shard_map/line_sweep/pallas_call | solution.py:359
  43.0 1.8 %collective-permute-start.7 = (f32[16,128]{1,0:T(8,128)S(1)}, f32[16,128]{1,0:T(8,128)S(1)}, u32[]{:S(2)}, u32[]{:S(2)}) collective-permute-start(f32[16,128]{1,0:T(8,128)S(1)} %get-tuple-element.39.own), channel_id=1, source_target_pairs={{0,1},{1,0},{2,3},{3,2},{4,5},{5,4},{6,7},{7,6},{8,9},{9,8},{10,11... | collective-permute-start | bytes 24584 | tf_op jit(solution)/shard_map/ppermute | solution.py:717
  46.2 2.0 %collective-permute-start.10 = (f32[16,128]{1,0:T(8,128)S(1)}, f32[16,128]{1,0:T(8,128)S(1)}, u32[]{:S(2)}, u32[]{:S(2)}) collective-permute-start(f32[16,128]{1,0:T(8,128)S(1)} %get-tuple-element.46), channel_id=1, source_target_pairs={{0,2},{1,3},{2,0},{3,1},{4,6},{5,7},{6,4},{7,5},{8,10},{9,11},{10,... | collective-permute-start | bytes 24584 | tf_op jit(solution)/shard_map/ppermute | solution.py:721
  48.2 1.8 %collective-permute-done.10.far = f32[16,128]{1,0:T(8,128)S(1)} collective-permute-done((f32[16,128]{1,0:T(8,128)S(1)}, f32[16,128]{1,0:T(8,128)S(1)}, u32[]{:S(2)}, u32[]{:S(2)}) %collective-permute-start.10) | collective-permute-done | bytes 8224 | tf_op jit(solution)/shard_map/ppermute | solution.py:721
  49.9 1.4 %line_correct.3 = (f32[64,128]{1,0:T(8,128)S(1)}, f32[16,128]{1,0:T(8,128)S(1)}, f32[64,32]{1,0:T(8,128)S(1)}) custom-call(f32[16,128]{1,0:T(8,128)S(1)} %get-tuple-element.39.own, f32[16,128]{1,0:T(8,128)S(1)} %collective-permute-done.7.other, f32[8,128]{1,0:T(8,128)S(1)} %get-tuple-element.45.crossing, f32[16,128]{1,0:T(8,128)S(1)} %collective-permute-done.10.far, ...), custom_call_target="tpu_custom_call" | custom-call | tf_op jit(solution)/shard_map/line_correct/pallas_call | solution.py:437
  53.8 1.5 %collective-permute-done.13.got_a = f32[64,32]{1,0:T(8,128)S(1)} collective-permute-done((f32[64,32]{1,0:T(8,128)S(1)}, f32[64,32]{1,0:T(8,128)S(1)}, u32[]{:S(2)}, u32[]{:S(2)}) %collective-permute-start.13) | collective-permute-done | bytes 8224 | tf_op jit(solution)/shard_map/ppermute | solution.py:727
  55.3 5.2 %faces_and_sweep.2 = (f32[64,128]{1,0:T(8,128)S(1)}, f32[16,128]{1,0:T(8,128)S(1)}, f32[64,128]{1,0:T(8,128)S(1)}) custom-call(f32[64,128]{1,0:T(8,128)S(1)} %get-tuple-element.52.vector.rest_0_, f32[64,32]{1,0:T(8,128)S(1)} %collective-permute-done.13.got_a, f32[64,32]{1,0:T(8,128)S(1)} %collective-permute-done.14.got_b, s32[4,128]{1,0:T(4,128)S(1)} %copy-done.9, ...), custom_call_target="tpu_custom_call" | custom-call | tf_op jit(solution)/shard_map/faces_and_sweep/pallas_call | solution.py:541
  62.2 2.0 %collective-permute-start.16 = (f32[16,128]{1,0:T(8,128)S(1)}, f32[16,128]{1,0:T(8,128)S(1)}, u32[]{:S(2)}, u32[]{:S(2)}) collective-permute-start(f32[16,128]{1,0:T(8,128)S(1)} %get-tuple-element.57), channel_id=1, source_target_pairs={{0,2},{1,3},{2,0},{3,1},{4,6},{5,7},{6,4},{7,5},{8,10},{9,11},{10,... | collective-permute-start | bytes 24584 | tf_op jit(solution)/shard_map/ppermute | solution.py:721
  64.2 1.8 %collective-permute-done.16.far = f32[16,128]{1,0:T(8,128)S(1)} collective-permute-done((f32[16,128]{1,0:T(8,128)S(1)}, f32[16,128]{1,0:T(8,128)S(1)}, u32[]{:S(2)}, u32[]{:S(2)}) %collective-permute-start.16) | collective-permute-done | bytes 8224 | tf_op jit(solution)/shard_map/ppermute | solution.py:721
  65.9 1.4 %line_correct.4 = (f32[64,128]{1,0:T(8,128)S(1)}, f32[16,128]{1,0:T(8,128)S(1)}, f32[64,32]{1,0:T(8,128)S(1)}) custom-call(f32[16,128]{1,0:T(8,128)S(1)} %get-tuple-element.55.own, f32[16,128]{1,0:T(8,128)S(1)} %collective-permute-done.15.other, f32[8,128]{1,0:T(8,128)S(1)} %get-tuple-element.56.crossing, f32[16,128]{1,0:T(8,128)S(1)} %collective-permute-done.16.far, ...), custom_call_target="tpu_custom_call" | custom-call | tf_op jit(solution)/shard_map/line_correct/pallas_call | solution.py:437
  67.3 4.9 %collective-permute-start.17 = (f32[64,32]{1,0:T(8,128)S(1)}, f32[64,32]{1,0:T(8,128)S(1)}, u32[]{:S(2)}, u32[]{:S(2)}) collective-permute-start(f32[64,32]{1,0:T(8,128)S(1)} %get-tuple-element.60), channel_id=1, source_target_pairs={{0,4},{4,0},{8,12},{12,8},{16,20},{20,16},{24,28},{28,24},{1,5},{5... | collective-permute-start | bytes 24584 | tf_op jit(solution)/shard_map/ppermute | solution.py:727
  74.1 5.3 %faces_and_sweep.3 = (f32[64,128]{1,0:T(8,128)S(1)}, f32[16,128]{1,0:T(8,128)S(1)}, f32[64,128]{1,0:T(8,128)S(1)}) custom-call(f32[64,128]{1,0:T(8,128)S(1)} %get-tuple-element.59.vector.rest_1_, f32[64,32]{1,0:T(8,128)S(1)} %collective-permute-done.17.got_a, f32[64,32]{1,0:T(8,128)S(1)} %collective-permute-done.18.got_b, s32[4,128]{1,0:T(4,128)S(1)} %copy-done.9, ...), custom_call_target="tpu_custom_call" | custom-call | tf_op jit(solution)/shard_map/faces_and_sweep/pallas_call | solution.py:541
  81.0 2.0 %collective-permute-start.20 = (f32[16,128]{1,0:T(8,128)S(1)}, f32[16,128]{1,0:T(8,128)S(1)}, u32[]{:S(2)}, u32[]{:S(2)}) collective-permute-start(f32[16,128]{1,0:T(8,128)S(1)} %get-tuple-element.64), channel_id=1, source_target_pairs={{0,2},{1,3},{2,0},{3,1},{4,6},{5,7},{6,4},{7,5},{8,10},{9,11},{10,... | collective-permute-start | bytes 24584 | tf_op jit(solution)/shard_map/ppermute | solution.py:721
  83.0 1.8 %collective-permute-done.20.far = f32[16,128]{1,0:T(8,128)S(1)} collective-permute-done((f32[16,128]{1,0:T(8,128)S(1)}, f32[16,128]{1,0:T(8,128)S(1)}, u32[]{:S(2)}, u32[]{:S(2)}) %collective-permute-start.20) | collective-permute-done | bytes 8224 | tf_op jit(solution)/shard_map/ppermute | solution.py:721
  86.1 4.9 %collective-permute-start.21 = (f32[64,32]{1,0:T(8,128)S(1)}, f32[64,32]{1,0:T(8,128)S(1)}, u32[]{:S(2)}, u32[]{:S(2)}) collective-permute-start(f32[64,32]{1,0:T(8,128)S(1)} %get-tuple-element.67), channel_id=1, source_target_pairs={{0,4},{4,0},{8,12},{12,8},{16,20},{20,16},{24,28},{28,24},{1,5},{5... | collective-permute-start | bytes 24584 | tf_op jit(solution)/shard_map/ppermute | solution.py:727
  95.4 1.9 %collective-permute-start.24 = (f32[16,128]{1,0:T(8,128)S(1)}, f32[16,128]{1,0:T(8,128)S(1)}, u32[]{:S(2)}, u32[]{:S(2)}) collective-permute-start(f32[16,128]{1,0:T(8,128)S(1)} %add.49), channel_id=1, source_target_pairs={{0,2},{1,3},{2,0},{3,1},{4,6},{5,7},{6,4},{7,5},{8,10},{9,11},{10,... | collective-permute-start | bytes 24584 | tf_op jit(solution)/shard_map/ppermute | solution.py:691
  97.3 4.8 %collective-permute-start.25 = (f32[16,128]{1,0:T(8,128)S(1)}, f32[16,128]{1,0:T(8,128)S(1)}, u32[]{:S(2)}, u32[]{:S(2)}) collective-permute-start(f32[16,128]{1,0:T(8,128)S(1)} %add.49), channel_id=1, source_target_pairs={{0,4},{1,5},{2,6},{3,7},{4,0},{5,1},{6,2},{7,3},{8,12},{9,13},{10,... | collective-permute-start | bytes 24584 | tf_op jit(solution)/shard_map/ppermute | solution.py:691
  102.1 1.6 %collective-permute-done.25 = f32[16,128]{1,0:T(8,128)S(1)} collective-permute-done((f32[16,128]{1,0:T(8,128)S(1)}, f32[16,128]{1,0:T(8,128)S(1)}, u32[]{:S(2)}, u32[]{:S(2)}) %collective-permute-start.25) | collective-permute-done | bytes 8224 | tf_op jit(solution)/shard_map/ppermute | solution.py:691
  103.7 2.9 %collective-permute-done.26 = f32[16,128]{1,0:T(8,128)S(1)} collective-permute-done((f32[16,128]{1,0:T(8,128)S(1)}, f32[16,128]{1,0:T(8,128)S(1)}, u32[]{:S(2)}, u32[]{:S(2)}) %collective-permute-start.26) | collective-permute-done | bytes 8224 | tf_op jit(solution)/shard_map/ppermute | solution.py:691
  106.7 2.7 %collective-permute-start.27 = (f32[16,128]{1,0:T(8,128)S(1)}, f32[16,128]{1,0:T(8,128)S(1)}, u32[]{:S(2)}, u32[]{:S(2)}) collective-permute-start(f32[16,128]{1,0:T(8,128)S(1)} %add_add_fusion.1), channel_id=1, source_target_pairs={{0,8},{1,9},{2,10},{3,11},{4,12},{5,13},{6,14},{7,15},{8,0},{9,1},... | collective-permute-start | bytes 24584 | tf_op jit(solution)/shard_map/ppermute | solution.py:691
  110.4 1.4 %collective-permute-start.29 = (f32[16,128]{1,0:T(8,128)S(1)}, f32[16,128]{1,0:T(8,128)S(1)}, u32[]{:S(2)}, u32[]{:S(2)}) collective-permute-start(f32[16,128]{1,0:T(8,128)S(1)} %add_add_fusion.1), channel_id=1, source_target_pairs={{0,24},{1,25},{2,26},{3,27},{4,28},{5,29},{6,30},{7,31},{8,16},{9,... | collective-permute-start | bytes 24584 | tf_op jit(solution)/shard_map/ppermute | solution.py:691
  111.8 2.1 %collective-permute-done.28 = f32[16,128]{1,0:T(8,128)S(1)} collective-permute-done((f32[16,128]{1,0:T(8,128)S(1)}, f32[16,128]{1,0:T(8,128)S(1)}, u32[]{:S(2)}, u32[]{:S(2)}) %collective-permute-start.28) | collective-permute-done | bytes 8224 | tf_op jit(solution)/shard_map/ppermute | solution.py:691
  113.9 2.0 %collective-permute-done.29 = f32[16,128]{1,0:T(8,128)S(1)} collective-permute-done((f32[16,128]{1,0:T(8,128)S(1)}, f32[16,128]{1,0:T(8,128)S(1)}, u32[]{:S(2)}, u32[]{:S(2)}) %collective-permute-start.29) | collective-permute-done | bytes 8224 | tf_op jit(solution)/shard_map/ppermute | solution.py:691
  (75 shorter events, 24.7 us)
Async XLA Ops:
  0.6 38.3 %copy-start.4 = (bf16[64,64,128]{2,1,0:T(8,128)(2,1)S(1)}, bf16[64,64,128]{2,1,0:T(8,128)(2,1)}, u32[]{:S(2)}) copy-start(bf16[64,64,128]{2,1,0:T(8,128)(2,1)} %inv.5) | copy-start | bytes 3145732
  12.1 37.8 %copy-start.10 = (s32[2,16]{1,0:T(2,128)S(1)}, s32[2,16]{1,0:T(2,128)}, u32[]{:S(2)}) copy-start(s32[2,16]{1,0:T(2,128)} %send_list.5) | copy-start | bytes 388
  12.1 8.7 %collective-permute-start.8 = (f32[24,64,128]{2,1,0:T(8,128)S(1)}, f32[24,64,128]{2,1,0:T(8,128)S(1)}, u32[]{:S(2)}, u32[]{:S(2)}) collective-permute-start(f32[24,64,128]{2,1,0:T(8,128)S(1)} %get-tuple-element.40.own), channel_id=1, source_target_pairs={{0,1},{1,0},{2,3},{3,2},{4,5},{5,4},{6,7},{7,6},{8,9},{9,8},{10,11... | collective-permute-start | bytes 2359304 | tf_op jit(solution)/shard_map/ppermute | solution.py:708
  14.7 1.2 %collective-permute-start = (f32[8,128]{1,0:T(8,128)S(1)}, f32[8,128]{1,0:T(8,128)S(1)}, u32[]{:S(2)}, u32[]{:S(2)}) collective-permute-start(f32[8,128]{1,0:T(8,128)S(1)} %broadcast_in_dim.3), channel_id=1, source_target_pairs={{0,1},{1,0},{2,3},{3,2},{4,5},{5,4},{6,7},{7,6},{8,9},{9,8},{10,11... | collective-permute-start | bytes 12296 | tf_op jit(solution)/shard_map/ppermute | solution.py:691
  16.6 8.0 %collective-permute-start.1 = (f32[8,128]{1,0:T(8,128)S(1)}, f32[8,128]{1,0:T(8,128)S(1)}, u32[]{:S(2)}, u32[]{:S(2)}) collective-permute-start(f32[8,128]{1,0:T(8,128)S(1)} %broadcast_add_fusion), channel_id=1, source_target_pairs={{0,2},{1,3},{2,0},{3,1},{4,6},{5,7},{6,4},{7,5},{8,10},{9,11},{10,... | collective-permute-start | bytes 12296 | tf_op jit(solution)/shard_map/ppermute | solution.py:691
  19.3 5.3 %collective-permute-start.2 = (f32[8,128]{1,0:T(8,128)S(1)}, f32[8,128]{1,0:T(8,128)S(1)}, u32[]{:S(2)}, u32[]{:S(2)}) collective-permute-start(f32[8,128]{1,0:T(8,128)S(1)} %broadcast_add_fusion), channel_id=1, source_target_pairs={{0,4},{1,5},{2,6},{3,7},{4,0},{5,1},{6,2},{7,3},{8,12},{9,13},{10,... | collective-permute-start | bytes 12296 | tf_op jit(solution)/shard_map/ppermute | solution.py:691
  20.7 4.6 %collective-permute-start.3 = (f32[8,128]{1,0:T(8,128)S(1)}, f32[8,128]{1,0:T(8,128)S(1)}, u32[]{:S(2)}, u32[]{:S(2)}) collective-permute-start(f32[8,128]{1,0:T(8,128)S(1)} %broadcast_add_fusion), channel_id=1, source_target_pairs={{0,6},{1,7},{2,4},{3,5},{4,2},{5,3},{6,0},{7,1},{8,14},{9,15},{10,... | collective-permute-start | bytes 12296 | tf_op jit(solution)/shard_map/ppermute | solution.py:691
  22.6 23.1 %collective-permute-start.9 = (f32[8,64,128]{2,1,0:T(8,128)S(1)}, f32[8,64,128]{2,1,0:T(8,128)S(1)}, u32[]{:S(2)}, u32[]{:S(2)}) collective-permute-start(f32[8,64,128]{2,1,0:T(8,128)S(1)} %get-tuple-element.44), channel_id=1, source_target_pairs={{0,2},{1,3},{2,0},{3,1},{4,6},{5,7},{6,4},{7,5},{8,10},{9,11},{10,... | collective-permute-start | bytes 786440 | tf_op jit(solution)/shard_map/ppermute | solution.py:710
  26.0 12.2 %collective-permute-start.4 = (f32[8,128]{1,0:T(8,128)S(1)}, f32[8,128]{1,0:T(8,128)S(1)}, u32[]{:S(2)}, u32[]{:S(2)}) collective-permute-start(f32[8,128]{1,0:T(8,128)S(1)} %add_add_fusion.2), channel_id=1, source_target_pairs={{0,8},{1,9},{2,10},{3,11},{4,12},{5,13},{6,14},{7,15},{8,0},{9,1},... | collective-permute-start | bytes 12296 | tf_op jit(solution)/shard_map/ppermute | solution.py:691
  27.7 11.2 %collective-permute-start.5 = (f32[8,128]{1,0:T(8,128)S(1)}, f32[8,128]{1,0:T(8,128)S(1)}, u32[]{:S(2)}, u32[]{:S(2)}) collective-permute-start(f32[8,128]{1,0:T(8,128)S(1)} %add_add_fusion.2), channel_id=1, source_target_pairs={{0,16},{1,17},{2,18},{3,19},{4,20},{5,21},{6,22},{7,23},{8,24},{9,... | collective-permute-start | bytes 12296 | tf_op jit(solution)/shard_map/ppermute | solution.py:691
  30.3 8.6 %collective-permute-start.6 = (f32[8,128]{1,0:T(8,128)S(1)}, f32[8,128]{1,0:T(8,128)S(1)}, u32[]{:S(2)}, u32[]{:S(2)}) collective-permute-start(f32[8,128]{1,0:T(8,128)S(1)} %add_add_fusion.2), channel_id=1, source_target_pairs={{0,24},{1,25},{2,26},{3,27},{4,28},{5,29},{6,30},{7,31},{8,16},{9,... | collective-permute-start | bytes 12296 | tf_op jit(solution)/shard_map/ppermute | solution.py:691
  38.1 10.0 %collective-permute-start.11 = (bf16[8,64,128]{2,1,0:T(8,128)(2,1)S(1)}, bf16[8,64,128]{2,1,0:T(8,128)(2,1)S(1)}, u32[]{:S(2)}, u32[]{:S(2)}) collective-permute-start(bf16[8,64,128]{2,1,0:T(8,128)(2,1)S(1)} %get-tuple-element.50), channel_id=1, source_target_pairs={{0,1},{1,0},{2,3},{3,2},{4,5},{5,4},{6,7},{7,6},{8,9},{9,8},{10,11... | collective-permute-start | bytes 393224 | tf_op jit(solution)/shard_map/ppermute | solution.py:705
  38.2 9.9 %collective-permute-start.12 = (bf16[8,64,128]{2,1,0:T(8,128)(2,1)S(1)}, bf16[8,64,128]{2,1,0:T(8,128)(2,1)S(1)}, u32[]{:S(2)}, u32[]{:S(2)}) collective-permute-start(bf16[8,64,128]{2,1,0:T(8,128)(2,1)S(1)} %get-tuple-element.50), channel_id=1, source_target_pairs={{0,0},{1,2},{2,1},{3,3},{4,4},{5,6},{6,5},{7,7},{8,8},{9,10},{10,9... | collective-permute-start | bytes 393224 | tf_op jit(solution)/shard_map/ppermute | solution.py:706
  43.0 2.6 %collective-permute-start.7 = (f32[16,128]{1,0:T(8,128)S(1)}, f32[16,128]{1,0:T(8,128)S(1)}, u32[]{:S(2)}, u32[]{:S(2)}) collective-permute-start(f32[16,128]{1,0:T(8,128)S(1)} %get-tuple-element.39.own), channel_id=1, source_target_pairs={{0,1},{1,0},{2,3},{3,2},{4,5},{5,4},{6,7},{7,6},{8,9},{9,8},{10,11... | collective-permute-start | bytes 24584 | tf_op jit(solution)/shard_map/ppermute | solution.py:717
  46.2 3.7 %collective-permute-start.10 = (f32[16,128]{1,0:T(8,128)S(1)}, f32[16,128]{1,0:T(8,128)S(1)}, u32[]{:S(2)}, u32[]{:S(2)}) collective-permute-start(f32[16,128]{1,0:T(8,128)S(1)} %get-tuple-element.46), channel_id=1, source_target_pairs={{0,2},{1,3},{2,0},{3,1},{4,6},{5,7},{6,4},{7,5},{8,10},{9,11},{10,... | collective-permute-start | bytes 24584 | tf_op jit(solution)/shard_map/ppermute | solution.py:721
  51.3 4.0 %collective-permute-start.13 = (f32[64,32]{1,0:T(8,128)S(1)}, f32[64,32]{1,0:T(8,128)S(1)}, u32[]{:S(2)}, u32[]{:S(2)}) collective-permute-start(f32[64,32]{1,0:T(8,128)S(1)} %get-tuple-element.53), channel_id=1, source_target_pairs={{0,4},{4,0},{8,12},{12,8},{16,20},{20,16},{24,28},{28,24},{1,5},{5... | collective-permute-start | bytes 24584 | tf_op jit(solution)/shard_map/ppermute | solution.py:727
  52.1 3.1 %collective-permute-start.14 = (f32[64,32]{1,0:T(8,128)S(1)}, f32[64,32]{1,0:T(8,128)S(1)}, u32[]{:S(2)}, u32[]{:S(2)}) collective-permute-start(f32[64,32]{1,0:T(8,128)S(1)} %get-tuple-element.53), channel_id=1, source_target_pairs={{0,0},{4,8},{8,4},{12,16},{16,12},{20,24},{24,20},{28,28},{1,1},{5... | collective-permute-start | bytes 24584 | tf_op jit(solution)/shard_map/ppermute | solution.py:728
  60.5 1.2 %collective-permute-start.15 = (f32[16,128]{1,0:T(8,128)S(1)}, f32[16,128]{1,0:T(8,128)S(1)}, u32[]{:S(2)}, u32[]{:S(2)}) collective-permute-start(f32[16,128]{1,0:T(8,128)S(1)} %get-tuple-element.55.own), channel_id=1, source_target_pairs={{0,1},{1,0},{2,3},{3,2},{4,5},{5,4},{6,7},{7,6},{8,9},{9,8},{10,11... | collective-permute-start | bytes 24584 | tf_op jit(solution)/shard_map/ppermute | solution.py:717
  62.2 3.7 %collective-permute-start.16 = (f32[16,128]{1,0:T(8,128)S(1)}, f32[16,128]{1,0:T(8,128)S(1)}, u32[]{:S(2)}, u32[]{:S(2)}) collective-permute-start(f32[16,128]{1,0:T(8,128)S(1)} %get-tuple-element.57), channel_id=1, source_target_pairs={{0,2},{1,3},{2,0},{3,1},{4,6},{5,7},{6,4},{7,5},{8,10},{9,11},{10,... | collective-permute-start | bytes 24584 | tf_op jit(solution)/shard_map/ppermute | solution.py:721
  67.3 6.8 %collective-permute-start.17 = (f32[64,32]{1,0:T(8,128)S(1)}, f32[64,32]{1,0:T(8,128)S(1)}, u32[]{:S(2)}, u32[]{:S(2)}) collective-permute-start(f32[64,32]{1,0:T(8,128)S(1)} %get-tuple-element.60), channel_id=1, source_target_pairs={{0,4},{4,0},{8,12},{12,8},{16,20},{20,16},{24,28},{28,24},{1,5},{5... | collective-permute-start | bytes 24584 | tf_op jit(solution)/shard_map/ppermute | solution.py:727
  72.2 1.9 %collective-permute-start.18 = (f32[64,32]{1,0:T(8,128)S(1)}, f32[64,32]{1,0:T(8,128)S(1)}, u32[]{:S(2)}, u32[]{:S(2)}) collective-permute-start(f32[64,32]{1,0:T(8,128)S(1)} %get-tuple-element.60), channel_id=1, source_target_pairs={{0,0},{4,8},{8,4},{12,16},{16,12},{20,24},{24,20},{28,28},{1,1},{5... | collective-permute-start | bytes 24584 | tf_op jit(solution)/shard_map/ppermute | solution.py:728
  79.3 1.2 %collective-permute-start.19 = (f32[16,128]{1,0:T(8,128)S(1)}, f32[16,128]{1,0:T(8,128)S(1)}, u32[]{:S(2)}, u32[]{:S(2)}) collective-permute-start(f32[16,128]{1,0:T(8,128)S(1)} %get-tuple-element.62.own), channel_id=1, source_target_pairs={{0,1},{1,0},{2,3},{3,2},{4,5},{5,4},{6,7},{7,6},{8,9},{9,8},{10,11... | collective-permute-start | bytes 24584 | tf_op jit(solution)/shard_map/ppermute | solution.py:717
  81.0 3.7 %collective-permute-start.20 = (f32[16,128]{1,0:T(8,128)S(1)}, f32[16,128]{1,0:T(8,128)S(1)}, u32[]{:S(2)}, u32[]{:S(2)}) collective-permute-start(f32[16,128]{1,0:T(8,128)S(1)} %get-tuple-element.64), channel_id=1, source_target_pairs={{0,2},{1,3},{2,0},{3,1},{4,6},{5,7},{6,4},{7,5},{8,10},{9,11},{10,... | collective-permute-start | bytes 24584 | tf_op jit(solution)/shard_map/ppermute | solution.py:721
  86.1 6.8 %collective-permute-start.21 = (f32[64,32]{1,0:T(8,128)S(1)}, f32[64,32]{1,0:T(8,128)S(1)}, u32[]{:S(2)}, u32[]{:S(2)}) collective-permute-start(f32[64,32]{1,0:T(8,128)S(1)} %get-tuple-element.67), channel_id=1, source_target_pairs={{0,4},{4,0},{8,12},{12,8},{16,20},{20,16},{24,28},{28,24},{1,5},{5... | collective-permute-start | bytes 24584 | tf_op jit(solution)/shard_map/ppermute | solution.py:727
  91.0 1.9 %collective-permute-start.22 = (f32[64,32]{1,0:T(8,128)S(1)}, f32[64,32]{1,0:T(8,128)S(1)}, u32[]{:S(2)}, u32[]{:S(2)}) collective-permute-start(f32[64,32]{1,0:T(8,128)S(1)} %get-tuple-element.67), channel_id=1, source_target_pairs={{0,0},{4,8},{8,4},{12,16},{16,12},{20,24},{24,20},{28,28},{1,1},{5... | collective-permute-start | bytes 24584 | tf_op jit(solution)/shard_map/ppermute | solution.py:728
  94.2 1.2 %collective-permute-start.23 = (f32[16,128]{1,0:T(8,128)S(1)}, f32[16,128]{1,0:T(8,128)S(1)}, u32[]{:S(2)}, u32[]{:S(2)}) collective-permute-start(f32[16,128]{1,0:T(8,128)S(1)} %faces_and_sums.1), channel_id=1, source_target_pairs={{0,1},{1,0},{2,3},{3,2},{4,5},{5,4},{6,7},{7,6},{8,9},{9,8},{10,11... | collective-permute-start | bytes 24584 | tf_op jit(solution)/shard_map/ppermute | solution.py:691
  95.4 6.7 %collective-permute-start.24 = (f32[16,128]{1,0:T(8,128)S(1)}, f32[16,128]{1,0:T(8,128)S(1)}, u32[]{:S(2)}, u32[]{:S(2)}) collective-permute-start(f32[16,128]{1,0:T(8,128)S(1)} %add.49), channel_id=1, source_target_pairs={{0,2},{1,3},{2,0},{3,1},{4,6},{5,7},{6,4},{7,5},{8,10},{9,11},{10,... | collective-permute-start | bytes 24584 | tf_op jit(solution)/shard_map/ppermute | solution.py:691
  97.3 6.5 %collective-permute-start.25 = (f32[16,128]{1,0:T(8,128)S(1)}, f32[16,128]{1,0:T(8,128)S(1)}, u32[]{:S(2)}, u32[]{:S(2)}) collective-permute-start(f32[16,128]{1,0:T(8,128)S(1)} %add.49), channel_id=1, source_target_pairs={{0,4},{1,5},{2,6},{3,7},{4,0},{5,1},{6,2},{7,3},{8,12},{9,13},{10,... | collective-permute-start | bytes 24584 | tf_op jit(solution)/shard_map/ppermute | solution.py:691
  102.1 4.5 %collective-permute-start.26 = (f32[16,128]{1,0:T(8,128)S(1)}, f32[16,128]{1,0:T(8,128)S(1)}, u32[]{:S(2)}, u32[]{:S(2)}) collective-permute-start(f32[16,128]{1,0:T(8,128)S(1)} %add.49), channel_id=1, source_target_pairs={{0,6},{1,7},{2,4},{3,5},{4,2},{5,3},{6,0},{7,1},{8,14},{9,15},{10,... | collective-permute-start | bytes 24584 | tf_op jit(solution)/shard_map/ppermute | solution.py:691
  106.7 5.2 %collective-permute-start.27 = (f32[16,128]{1,0:T(8,128)S(1)}, f32[16,128]{1,0:T(8,128)S(1)}, u32[]{:S(2)}, u32[]{:S(2)}) collective-permute-start(f32[16,128]{1,0:T(8,128)S(1)} %add_add_fusion.1), channel_id=1, source_target_pairs={{0,8},{1,9},{2,10},{3,11},{4,12},{5,13},{6,14},{7,15},{8,0},{9,1},... | collective-permute-start | bytes 24584 | tf_op jit(solution)/shard_map/ppermute | solution.py:691
  109.3 4.5 %collective-permute-start.28 = (f32[16,128]{1,0:T(8,128)S(1)}, f32[16,128]{1,0:T(8,128)S(1)}, u32[]{:S(2)}, u32[]{:S(2)}) collective-permute-start(f32[16,128]{1,0:T(8,128)S(1)} %add_add_fusion.1), channel_id=1, source_target_pairs={{0,16},{1,17},{2,18},{3,19},{4,20},{5,21},{6,22},{7,23},{8,24},{9,... | collective-permute-start | bytes 24584 | tf_op jit(solution)/shard_map/ppermute | solution.py:691
  110.4 5.4 %collective-permute-start.29 = (f32[16,128]{1,0:T(8,128)S(1)}, f32[16,128]{1,0:T(8,128)S(1)}, u32[]{:S(2)}, u32[]{:S(2)}) collective-permute-start(f32[16,128]{1,0:T(8,128)S(1)} %add_add_fusion.1), channel_id=1, source_target_pairs={{0,24},{1,25},{2,26},{3,27},{4,28},{5,29},{6,30},{7,31},{8,16},{9,... | collective-permute-start | bytes 24584 | tf_op jit(solution)/shard_map/ppermute | solution.py:691
  (9 other events, 117.9 us)
where the time goes:
time: 117 us
  starting transfers between devices  44.3 us (38%)
  Pallas kernels  43.3 us (37%)
  waiting for transfers between devices  22.1 us (19%)
  local copies, waits for them, and re-layouts  3.22 us (3%)
  other arithmetic  2.69 us (2%)
    ppermute x14, starting transfers between devices, sum_all(): lax.ppermute(value, axes, flip(total, m))  20.7 us
    ppermute x14, waiting for transfers between devices, sum_all(): lax.ppermute(value, axes, flip(total, m))  11.7 us
    ppermute x3, starting transfers between devices, shards(): got_a = lax.ppermute(sent, 'dom', flip(doms, 1))  10.6 us
    pallas_call x2, Pallas kernels, advance(): pl.pallas_call(functools.partial(advance_kernel, width, rounded), out_sha...  10.5 us
    pallas_call x1, Pallas kernels, chain_products(): pl.pallas_call(functools.partial(chain_kernel, width), out_shape=(jax.Sha...  8.9 us
    pallas_call x1, Pallas kernels, step_layouts(): pl.pallas_call(functools.partial(steps_kernel, width), out_shape=(steps,...  7.66 us
    ppermute x3, starting transfers between devices, shards(): pair_far = lax.ppermute(pair_own, 'line', flip(lines, 2))  5.87 us
    ppermute x3, waiting for transfers between devices, shards(): pair_far = lax.ppermute(pair_own, 'line', flip(lines, 2))  5.27 us
  transfers between devices with their start and end apart: 30, of which 16 were waited for; matrix products, arithmetic and copies ran while one was open for 3% of the time, Pallas kernels for 14%

commit v1 on v0

--- a/solution.py
+++ b/solution.py
@@ -6,6 +6,7 @@
 from jax.experimental import pallas as pl
 from jax.experimental.pallas import tpu as pltpu
 from jax.sharding import PartitionSpec as P
+
 
 ITERS = 3
 LINES_DEV = 16
@@ -40,38 +41,29 @@
     return parts[0]
 
 
+def choose(arrays, index):
+    step = 1
+    while len(arrays) > 1:
+        clear = (index & step) == 0
+        arrays = [jnp.where(clear, arrays[a], arrays[a + 1]) for a in range(0, len(arrays), 2)]
+        step *= 2
+    return arrays[0]
+
+
 def spread_groups(packed, width):
-    total = packed.shape[1]
+    count = packed.shape[1] // width
     group = lanes_of(packed.shape) // width
-    step = total // width // 2
-    arrays = [packed]
-    while step:
-        clear = (group & step) == 0
-        grown = []
-        for item in arrays:
-            moved = pltpu.roll(item, step * width, 1)
-            grown.append(jnp.where(clear, item, moved))
-            grown.append(jnp.where(clear, moved, item))
-        arrays = grown
-        step //= 2
-    return arrays
+    moved = [packed] + [pltpu.roll(packed, step * width, 1) for step in range(1, count)]
+    return [choose([moved[(g - v) % count] for g in range(count)], group) for v in range(count)]
 
 
 def swap_groups(arrays, width):
     count = len(arrays)
-    total = arrays[0].shape[1]
     group = lanes_of(arrays[0].shape) // width
-    arrays = list(arrays)
-    step = count // 2
-    while step:
-        clear = (group & step) == 0
-        for a in range(count):
-            if a & step == 0:
-                low, high = arrays[a], arrays[a + step]
-                arrays[a] = jnp.where(clear, low, pltpu.roll(high, step * width, 1))
-                arrays[a + step] = jnp.where(clear, pltpu.roll(low, total - step * width, 1), high)
-        step //= 2
-    return arrays
+    moved = [
+        [array] + [pltpu.roll(array, step * width, 1) for step in range(1, count)] for array in arrays
+    ]
+    return [choose([moved[a][(a - q) % count] for a in range(count)], group) for q in range(count)]
 
 
 def group_zero(arrays, width):
@@ -126,43 +118,8 @@
     return arrays
 
 
-def steps_kernel(width, fwd, bwd, fwd_steps, bwd_steps, last):
+def tiles_kernel(fwd, bwd, tiles):
     size, _, elements = fwd.shape
-    positions = elements // width
-    pack = 2 * SUB
-    split = size // pack
-
-    @pl.loop(0, SUB * split)
-    def _(n):
-        il = n // split
-        at = pl.multiple_of((n % split) * pack, pack)
-        for blocks, steps in ((fwd, fwd_steps), (bwd, bwd_steps)):
-            arrays = [
-                -blocks[ih * SUB + il, pl.ds(at, pack), :].astype(F32) for ih in range(size // SUB)
-            ]
-            arrays = swap_groups(arrays, width)
-            for q in range(positions):
-                steps[q, il, pl.ds(at, pack), :] = arrays[q].astype(BF16)
-            if steps is bwd_steps:
-                last[il, pl.ds(at, pack), :] = arrays[-1].astype(BF16)
-
-
-def step_layouts(fwd, bwd, width):
-    size, _, elements = fwd.shape
-    steps = jax.ShapeDtypeStruct((elements // width, SUB, size, elements), BF16)
-    return pl.pallas_call(
-        functools.partial(steps_kernel, width),
-        out_shape=(steps, steps, jax.ShapeDtypeStruct((SUB, size, elements), BF16)),
-        name="step_layouts",
-        compiler_params=pltpu.CompilerParams(vmem_limit_bytes=10 * MIB),
-        cost_estimate=pl.CostEstimate(flops=4000000, bytes_accessed=8 * MIB, transcendentals=0),
-    )(fwd, bwd)
-
-
-def chain_kernel(width, fwd, bwd, response, ends, tiles, chain):
-    size, _, elements = fwd.shape
-    positions = elements // width
-    half = lanes_of((size, elements)) < size
 
     @pl.loop(0, size // SUB)
     def _(n):
@@ -177,6 +134,38 @@
             for a in range(SUB):
                 tiles[pl.ds((g * SUB + a) * size + n * SUB, SUB), :] = rows[a]
 
+
+def tile_layouts(fwd, bwd):
+    size, _, elements = fwd.shape
+    return pl.pallas_call(
+        tiles_kernel,
+        out_shape=jax.ShapeDtypeStruct((elements * size, 2 * size), F32),
+        name="tile_layouts",
+        compiler_params=pltpu.CompilerParams(vmem_limit_bytes=10 * MIB),
+        cost_estimate=pl.CostEstimate(flops=4000000, bytes_accessed=10 * MIB, transcendentals=0),
+    )(fwd, bwd)
+
+
+def squares_kernel(vector, squares):
+    total = sum(rows * rows for rows in rows_of(vector[...]))
+    total = jnp.sum(jnp.sum(total, axis=1, keepdims=True), axis=0, keepdims=True)
+    squares[...] = jnp.broadcast_to(total, squares.shape)
+
+
+def sum_squares(vector):
+    return pl.pallas_call(
+        squares_kernel,
+        out_shape=jax.ShapeDtypeStruct((SUB, vector.shape[1]), F32),
+        name="sum_squares",
+        compiler_params=pltpu.CompilerParams(vmem_limit_bytes=MIB),
+    )(vector)
+
+
+def chain_kernel(width, size, tiles, fwd_steps, bwd_steps, response, ends, chain):
+    elements = tiles.shape[0] // size
+    positions = elements // width
+    half = lanes_of((size, elements)) < size
+
     def tile(e):
         return tiles[pl.ds(pl.multiple_of(e * size, size), size), :]
 
@@ -189,8 +178,22 @@
         first = tile(line)
         chain[pl.ds(line * size, size), :] = jnp.where(half, first, pltpu.roll(first, size, 1))
 
+    def form_steps(q):
+        groups = []
+        for ih in range(size // SUB):
+            for lh in range(width // SUB):
+                start = (q * width + lh * SUB) * size + ih * SUB
+                groups.append(
+                    swap_sublanes([tiles[pl.ds(start + a * size, SUB), :] for a in range(SUB)])
+                )
+        for il in range(SUB):
+            turned = jnp.concatenate([rows[il] for rows in groups], axis=0).T
+            fwd_steps[q, il] = turned[:size].astype(BF16)
+            bwd_steps[q, il] = turned[size:].astype(BF16)
+
     @pl.loop(1, positions)
     def _(q):
+        form_steps(q)
         for line in range(width):
             e = q * width + line
             before = chain[pl.ds(pl.multiple_of((e - width) * size, size), size), :]
@@ -199,6 +202,7 @@
             out = jnp.dot(tile(e)[:, :size].astype(BF16), right, preferred_element_type=F32)
             chain[pl.ds(pl.multiple_of(e * size, size), size), :] = out + pltpu.roll(out, size, 1)
 
+    form_steps(0)
     last = positions - 1
     paired = width // 2
     for line in range(paired):
@@ -226,6 +230,7 @@
 
     for line in range(width):
         ends[paired + line] = chain[pl.ds(line * size, size), :]
+    ends[paired + width :] = bwd_steps[last].astype(F32)
 
     @pl.loop(0, size // SUB)
     def _(n):
@@ -240,25 +245,28 @@
             response[n * SUB + il] = jnp.concatenate([rows[il] for rows in groups], axis=0).T
 
 
-def chain_products(fwd, bwd, width):
-    size, _, elements = fwd.shape
-    return pl.pallas_call(
-        functools.partial(chain_kernel, width),
+def chain_products(tiles, width):
+    elements = tiles.shape[1]
+    size = tiles.shape[0] // elements
+    steps = jax.ShapeDtypeStruct((elements // width, SUB, size, elements), BF16)
+    return pl.pallas_call(
+        functools.partial(chain_kernel, width, size),
         out_shape=(
+            steps,
+            steps,
             jax.ShapeDtypeStruct((size, 2 * size, elements), F32),
-            jax.ShapeDtypeStruct((width + width // 2, size, elements), F32),
+            jax.ShapeDtypeStruct((width + width // 2 + SUB, size, elements), F32),
         ),
-        scratch_shapes=[
-            pltpu.VMEM((elements * size, elements), F32),
-            pltpu.VMEM((elements * size, elements), F32),
-        ],
+        scratch_shapes=[pltpu.VMEM((elements * size, elements), F32)],
         name="chain_products",
-        compiler_params=pltpu.CompilerParams(vmem_limit_bytes=20 * MIB),
+        compiler_params=pltpu.CompilerParams(vmem_limit_bytes=16 * MIB),
         cost_estimate=pl.CostEstimate(flops=40000000, bytes_accessed=12 * MIB, transcendentals=0),
-    )(fwd, bwd)
-
-
-def maps_kernel(width, own, other, through_low, through_high, reach_high, back_low, back_high, pair):
+    )(tiles)
+
+
+def maps_kernel(
+    width, own, other, through_low, through_high, reach_high, back_low, back_high, before, message, pair
+):
     size = own.shape[1]
     elements = own.shape[2]
     is_odd = lax.axis_index("line") % 2 == 1
@@ -307,6 +315,12 @@
     pack(lambda line: second[line], (reach_high, back_low))
     third = [joined(line) for line in range(width)]
     pack(lambda line: third[line], (back_high, pair))
+    for il in range(SUB):
+        top = pair[il].astype(BF16)
+        message[il] = top
+        message[SUB + il] = (pair[il] - top.astype(F32)).astype(BF16)
+        before[il] = other[paired + width + il]
+        message[2 * SUB + il] = other[paired + width + il].astype(BF16)
 
 
 def maps(own, other, width):
@@ -314,7 +328,8 @@
     shape = jax.ShapeDtypeStruct((SUB, size, elements), F32)
     return pl.pallas_call(
         functools.partial(maps_kernel, width),
-        out_shape=(shape,) * 6,
+        out_shape=(shape,) * 6 + (jax.ShapeDtypeStruct((3 * SUB, size, elements), BF16),),
+        scratch_shapes=[pltpu.VMEM((SUB, size, elements), F32)],
         name="line_maps",
         compiler_params=pltpu.CompilerParams(vmem_limit_bytes=10 * MIB),
     )(own, other)
@@ -371,29 +386,25 @@
     return is_odd, jnp.where(is_odd, theirs, mine), jnp.where(is_odd, mine, theirs)
 
 
-def pair_kernel(width, own, other, through_high, reach_high, back_low, far_pair, ends, crossing):
+def pair_kernel(width, own, other, through_high, reach_high, back_low, ends):
     _, low, high = low_high(own, other)
     passed = high[:SUB] + packed_product(lambda il: through_high[il], low[:SUB], width)
     reached = high[SUB:] + packed_product(lambda il: reach_high[il], low[:SUB], width)
     ends[:SUB] = passed
     ends[SUB:] = low[SUB:] + packed_product(lambda il: back_low[il], reached, width)
-    crossing[...] = packed_product(lambda il: far_pair[il], passed, width)
-
-
-def pair_ends(own, other, through_high, reach_high, back_low, far_pair, width):
+
+
+def pair_ends(own, other, through_high, reach_high, back_low, width):
     return pl.pallas_call(
         functools.partial(pair_kernel, width),
-        out_shape=(
-            jax.ShapeDtypeStruct((2 * SUB, own.shape[1]), F32),
-            jax.ShapeDtypeStruct((SUB, own.shape[1]), F32),
-        ),
+        out_shape=jax.ShapeDtypeStruct((2 * SUB, own.shape[1]), F32),
         name="line_pair",
         compiler_params=pltpu.CompilerParams(vmem_limit_bytes=4 * MIB),
-    )(own, other, through_high, reach_high, back_low, far_pair)
+    )(own, other, through_high, reach_high, back_low)
 
 
 def correct_kernel(
-    width, own, other, crossing, far, local, through_low, reach_high, back_high, before_a, before_b,
+    width, own, other, pair, far, local, through_low, reach_high, back_high, before, far_maps,
     response, send_list, result, edges, sent,
 ):
     place = lax.axis_index("line")
@@ -401,7 +412,10 @@
     is_odd, low, high = low_high(own, other)
     zero = jnp.zeros(low[:SUB].shape, F32)
     enter = jnp.where(is_upper, far[:SUB], zero)
-    leave = jnp.where(is_upper, zero, far[SUB:] + crossing[...])
+    crossing = packed_product(
+        lambda il: far_maps[il].astype(F32) + far_maps[SUB + il].astype(F32), pair[:SUB], width
+    )
+    leave = jnp.where(is_upper, zero, far[SUB:] + crossing)
     middle = low[:SUB] + packed_product(lambda il: through_low[il], enter, width)
     meet = (
         high[SUB:]
@@ -421,18 +435,18 @@
 
     first = group_zero(rows_of(result[...]), width)
     back = packed_product(
-        lambda il: jnp.where(is_odd, before_a[il].astype(F32), before_b[il].astype(F32)), first, width
+        lambda il: jnp.where(is_odd, before[il], far_maps[2 * SUB + il].astype(F32)), first, width
     )
     edges[:SUB] = forward + jnp.where(place == 0, zero, back)
     edges[SUB:] = backward
-    size, elements = result.shape
+    _, elements = result.shape
     rest = jnp.zeros((1, elements - send_list.shape[0] * send_list.shape[1]), jnp.int32)
     index = jnp.concatenate([send_list[0:1, :], send_list[1:2, :], rest], axis=1)
     index = jnp.broadcast_to(index, result.shape)
     sent[...] = jnp.take_along_axis(result[...], index, axis=1)[:, : sent.shape[1]]
 
 
-def correct(own, other, crossing, far, local, through_low, reach_high, back_high, before_a, before_b, response, send_list, width):
+def correct(own, other, pair, far, local, through_low, reach_high, back_high, before, far_maps, response, send_list, width):
     size, elements = local.shape
     return pl.pallas_call(
         functools.partial(correct_kernel, width),
@@ -443,7 +457,7 @@
         ),
         name="line_correct",
         compiler_params=pltpu.CompilerParams(vmem_limit_bytes=10 * MIB),
-    )(own, other, crossing, far, local, through_low, reach_high, back_high, before_a, before_b, response, send_list)
+    )(own, other, pair, far, local, through_low, reach_high, back_high, before, far_maps, response, send_list)
 
 
 def near_kernel(width, rounded, vector, edges, diag, lower, upper, out):
@@ -515,7 +529,7 @@
 
 
 def add_faces(partial, faces, picked, out):
-    count, size, elements = picked.shape
+    count, size, _ = picked.shape
     reads = [functools.partial(lambda f, at, i: faces[f, at + i], f) for f in range(count)]
 
     @pl.loop(0, size // SUB)
@@ -674,16 +688,9 @@
     return pairs
 
 
-def sum_all(value):
+def sum_over(value, groups):
     axes = ("dom", "line")
-    doms, lines = lax.axis_size("dom"), lax.axis_size("line")
-    total = doms * lines
-    bits = []
-    bit = 1
-    while bit < total:
-        bits.append(bit)
-        bit *= 2
-    groups = [bits[:1]] + [bits[n : n + 2] for n in range(1, len(bits), 2)]
+    total = lax.axis_size("dom") * lax.axis_size("line")
     for group in groups:
         masks = [0]
         for bit in group:
@@ -692,22 +699,28 @@
     return value
 
 
-def shards(
+def index_bits(limit):
+    return [1 << n for n in range((limit - 1).bit_length())]
+
+
+def steps(
     right_side, diag_blocks, lower_blocks, upper_blocks, face_blocks, face_nbr, send_list,
     inv_blocks, fwd_blocks, bwd_blocks,
 ):
     width = LINES_DEV
     lines, doms = lax.axis_size("line"), lax.axis_size("dom")
 
-    squares = jnp.broadcast_to(jnp.sum(right_side * right_side), (SUB, right_side.shape[1]))
-    norm = jnp.sqrt(sum_all(squares))
-    fwd_steps, bwd_steps, last_block = step_layouts(fwd_blocks, bwd_blocks, width)
-    before_a = lax.ppermute(last_block, "line", flip(lines, 1))
-    before_b = lax.ppermute(last_block, "line", neighbour_pairs(lines))
-    response, ends = chain_products(fwd_blocks, bwd_blocks, width)
+    bits = index_bits(doms * lines)
+    start, tiles = lax.optimization_barrier((right_side, tile_layouts(fwd_blocks, bwd_blocks)))
+    squares = sum_over(sum_squares(start), [bits[1:3]])
+    squares = sum_over(squares, [bits[n : n + 2] for n in range(3, len(bits), 2)])
+    fwd_steps, bwd_steps, response, ends = chain_products(tiles, width)
     other_ends = lax.ppermute(ends, "line", flip(lines, 1))
-    through_low, through_high, reach_high, back_low, back_high, pair = maps(ends, other_ends, width)
-    far_pair = lax.ppermute(pair, "line", flip(lines, 2))
+    norm = jnp.sqrt(sum_over(squares, [bits[:1]]))
+    through_low, through_high, reach_high, back_low, back_high, before, message = maps(
+        ends, other_ends, width
+    )
+    far_maps = lax.ppermute(message, "line", flip(lines, 2))
 
     local, ends_own, first = sweep(right_side, norm, inv_blocks, fwd_steps, bwd_steps, width)
     basis = [first]
@@ -715,13 +728,11 @@
     for iteration in range(ITERS):
         rounded = iteration == 0
         ends_other = lax.ppermute(ends_own, "line", flip(lines, 1))
-        pair_own, crossing = pair_ends(
-            ends_own, ends_other, through_high, reach_high, back_low, far_pair, width
-        )
+        pair_own = pair_ends(ends_own, ends_other, through_high, reach_high, back_low, width)
         pair_far = lax.ppermute(pair_own, "line", flip(lines, 2))
         direction, edges, sent = correct(
-            ends_own, ends_other, crossing, pair_far, local, through_low, reach_high, back_high,
-            before_a, before_b, response, send_list, width,
+            ends_own, ends_other, pair_own, pair_far, local, through_low, reach_high, back_high,
+            before, far_maps, response, send_list, width,
         )
         search.append(direction)
         got_a = lax.ppermute(sent, "dom", flip(doms, 1))
@@ -733,7 +744,8 @@
                 *given, inv_blocks, fwd_steps, bwd_steps, width, rounded
             )
             basis.append(following)
-    sums = sum_all(closing(*given, basis, rounded))
+    groups = [bits[:1]] + [bits[n : n + 2] for n in range(1, len(bits), 2)]
+    sums = sum_over(closing(*given, basis, rounded), groups)
     update, hessenberg = finish(norm, sums, search)
     return (update, hessenberg)
 
@@ -752,4 +764,4 @@
         P(None, None, ("dom", "line")),
     )
     out_specs = (P(None, ("dom", "line")), P())
-    return jax.shard_map(shards, mesh=mesh, in_specs=in_specs, out_specs=out_specs, check_vma=False)
+    return jax.shard_map(steps, mesh=mesh, in_specs=in_specs, out_specs=out_specs, check_vma=False)

time: 117 us -> 95.6 us (0.82)
  Pallas kernels: 43.3 us -> 27.6 us
  starting transfers between devices: 44.3 us -> 35.7 us
  waiting for transfers between devices: 22.1 us -> 28.7 us
  other arithmetic: 2.69 us -> 0.03 us
    ppermute x30 -> x28, starting transfers between devices: 44.3 us -> 35.7 us  [the longest x14 16.4 us: sum_over(): lax.ppermute(value, axes, flip(total, m))]
    pallas_call x5 -> x6, Pallas kernels: 18 us -> 10.2 us  [the longest x1 7.57 us: chain_products(): pl.pallas_call(functools.partial(chain_kernel, width, size), out_shape=(s...]
    ppermute x30 -> x28, waiting for transfers between devices: 22.1 us -> 28.7 us  [the longest x14 13.5 us: sum_over(): lax.ppermute(value, axes, flip(total, m))]
    pallas_call x2, Pallas kernels: 10.5 us -> 6.45 us  [advance(): pl.pallas_call(functools.partial(advance_kernel, width, rounded), out_sha...]
    pallas_call x1, Pallas kernels: 4.05 us -> 2.03 us  [sweep(): pl.pallas_call(functools.partial(sweep_kernel, width), out_shape=sweep_sh...]
    pallas_call x3, Pallas kernels: 4.11 us -> 2.63 us  [correct(): pl.pallas_call(functools.partial(correct_kernel, width), out_shape=(jax.S...]
    reduce_sum x1 -> x0, other arithmetic: 1.37 us -> none  [shards(): jnp.sum(right_side * right_side)]
    add x5, other arithmetic: 1.31 us -> 0.02 us  [sum_over(): sum((lax.ppermute(value, axes, flip(total, m)) for m in masks[1:]), value)]
  transfers between devices with their start and end apart: 30 -> 28, of which waited for: 16 -> 20; matrix products, arithmetic and copies ran while one was open for 3% -> 0% of each run, Pallas kernels for 14% -> 7%
where the time goes in v1:
time: 95.6 us; the launch traced here: 95.4 us
  starting transfers between devices  35.7 us (37%)
  waiting for transfers between devices  28.7 us (30%)
  Pallas kernels  27.6 us (29%)
  local copies, waits for them, and re-layouts  2.49 us (3%)
    ppermute x14, starting transfers between devices, sum_over(): lax.ppermute(value, axes, flip(total, m))  16.4 us
    ppermute x3, starting transfers between devices, steps(): got_a = lax.ppermute(sent, 'dom', flip(doms, 1))  13.6 us
    ppermute x14, waiting for transfers between devices, sum_over(): lax.ppermute(value, axes, flip(total, m))  13.5 us
    ppermute x3, waiting for transfers between devices, steps(): pair_far = lax.ppermute(pair_own, 'line', flip(lines, 2))  8.82 us
    pallas_call x1, Pallas kernels, chain_products(): pl.pallas_call(functools.partial(chain_kernel, width, size), out_shape=(s...  7.57 us
    pallas_call x2, Pallas kernels, advance(): pl.pallas_call(functools.partial(advance_kernel, width, rounded), out_sha...  6.45 us
    ppermute x3, waiting for transfers between devices, steps(): ends_other = lax.ppermute(ends_own, 'line', flip(lines, 1))  3.33 us
    ppermute x3, waiting for transfers between devices, steps(): got_a = lax.ppermute(sent, 'dom', flip(doms, 1))  3.11 us
  transfers between devices with their start and end apart: 28, of which 20 were waited for; matrix products, arithmetic and copies ran while one was open for 0% of the time, Pallas kernels for 7%

profile of v1, /device:TPU:0, one launch (start us, length us, event | category | flops | bytes accessed | tf_op | source)
XLA Modules:
  0.0 95.4 jit_solution(7906426375962783060)
XLA Ops:
  0.6 1.2 %copy-done.5 = bf16[64,64,128]{2,1,0:T(8,128)(2,1)S(1)} copy-done((bf16[64,64,128]{2,1,0:T(8,128)(2,1)S(1)}, bf16[64,64,128]{2,1,0:T(8,128)(2,1)}, u32[]{:S(2)}) %copy-start.5) | copy-done | bytes 1048600
  1.9 1.2 %copy-done.6 = bf16[64,64,128]{2,1,0:T(8,128)(2,1)S(1)} copy-done((bf16[64,64,128]{2,1,0:T(8,128)(2,1)S(1)}, bf16[64,64,128]{2,1,0:T(8,128)(2,1)}, u32[]{:S(2)}) %copy-start.6) | copy-done | bytes 1048600
  3.1 1.8 %tile_layouts.1.tiles = f32[8192,128]{1,0:T(8,128)S(1)} custom-call(bf16[64,64,128]{2,1,0:T(8,128)(2,1)S(1)} %copy-done.5, bf16[64,64,128]{2,1,0:T(8,128)(2,1)S(1)} %copy-done.6), custom_call_target="tpu_custom_call" | custom-call | flops 4000000 | bytes 10485760 | tf_op jit(solution)/shard_map/tile_layouts/pallas_call | solution.py:140
  5.0 7.6 %chain_products.1 = (bf16[8,8,64,128]{3,2,1,0:T(8,128)(2,1)S(1)}, bf16[8,8,64,128]{3,2,1,0:T(8,128)(2,1)S(1)}, f32[64,128,128]{2,1,0:T(8,128)S(1)}, f32[32,64,128]{2,1,0:T(8,128)S(1)}) custom-call(f32[8192,128]{1,0:T(8,128)S(1)} %tile_layouts.1.tiles), custom_call_target="tpu_custom_call" | custom-call | flops 40000000 | bytes 12582912 | tf_op jit(solution)/shard_map/chain_products/pallas_call | solution.py:252
  13.2 3.4 %collective-permute-start.2 = (f32[8,128]{1,0:T(8,128)S(1)}, f32[8,128]{1,0:T(8,128)S(1)}, u32[]{:S(2)}, u32[]{:S(2)}) collective-permute-start(f32[8,128]{1,0:T(8,128)S(1)} %sum_squares.1), channel_id=1, source_target_pairs={{0,6},{1,7},{2,4},{3,5},{4,2},{5,3},{6,0},{7,1},{8,14},{9,15},{10,... | collective-permute-start | bytes 12296 | tf_op jit(solution)/shard_map/ppermute | solution.py:698
  18.2 2.0 %collective-permute-done.1 = f32[8,128]{1,0:T(8,128)S(1)} collective-permute-done((f32[8,128]{1,0:T(8,128)S(1)}, f32[8,128]{1,0:T(8,128)S(1)}, u32[]{:S(2)}, u32[]{:S(2)}) %collective-permute-start.1) | collective-permute-done | bytes 4128 | tf_op jit(solution)/shard_map/ppermute | solution.py:698
  20.8 3.6 %collective-permute-start.5 = (f32[8,128]{1,0:T(8,128)S(1)}, f32[8,128]{1,0:T(8,128)S(1)}, u32[]{:S(2)}, u32[]{:S(2)}) collective-permute-start(f32[8,128]{1,0:T(8,128)S(1)} %add_add_fusion.3), channel_id=1, source_target_pairs={{0,24},{1,25},{2,26},{3,27},{4,28},{5,29},{6,30},{7,31},{8,16},{9,... | collective-permute-start | bytes 12296 | tf_op jit(solution)/shard_map/ppermute | solution.py:698
  25.2 1.7 %line_maps.1 = (f32[8,64,128]{2,1,0:T(8,128)S(1)}, f32[8,64,128]{2,1,0:T(8,128)S(1)}, f32[8,64,128]{2,1,0:T(8,128)S(1)}, f32[8,64,128]{2,1,0:T(8,128)S(1)}, f32[...) custom-call(f32[32,64,128]{2,1,0:T(8,128)S(1)} %get-tuple-element.38.own, ...), custom_call_target="tpu_custom_call" | custom-call | tf_op jit(solution)/shard_map/line_maps/pallas_call | solution.py:329
  27.3 1.6 %collective-permute-done.4 = f32[8,128]{1,0:T(8,128)S(1)} collective-permute-done((f32[8,128]{1,0:T(8,128)S(1)}, f32[8,128]{1,0:T(8,128)S(1)}, u32[]{:S(2)}, u32[]{:S(2)}) %collective-permute-start.4) | collective-permute-done | bytes 4128 | tf_op jit(solution)/shard_map/ppermute | solution.py:698
  29.0 1.2 %collective-permute-done.6 = f32[8,128]{1,0:T(8,128)S(1)} collective-permute-done((f32[8,128]{1,0:T(8,128)S(1)}, f32[8,128]{1,0:T(8,128)S(1)}, u32[]{:S(2)}, u32[]{:S(2)}) %collective-permute-start.6) | collective-permute-done | bytes 4128 | tf_op jit(solution)/shard_map/ppermute | solution.py:698
  30.2 2.0 %line_sweep.1 = (f32[64,128]{1,0:T(8,128)S(1)}, f32[16,128]{1,0:T(8,128)S(1)}, f32[64,128]{1,0:T(8,128)S(1)}) custom-call(f32[64,128]{1,0:T(8,128)S(1)} %copy-done.7, f32[8,128]{1,0:T(8,128)S(1)} %add_sqrt_fusion.norm, bf16[64,64,128]{2,1,0:T(8,128)(2,1)S(1)} %copy-done.4, bf16[8,8,64,128]{3,2,1,0:T(8,128)(2,1)S(1)} %get-tuple-element.35.fwd_steps, ...), custom_call_target="tpu_custom_call" | custom-call | tf_op jit(solution)/shard_map/line_sweep/pallas_call | solution.py:374
  34.3 3.1 %collective-permute-done.9.far = f32[16,128]{1,0:T(8,128)S(1)} collective-permute-done((f32[16,128]{1,0:T(8,128)S(1)}, f32[16,128]{1,0:T(8,128)S(1)}, u32[]{:S(2)}, u32[]{:S(2)}) %collective-permute-start.9) | collective-permute-done | bytes 8224 | tf_op jit(solution)/shard_map/ppermute | solution.py:732
  39.1 3.0 %collective-permute-start.11 = (f32[64,32]{1,0:T(8,128)S(1)}, f32[64,32]{1,0:T(8,128)S(1)}, u32[]{:S(2)}, u32[]{:S(2)}) collective-permute-start(f32[64,32]{1,0:T(8,128)S(1)} %get-tuple-element.49), channel_id=1, source_target_pairs={{0,4},{4,0},{8,12},{12,8},{16,20},{20,16},{24,28},{28,24},{1,5},{5... | collective-permute-start | bytes 24584 | tf_op jit(solution)/shard_map/ppermute | solution.py:738
  44.0 3.2 %faces_and_sweep.2 = (f32[64,128]{1,0:T(8,128)S(1)}, f32[16,128]{1,0:T(8,128)S(1)}, f32[64,128]{1,0:T(8,128)S(1)}) custom-call(f32[64,128]{1,0:T(8,128)S(1)} %get-tuple-element.48.vector.rest_0_, f32[64,32]{1,0:T(8,128)S(1)} %collective-permute-done.11.got_a, f32[64,32]{1,0:T(8,128)S(1)} %collective-permute-done.12.got_b, s32[4,128]{1,0:T(4,128)S(1)} %copy-done.8, ...), custom_call_target="tpu_custom_call" | custom-call | tf_op jit(solution)/shard_map/faces_and_sweep/pallas_call | solution.py:555
  47.3 1.2 %collective-permute-done.13.other = f32[16,128]{1,0:T(8,128)S(1)} collective-permute-done((f32[16,128]{1,0:T(8,128)S(1)}, f32[16,128]{1,0:T(8,128)S(1)}, u32[]{:S(2)}, u32[]{:S(2)}) %collective-permute-start.13) | collective-permute-done | bytes 8224 | tf_op jit(solution)/shard_map/ppermute | solution.py:730
  48.7 1.2 %collective-permute-start.14 = (f32[16,128]{1,0:T(8,128)S(1)}, f32[16,128]{1,0:T(8,128)S(1)}, u32[]{:S(2)}, u32[]{:S(2)}) collective-permute-start(f32[16,128]{1,0:T(8,128)S(1)} %line_pair.4.pair), channel_id=1, source_target_pairs={{0,2},{1,3},{2,0},{3,1},{4,6},{5,7},{6,4},{7,5},{8,10},{9,11},{10,... | collective-permute-start | bytes 24584 | tf_op jit(solution)/shard_map/ppermute | solution.py:732
  49.9 2.5 %collective-permute-done.14.far = f32[16,128]{1,0:T(8,128)S(1)} collective-permute-done((f32[16,128]{1,0:T(8,128)S(1)}, f32[16,128]{1,0:T(8,128)S(1)}, u32[]{:S(2)}, u32[]{:S(2)}) %collective-permute-start.14) | collective-permute-done | bytes 8224 | tf_op jit(solution)/shard_map/ppermute | solution.py:732
  54.0 6.0 %collective-permute-start.15 = (f32[64,32]{1,0:T(8,128)S(1)}, f32[64,32]{1,0:T(8,128)S(1)}, u32[]{:S(2)}, u32[]{:S(2)}) collective-permute-start(f32[64,32]{1,0:T(8,128)S(1)} %get-tuple-element.54), channel_id=1, source_target_pairs={{0,4},{4,0},{8,12},{12,8},{16,20},{20,16},{24,28},{28,24},{1,5},{5... | collective-permute-start | bytes 24584 | tf_op jit(solution)/shard_map/ppermute | solution.py:738
  60.9 1.0 %collective-permute-done.15.got_a = f32[64,32]{1,0:T(8,128)S(1)} collective-permute-done((f32[64,32]{1,0:T(8,128)S(1)}, f32[64,32]{1,0:T(8,128)S(1)}, u32[]{:S(2)}, u32[]{:S(2)}) %collective-permute-start.15) | collective-permute-done | bytes 8224 | tf_op jit(solution)/shard_map/ppermute | solution.py:738
  61.9 3.2 %faces_and_sweep.3 = (f32[64,128]{1,0:T(8,128)S(1)}, f32[16,128]{1,0:T(8,128)S(1)}, f32[64,128]{1,0:T(8,128)S(1)}) custom-call(f32[64,128]{1,0:T(8,128)S(1)} %get-tuple-element.53.vector.rest_1_, f32[64,32]{1,0:T(8,128)S(1)} %collective-permute-done.15.got_a, f32[64,32]{1,0:T(8,128)S(1)} %collective-permute-done.16.got_b, s32[4,128]{1,0:T(4,128)S(1)} %copy-done.8, ...), custom_call_target="tpu_custom_call" | custom-call | tf_op jit(solution)/shard_map/faces_and_sweep/pallas_call | solution.py:555
  65.2 1.2 %collective-permute-done.17.other = f32[16,128]{1,0:T(8,128)S(1)} collective-permute-done((f32[16,128]{1,0:T(8,128)S(1)}, f32[16,128]{1,0:T(8,128)S(1)}, u32[]{:S(2)}, u32[]{:S(2)}) %collective-permute-start.17) | collective-permute-done | bytes 8224 | tf_op jit(solution)/shard_map/ppermute | solution.py:730
  67.2 3.1 %collective-permute-done.18.far = f32[16,128]{1,0:T(8,128)S(1)} collective-permute-done((f32[16,128]{1,0:T(8,128)S(1)}, f32[16,128]{1,0:T(8,128)S(1)}, u32[]{:S(2)}, u32[]{:S(2)}) %collective-permute-start.18) | collective-permute-done | bytes 8224 | tf_op jit(solution)/shard_map/ppermute | solution.py:732
  71.9 4.5 %collective-permute-start.19 = (f32[64,32]{1,0:T(8,128)S(1)}, f32[64,32]{1,0:T(8,128)S(1)}, u32[]{:S(2)}, u32[]{:S(2)}) collective-permute-start(f32[64,32]{1,0:T(8,128)S(1)} %get-tuple-element.59), channel_id=1, source_target_pairs={{0,4},{4,0},{8,12},{12,8},{16,20},{20,16},{24,28},{28,24},{1,5},{5... | collective-permute-start | bytes 24584 | tf_op jit(solution)/shard_map/ppermute | solution.py:738
  78.3 1.3 %faces_and_sums.1 = f32[16,128]{1,0:T(8,128)S(1)} custom-call(f32[64,128]{1,0:T(8,128)S(1)} %get-tuple-element.58.vector.rest_2_, f32[64,32]{1,0:T(8,128)S(1)} %collective-permute-done.19.got_a, f32[64,32]{1,0:T(8,128)S(1)} %collective-permute-done.20.got_b, s32[4,128]{1,0:T(4,128)S(1)} %copy-done.8, f32[64,128]{1,0:T(8,128)S(1)} %near_faces.5.partial, ...), custom_call_target="tpu_custom_call" | custom-call | tf_op jit(solution)/shard_map/faces_and_sums/pallas_call | solution.py:588
  79.6 1.2 %collective-permute-done.21 = f32[16,128]{1,0:T(8,128)S(1)} collective-permute-done((f32[16,128]{1,0:T(8,128)S(1)}, f32[16,128]{1,0:T(8,128)S(1)}, u32[]{:S(2)}, u32[]{:S(2)}) %collective-permute-start.21) | collective-permute-done | bytes 8224 | tf_op jit(solution)/shard_map/ppermute | solution.py:698
  80.8 2.0 %collective-permute-start.24 = (f32[16,128]{1,0:T(8,128)S(1)}, f32[16,128]{1,0:T(8,128)S(1)}, u32[]{:S(2)}, u32[]{:S(2)}) collective-permute-start(f32[16,128]{1,0:T(8,128)S(1)} %add.49), channel_id=1, source_target_pairs={{0,6},{1,7},{2,4},{3,5},{4,2},{5,3},{6,0},{7,1},{8,14},{9,15},{10,... | collective-permute-start | bytes 24584 | tf_op jit(solution)/shard_map/ppermute | solution.py:698
  82.8 1.5 %collective-permute-start.22 = (f32[16,128]{1,0:T(8,128)S(1)}, f32[16,128]{1,0:T(8,128)S(1)}, u32[]{:S(2)}, u32[]{:S(2)}) collective-permute-start(f32[16,128]{1,0:T(8,128)S(1)} %add.49), channel_id=1, source_target_pairs={{0,2},{1,3},{2,0},{3,1},{4,6},{5,7},{6,4},{7,5},{8,10},{9,11},{10,... | collective-permute-start | bytes 24584 | tf_op jit(solution)/shard_map/ppermute | solution.py:698
  84.2 1.1 %collective-permute-done.24 = f32[16,128]{1,0:T(8,128)S(1)} collective-permute-done((f32[16,128]{1,0:T(8,128)S(1)}, f32[16,128]{1,0:T(8,128)S(1)}, u32[]{:S(2)}, u32[]{:S(2)}) %collective-permute-start.24) | collective-permute-done | bytes 8224 | tf_op jit(solution)/shard_map/ppermute | solution.py:698
  85.3 1.1 %collective-permute-done.23 = f32[16,128]{1,0:T(8,128)S(1)} collective-permute-done((f32[16,128]{1,0:T(8,128)S(1)}, f32[16,128]{1,0:T(8,128)S(1)}, u32[]{:S(2)}, u32[]{:S(2)}) %collective-permute-start.23) | collective-permute-done | bytes 8224 | tf_op jit(solution)/shard_map/ppermute | solution.py:698
  86.4 3.7 %collective-permute-start.27 = (f32[16,128]{1,0:T(8,128)S(1)}, f32[16,128]{1,0:T(8,128)S(1)}, u32[]{:S(2)}, u32[]{:S(2)}) collective-permute-start(f32[16,128]{1,0:T(8,128)S(1)} %add_add_fusion.1), channel_id=1, source_target_pairs={{0,24},{1,25},{2,26},{3,27},{4,28},{5,29},{6,30},{7,31},{8,16},{9,... | collective-permute-start | bytes 24584 | tf_op jit(solution)/shard_map/ppermute | solution.py:698
  90.8 1.1 %collective-permute-done.27 = f32[16,128]{1,0:T(8,128)S(1)} collective-permute-done((f32[16,128]{1,0:T(8,128)S(1)}, f32[16,128]{1,0:T(8,128)S(1)}, u32[]{:S(2)}, u32[]{:S(2)}) %collective-permute-start.27) | collective-permute-done | bytes 8224 | tf_op jit(solution)/shard_map/ppermute | solution.py:698
  91.9 2.8 %collective-permute-done.26 = f32[16,128]{1,0:T(8,128)S(1)} collective-permute-done((f32[16,128]{1,0:T(8,128)S(1)}, f32[16,128]{1,0:T(8,128)S(1)}, u32[]{:S(2)}, u32[]{:S(2)}) %collective-permute-start.26) | collective-permute-done | bytes 8224 | tf_op jit(solution)/shard_map/ppermute | solution.py:698
  (68 shorter events, 18.2 us)
Async XLA Ops:
  4.9 25.2 %copy-start.4 = (bf16[64,64,128]{2,1,0:T(8,128)(2,1)S(1)}, bf16[64,64,128]{2,1,0:T(8,128)(2,1)}, u32[]{:S(2)}) copy-start(bf16[64,64,128]{2,1,0:T(8,128)(2,1)} %inv.5) | copy-start | bytes 3145732
  5.0 32.5 %copy-start.9 = (s32[2,16]{1,0:T(2,128)S(1)}, s32[2,16]{1,0:T(2,128)}, u32[]{:S(2)}) copy-start(s32[2,16]{1,0:T(2,128)} %send_list.5) | copy-start | bytes 388
  12.5 12.6 %collective-permute-start.8 = (f32[32,64,128]{2,1,0:T(8,128)S(1)}, f32[32,64,128]{2,1,0:T(8,128)S(1)}, u32[]{:S(2)}, u32[]{:S(2)}) collective-permute-start(f32[32,64,128]{2,1,0:T(8,128)S(1)} %get-tuple-element.38.own), channel_id=1, source_target_pairs={{0,1},{1,0},{2,3},{3,2},{4,5},{5,4},{6,7},{7,6},{8,9},{9,8},{10,11... | collective-permute-start | bytes 3145736 | tf_op jit(solution)/shard_map/ppermute | solution.py:718
  13.2 5.0 %collective-permute-start.2 = (f32[8,128]{1,0:T(8,128)S(1)}, f32[8,128]{1,0:T(8,128)S(1)}, u32[]{:S(2)}, u32[]{:S(2)}) collective-permute-start(f32[8,128]{1,0:T(8,128)S(1)} %sum_squares.1), channel_id=1, source_target_pairs={{0,6},{1,7},{2,4},{3,5},{4,2},{5,3},{6,0},{7,1},{8,14},{9,15},{10,... | collective-permute-start | bytes 12296 | tf_op jit(solution)/shard_map/ppermute | solution.py:698
  16.6 3.6 %collective-permute-start.1 = (f32[8,128]{1,0:T(8,128)S(1)}, f32[8,128]{1,0:T(8,128)S(1)}, u32[]{:S(2)}, u32[]{:S(2)}) collective-permute-start(f32[8,128]{1,0:T(8,128)S(1)} %sum_squares.1), channel_id=1, source_target_pairs={{0,4},{1,5},{2,6},{3,7},{4,0},{5,1},{6,2},{7,3},{8,12},{9,13},{10,... | collective-permute-start | bytes 12296 | tf_op jit(solution)/shard_map/ppermute | solution.py:698
  17.2 3.6 %collective-permute-start = (f32[8,128]{1,0:T(8,128)S(1)}, f32[8,128]{1,0:T(8,128)S(1)}, u32[]{:S(2)}, u32[]{:S(2)}) collective-permute-start(f32[8,128]{1,0:T(8,128)S(1)} %sum_squares.1), channel_id=1, source_target_pairs={{0,2},{1,3},{2,0},{3,1},{4,6},{5,7},{6,4},{7,5},{8,10},{9,11},{10,... | collective-permute-start | bytes 12296 | tf_op jit(solution)/shard_map/ppermute | solution.py:698
  20.8 6.5 %collective-permute-start.5 = (f32[8,128]{1,0:T(8,128)S(1)}, f32[8,128]{1,0:T(8,128)S(1)}, u32[]{:S(2)}, u32[]{:S(2)}) collective-permute-start(f32[8,128]{1,0:T(8,128)S(1)} %add_add_fusion.3), channel_id=1, source_target_pairs={{0,24},{1,25},{2,26},{3,27},{4,28},{5,29},{6,30},{7,31},{8,16},{9,... | collective-permute-start | bytes 12296 | tf_op jit(solution)/shard_map/ppermute | solution.py:698
  24.4 4.5 %collective-permute-start.4 = (f32[8,128]{1,0:T(8,128)S(1)}, f32[8,128]{1,0:T(8,128)S(1)}, u32[]{:S(2)}, u32[]{:S(2)}) collective-permute-start(f32[8,128]{1,0:T(8,128)S(1)} %add_add_fusion.3), channel_id=1, source_target_pairs={{0,16},{1,17},{2,18},{3,19},{4,20},{5,21},{6,22},{7,23},{8,24},{9,... | collective-permute-start | bytes 12296 | tf_op jit(solution)/shard_map/ppermute | solution.py:698
  24.4 4.5 %collective-permute-start.3 = (f32[8,128]{1,0:T(8,128)S(1)}, f32[8,128]{1,0:T(8,128)S(1)}, u32[]{:S(2)}, u32[]{:S(2)}) collective-permute-start(f32[8,128]{1,0:T(8,128)S(1)} %add_add_fusion.3), channel_id=1, source_target_pairs={{0,8},{1,9},{2,10},{3,11},{4,12},{5,13},{6,14},{7,15},{8,0},{9,1},... | collective-permute-start | bytes 12296 | tf_op jit(solution)/shard_map/ppermute | solution.py:698
  26.9 10.5 %collective-permute-start.10 = (bf16[24,64,128]{2,1,0:T(8,128)(2,1)S(1)}, bf16[24,64,128]{2,1,0:T(8,128)(2,1)S(1)}, u32[]{:S(2)}, u32[]{:S(2)}) collective-permute-start(bf16[24,64,128]{2,1,0:T(8,128)(2,1)S(1)} %get-tuple-element.46), channel_id=1, source_target_pairs={{0,2},{1,3},{2,0},{3,1},{4,6},{5,7},{6,4},{7,5},{8,10},{9,11},{10,... | collective-permute-start | bytes 1179656 | tf_op jit(solution)/shard_map/ppermute | solution.py:723
  28.9 1.2 %collective-permute-start.6 = (f32[8,128]{1,0:T(8,128)S(1)}, f32[8,128]{1,0:T(8,128)S(1)}, u32[]{:S(2)}, u32[]{:S(2)}) collective-permute-start(f32[8,128]{1,0:T(8,128)S(1)} %add_add_fusion.2), channel_id=1, source_target_pairs={{0,1},{1,0},{2,3},{3,2},{4,5},{5,4},{6,7},{7,6},{8,9},{9,8},{10,11... | collective-permute-start | bytes 12296 | tf_op jit(solution)/shard_map/ppermute | solution.py:698
  30.2 12.0 %copy-start.1 = (bf16[64,64,128]{2,1,0:T(8,128)(2,1)S(1)}, bf16[64,64,128]{2,1,0:T(8,128)(2,1)}, u32[]{:S(2)}) copy-start(bf16[64,64,128]{2,1,0:T(8,128)(2,1)} %diag.5) | copy-start | bytes 3145732
  30.2 12.0 %copy-start.2 = (bf16[64,64,128]{2,1,0:T(8,128)(2,1)S(1)}, bf16[64,64,128]{2,1,0:T(8,128)(2,1)}, u32[]{:S(2)}) copy-start(bf16[64,64,128]{2,1,0:T(8,128)(2,1)} %lower.5) | copy-start | bytes 3145732
  32.2 1.2 %collective-permute-start.7 = (f32[16,128]{1,0:T(8,128)S(1)}, f32[16,128]{1,0:T(8,128)S(1)}, u32[]{:S(2)}, u32[]{:S(2)}) collective-permute-start(f32[16,128]{1,0:T(8,128)S(1)} %get-tuple-element.37.own), channel_id=1, source_target_pairs={{0,1},{1,0},{2,3},{3,2},{4,5},{5,4},{6,7},{7,6},{8,9},{9,8},{10,11... | collective-permute-start | bytes 24584 | tf_op jit(solution)/shard_map/ppermute | solution.py:730
  33.7 3.7 %collective-permute-start.9 = (f32[16,128]{1,0:T(8,128)S(1)}, f32[16,128]{1,0:T(8,128)S(1)}, u32[]{:S(2)}, u32[]{:S(2)}) collective-permute-start(f32[16,128]{1,0:T(8,128)S(1)} %line_pair.3.pair), channel_id=1, source_target_pairs={{0,2},{1,3},{2,0},{3,1},{4,6},{5,7},{6,4},{7,5},{8,10},{9,11},{10,... | collective-permute-start | bytes 24584 | tf_op jit(solution)/shard_map/ppermute | solution.py:732
  38.3 4.7 %collective-permute-start.12 = (f32[64,32]{1,0:T(8,128)S(1)}, f32[64,32]{1,0:T(8,128)S(1)}, u32[]{:S(2)}, u32[]{:S(2)}) collective-permute-start(f32[64,32]{1,0:T(8,128)S(1)} %get-tuple-element.49), channel_id=1, source_target_pairs={{0,0},{4,8},{8,4},{12,16},{16,12},{20,24},{24,20},{28,28},{1,1},{5... | collective-permute-start | bytes 24584 | tf_op jit(solution)/shard_map/ppermute | solution.py:739
  39.1 4.9 %collective-permute-start.11 = (f32[64,32]{1,0:T(8,128)S(1)}, f32[64,32]{1,0:T(8,128)S(1)}, u32[]{:S(2)}, u32[]{:S(2)}) collective-permute-start(f32[64,32]{1,0:T(8,128)S(1)} %get-tuple-element.49), channel_id=1, source_target_pairs={{0,4},{4,0},{8,12},{12,8},{16,20},{20,16},{24,28},{28,24},{1,5},{5... | collective-permute-start | bytes 24584 | tf_op jit(solution)/shard_map/ppermute | solution.py:738
  47.2 1.2 %collective-permute-start.13 = (f32[16,128]{1,0:T(8,128)S(1)}, f32[16,128]{1,0:T(8,128)S(1)}, u32[]{:S(2)}, u32[]{:S(2)}) collective-permute-start(f32[16,128]{1,0:T(8,128)S(1)} %get-tuple-element.51.own), channel_id=1, source_target_pairs={{0,1},{1,0},{2,3},{3,2},{4,5},{5,4},{6,7},{7,6},{8,9},{9,8},{10,11... | collective-permute-start | bytes 24584 | tf_op jit(solution)/shard_map/ppermute | solution.py:730
  48.7 3.7 %collective-permute-start.14 = (f32[16,128]{1,0:T(8,128)S(1)}, f32[16,128]{1,0:T(8,128)S(1)}, u32[]{:S(2)}, u32[]{:S(2)}) collective-permute-start(f32[16,128]{1,0:T(8,128)S(1)} %line_pair.4.pair), channel_id=1, source_target_pairs={{0,2},{1,3},{2,0},{3,1},{4,6},{5,7},{6,4},{7,5},{8,10},{9,11},{10,... | collective-permute-start | bytes 24584 | tf_op jit(solution)/shard_map/ppermute | solution.py:732
  53.3 7.6 %collective-permute-start.16 = (f32[64,32]{1,0:T(8,128)S(1)}, f32[64,32]{1,0:T(8,128)S(1)}, u32[]{:S(2)}, u32[]{:S(2)}) collective-permute-start(f32[64,32]{1,0:T(8,128)S(1)} %get-tuple-element.54), channel_id=1, source_target_pairs={{0,0},{4,8},{8,4},{12,16},{16,12},{20,24},{24,20},{28,28},{1,1},{5... | collective-permute-start | bytes 24584 | tf_op jit(solution)/shard_map/ppermute | solution.py:739
  54.0 7.9 %collective-permute-start.15 = (f32[64,32]{1,0:T(8,128)S(1)}, f32[64,32]{1,0:T(8,128)S(1)}, u32[]{:S(2)}, u32[]{:S(2)}) collective-permute-start(f32[64,32]{1,0:T(8,128)S(1)} %get-tuple-element.54), channel_id=1, source_target_pairs={{0,4},{4,0},{8,12},{12,8},{16,20},{20,16},{24,28},{28,24},{1,5},{5... | collective-permute-start | bytes 24584 | tf_op jit(solution)/shard_map/ppermute | solution.py:738
  65.1 1.2 %collective-permute-start.17 = (f32[16,128]{1,0:T(8,128)S(1)}, f32[16,128]{1,0:T(8,128)S(1)}, u32[]{:S(2)}, u32[]{:S(2)}) collective-permute-start(f32[16,128]{1,0:T(8,128)S(1)} %get-tuple-element.56.own), channel_id=1, source_target_pairs={{0,1},{1,0},{2,3},{3,2},{4,5},{5,4},{6,7},{7,6},{8,9},{9,8},{10,11... | collective-permute-start | bytes 24584 | tf_op jit(solution)/shard_map/ppermute | solution.py:730
  66.6 3.7 %collective-permute-start.18 = (f32[16,128]{1,0:T(8,128)S(1)}, f32[16,128]{1,0:T(8,128)S(1)}, u32[]{:S(2)}, u32[]{:S(2)}) collective-permute-start(f32[16,128]{1,0:T(8,128)S(1)} %line_pair.5.pair), channel_id=1, source_target_pairs={{0,2},{1,3},{2,0},{3,1},{4,6},{5,7},{6,4},{7,5},{8,10},{9,11},{10,... | collective-permute-start | bytes 24584 | tf_op jit(solution)/shard_map/ppermute | solution.py:732
  71.2 6.0 %collective-permute-start.20 = (f32[64,32]{1,0:T(8,128)S(1)}, f32[64,32]{1,0:T(8,128)S(1)}, u32[]{:S(2)}, u32[]{:S(2)}) collective-permute-start(f32[64,32]{1,0:T(8,128)S(1)} %get-tuple-element.59), channel_id=1, source_target_pairs={{0,0},{4,8},{8,4},{12,16},{16,12},{20,24},{24,20},{28,28},{1,1},{5... | collective-permute-start | bytes 24584 | tf_op jit(solution)/shard_map/ppermute | solution.py:739
  71.9 6.4 %collective-permute-start.19 = (f32[64,32]{1,0:T(8,128)S(1)}, f32[64,32]{1,0:T(8,128)S(1)}, u32[]{:S(2)}, u32[]{:S(2)}) collective-permute-start(f32[64,32]{1,0:T(8,128)S(1)} %get-tuple-element.59), channel_id=1, source_target_pairs={{0,4},{4,0},{8,12},{12,8},{16,20},{20,16},{24,28},{28,24},{1,5},{5... | collective-permute-start | bytes 24584 | tf_op jit(solution)/shard_map/ppermute | solution.py:738
  79.6 1.2 %collective-permute-start.21 = (f32[16,128]{1,0:T(8,128)S(1)}, f32[16,128]{1,0:T(8,128)S(1)}, u32[]{:S(2)}, u32[]{:S(2)}) collective-permute-start(f32[16,128]{1,0:T(8,128)S(1)} %faces_and_sums.1), channel_id=1, source_target_pairs={{0,1},{1,0},{2,3},{3,2},{4,5},{5,4},{6,7},{7,6},{8,9},{9,8},{10,11... | collective-permute-start | bytes 24584 | tf_op jit(solution)/shard_map/ppermute | solution.py:698
  80.8 4.5 %collective-permute-start.24 = (f32[16,128]{1,0:T(8,128)S(1)}, f32[16,128]{1,0:T(8,128)S(1)}, u32[]{:S(2)}, u32[]{:S(2)}) collective-permute-start(f32[16,128]{1,0:T(8,128)S(1)} %add.49), channel_id=1, source_target_pairs={{0,6},{1,7},{2,4},{3,5},{4,2},{5,3},{6,0},{7,1},{8,14},{9,15},{10,... | collective-permute-start | bytes 24584 | tf_op jit(solution)/shard_map/ppermute | solution.py:698
  82.7 3.7 %collective-permute-start.23 = (f32[16,128]{1,0:T(8,128)S(1)}, f32[16,128]{1,0:T(8,128)S(1)}, u32[]{:S(2)}, u32[]{:S(2)}) collective-permute-start(f32[16,128]{1,0:T(8,128)S(1)} %add.49), channel_id=1, source_target_pairs={{0,4},{1,5},{2,6},{3,7},{4,0},{5,1},{6,2},{7,3},{8,12},{9,13},{10,... | collective-permute-start | bytes 24584 | tf_op jit(solution)/shard_map/ppermute | solution.py:698
  82.8 3.7 %collective-permute-start.22 = (f32[16,128]{1,0:T(8,128)S(1)}, f32[16,128]{1,0:T(8,128)S(1)}, u32[]{:S(2)}, u32[]{:S(2)}) collective-permute-start(f32[16,128]{1,0:T(8,128)S(1)} %add.49), channel_id=1, source_target_pairs={{0,2},{1,3},{2,0},{3,1},{4,6},{5,7},{6,4},{7,5},{8,10},{9,11},{10,... | collective-permute-start | bytes 24584 | tf_op jit(solution)/shard_map/ppermute | solution.py:698
  86.4 5.5 %collective-permute-start.27 = (f32[16,128]{1,0:T(8,128)S(1)}, f32[16,128]{1,0:T(8,128)S(1)}, u32[]{:S(2)}, u32[]{:S(2)}) collective-permute-start(f32[16,128]{1,0:T(8,128)S(1)} %add_add_fusion.1), channel_id=1, source_target_pairs={{0,24},{1,25},{2,26},{3,27},{4,28},{5,29},{6,30},{7,31},{8,16},{9,... | collective-permute-start | bytes 24584 | tf_op jit(solution)/shard_map/ppermute | solution.py:698
  90.1 4.5 %collective-permute-start.26 = (f32[16,128]{1,0:T(8,128)S(1)}, f32[16,128]{1,0:T(8,128)S(1)}, u32[]{:S(2)}, u32[]{:S(2)}) collective-permute-start(f32[16,128]{1,0:T(8,128)S(1)} %add_add_fusion.1), channel_id=1, source_target_pairs={{0,16},{1,17},{2,18},{3,19},{4,20},{5,21},{6,22},{7,23},{8,24},{9,... | collective-permute-start | bytes 24584 | tf_op jit(solution)/shard_map/ppermute | solution.py:698
  90.2 4.5 %collective-permute-start.25 = (f32[16,128]{1,0:T(8,128)S(1)}, f32[16,128]{1,0:T(8,128)S(1)}, u32[]{:S(2)}, u32[]{:S(2)}) collective-permute-start(f32[16,128]{1,0:T(8,128)S(1)} %add_add_fusion.1), channel_id=1, source_target_pairs={{0,8},{1,9},{2,10},{3,11},{4,12},{5,13},{6,14},{7,15},{8,0},{9,1},... | collective-permute-start | bytes 24584 | tf_op jit(solution)/shard_map/ppermute | solution.py:698
  (6 other events, 37.7 us)

commit v2 on v1

--- a/solution.py
+++ b/solution.py
@@ -12,6 +12,7 @@
 LINES_DEV = 16
 SUB = 8
 MIB = 1 << 20
+INDEPENDENT = 0.01
 HIGHEST = lax.Precision.HIGHEST
 F32 = jnp.float32
 BF16 = jnp.bfloat16
@@ -158,6 +159,7 @@
         out_shape=jax.ShapeDtypeStruct((SUB, vector.shape[1]), F32),
         name="sum_squares",
         compiler_params=pltpu.CompilerParams(vmem_limit_bytes=MIB),
+        cost_estimate=pl.CostEstimate(flops=10**10, bytes_accessed=64 * MIB, transcendentals=0),
     )(vector)
 
 
@@ -613,7 +615,7 @@
 
 
 def finish_kernel(iters, norm, sums, *rest):
-    search, (update, hessenberg) = rest[:iters], rest[iters:]
+    search, (update, hessenberg, quality) = rest[:iters], rest[iters:]
     count = iters + 1
     entry = {}
     n = 0
@@ -622,6 +624,11 @@
             entry[i, j] = sums[n : n + 1, :]
             n += 1
     tri = cholesky(entry, count)
+    worst = tri[0, 0] * tri[0, 0] / entry[0, 0]
+    for i in range(1, count):
+        ratio = tri[i, i] * tri[i, i] / entry[i, i]
+        worst = jnp.where(ratio > worst, worst, ratio)
+    quality[...] = jnp.broadcast_to(worst, quality.shape)
     hess = {}
     for j in range(iters):
         for i in range(j + 2):
@@ -670,6 +677,7 @@
         out_shape=(
             jax.ShapeDtypeStruct((size, elements), F32),
             jax.ShapeDtypeStruct((iters + 1, iters), F32),
+            jax.ShapeDtypeStruct((1, elements), F32),
         ),
         name="solve_and_update",
         compiler_params=pltpu.CompilerParams(vmem_limit_bytes=2 * MIB),
@@ -695,7 +703,10 @@
         masks = [0]
         for bit in group:
             masks = masks + [m | bit for m in masks]
-        value = sum((lax.ppermute(value, axes, flip(total, m)) for m in masks[1:]), value)
+        terms = [value] + [lax.ppermute(value, axes, flip(total, m)) for m in masks[1:]]
+        while len(terms) > 1:
+            terms = [terms[t] + terms[t + 1] for t in range(0, len(terms), 2)]
+        value = terms[0]
     return value
 
 
@@ -703,51 +714,111 @@
     return [1 << n for n in range((limit - 1).bit_length())]
 
 
-def steps(
-    right_side, diag_blocks, lower_blocks, upper_blocks, face_blocks, face_nbr, send_list,
-    inv_blocks, fwd_blocks, bwd_blocks,
-):
-    width = LINES_DEV
+def set_up(fwd_blocks, bwd_blocks, right_side, width):
     lines, doms = lax.axis_size("line"), lax.axis_size("dom")
-
     bits = index_bits(doms * lines)
-    start, tiles = lax.optimization_barrier((right_side, tile_layouts(fwd_blocks, bwd_blocks)))
-    squares = sum_over(sum_squares(start), [bits[1:3]])
+    squares = sum_over(sum_squares(right_side), [bits[1:3]])
+    tiles = tile_layouts(fwd_blocks, bwd_blocks)
+    fwd_steps, bwd_steps, response, ends = chain_products(tiles, width)
     squares = sum_over(squares, [bits[n : n + 2] for n in range(3, len(bits), 2)])
-    fwd_steps, bwd_steps, response, ends = chain_products(tiles, width)
     other_ends = lax.ppermute(ends, "line", flip(lines, 1))
     norm = jnp.sqrt(sum_over(squares, [bits[:1]]))
     through_low, through_high, reach_high, back_low, back_high, before, message = maps(
         ends, other_ends, width
     )
     far_maps = lax.ppermute(message, "line", flip(lines, 2))
-
-    local, ends_own, first = sweep(right_side, norm, inv_blocks, fwd_steps, bwd_steps, width)
+    sweeps = (fwd_steps, bwd_steps)
+    pairs = (through_high, reach_high, back_low)
+    rest = (through_low, reach_high, back_high, before, far_maps, response)
+    return norm, sweeps, pairs, rest
+
+
+def finish_solve(local, ends_own, pairs, rest, send_list, width):
+    lines, doms = lax.axis_size("line"), lax.axis_size("dom")
+    ends_other = lax.ppermute(ends_own, "line", flip(lines, 1))
+    pair_own = pair_ends(ends_own, ends_other, *pairs, width)
+    pair_far = lax.ppermute(pair_own, "line", flip(lines, 2))
+    direction, edges, sent = correct(
+        ends_own, ends_other, pair_own, pair_far, local, *rest, send_list, width
+    )
+    got_a = lax.ppermute(sent, "dom", flip(doms, 1))
+    got_b = lax.ppermute(sent, "dom", neighbour_pairs(doms))
+    return direction, edges, got_a, got_b
+
+
+def power_basis(
+    right_side, diag_blocks, lower_blocks, upper_blocks, face_blocks, face_nbr, send_list,
+    inv_blocks, fwd_blocks, bwd_blocks,
+):
+    width = LINES_DEV
+    bits = index_bits(lax.axis_size("dom") * lax.axis_size("line"))
+    norm, sweeps, pairs, rest = set_up(fwd_blocks, bwd_blocks, right_side, width)
+    local, ends_own, first = sweep(right_side, norm, inv_blocks, *sweeps, width)
     basis = [first]
     search = []
     for iteration in range(ITERS):
         rounded = iteration == 0
-        ends_other = lax.ppermute(ends_own, "line", flip(lines, 1))
-        pair_own = pair_ends(ends_own, ends_other, through_high, reach_high, back_low, width)
-        pair_far = lax.ppermute(pair_own, "line", flip(lines, 2))
-        direction, edges, sent = correct(
-            ends_own, ends_other, pair_own, pair_far, local, through_low, reach_high, back_high,
-            before, far_maps, response, send_list, width,
-        )
+        direction, edges, *got = finish_solve(local, ends_own, pairs, rest, send_list, width)
         search.append(direction)
-        got_a = lax.ppermute(sent, "dom", flip(doms, 1))
-        got_b = lax.ppermute(sent, "dom", neighbour_pairs(doms))
         partial = near(direction, edges, diag_blocks, lower_blocks, upper_blocks, width, rounded)
-        given = (direction, got_a, got_b, face_nbr, partial, face_blocks)
+        given = (direction, *got, face_nbr, partial, face_blocks)
         if iteration + 1 < ITERS:
-            local, ends_own, following = advance(
-                *given, inv_blocks, fwd_steps, bwd_steps, width, rounded
-            )
+            local, ends_own, following = advance(*given, inv_blocks, *sweeps, width, rounded)
             basis.append(following)
-    groups = [bits[:1]] + [bits[n : n + 2] for n in range(1, len(bits), 2)]
-    sums = sum_over(closing(*given, basis, rounded), groups)
-    update, hessenberg = finish(norm, sums, search)
-    return (update, hessenberg)
+    groups = [bits[n : n + 2] for n in range(1, len(bits), 2)] + [bits[:1]]
+    return finish(norm, sum_over(closing(*given, basis, rounded), groups), search)
+
+
+def orthogonal_basis(
+    right_side, diag_blocks, lower_blocks, upper_blocks, face_blocks, face_nbr, send_list,
+    inv_blocks, fwd_blocks, bwd_blocks,
+):
+    width = LINES_DEV
+    _, elements = right_side.shape
+    bits = index_bits(lax.axis_size("dom") * lax.axis_size("line"))
+
+    def total(product):
+        value = jnp.broadcast_to(jnp.sum(product), (SUB, elements))
+        return sum_over(value, [[bit] for bit in bits])
+
+    norm, sweeps, pairs, rest = set_up(fwd_blocks, bwd_blocks, right_side, width)
+    local, ends_own, first = sweep(right_side, norm, inv_blocks, *sweeps, width)
+    basis = [first]
+    search = []
+    hess = {}
+    for iteration in range(ITERS):
+        direction, edges, *got = finish_solve(local, ends_own, pairs, rest, send_list, width)
+        search.append(direction)
+        partial = near(direction, edges, diag_blocks, lower_blocks, upper_blocks, width, True)
+        given = (direction, *got, face_nbr, partial, face_blocks)
+        vector = advance(*given, inv_blocks, *sweeps, width, True)[2]
+        for column in range(iteration + 1):
+            weight = total(vector * basis[column])
+            hess[column, iteration] = weight[0, 0]
+            vector = vector - weight[0:1] * basis[column]
+        height = jnp.sqrt(total(vector * vector))
+        hess[iteration + 1, iteration] = height[0, 0]
+        if iteration + 1 < ITERS:
+            local, ends_own, following = sweep(vector, height, inv_blocks, *sweeps, width)
+            basis.append(following)
+    zero = jnp.zeros((), F32)
+    rows = [[hess.get((i, j), zero) for j in range(ITERS)] for i in range(ITERS + 1)]
+    hessenberg = jnp.stack([jnp.stack(row) for row in rows])
+    normal = jnp.dot(hessenberg.T, hessenberg, precision=HIGHEST)
+    factor = jnp.linalg.cholesky(normal)
+    coeffs = jax.scipy.linalg.cho_solve((factor, True), norm[0, 0] * hessenberg[0])
+    update = sum(coeffs[n] * search[n] for n in range(ITERS))
+    return update, hessenberg
+
+
+def shards(*arrays):
+    update, hessenberg, quality = power_basis(*arrays)
+    return lax.cond(
+        quality[0, 0] > INDEPENDENT,
+        lambda *_: (update, hessenberg),
+        orthogonal_basis,
+        *arrays,
+    )
 
 
 def solution(mesh):
@@ -764,4 +835,4 @@
         P(None, None, ("dom", "line")),
     )
     out_specs = (P(None, ("dom", "line")), P())
-    return jax.shard_map(steps, mesh=mesh, in_specs=in_specs, out_specs=out_specs, check_vma=False)
+    return jax.shard_map(shards, mesh=mesh, in_specs=in_specs, out_specs=out_specs, check_vma=False)

time: 95.6 us -> 97.2 us (1.017)
  waiting for transfers between devices: 28.7 us -> 31.6 us
  local copies, waits for them, and re-layouts: 2.49 us -> 0.67 us
  Pallas kernels: 27.6 us -> 28.8 us
    ppermute x14, starting transfers between devices: 19.3 us -> 15.4 us  [the longest x3 10.4 us: finish_solve(): got_a = lax.ppermute(sent, 'dom', flip(doms, 1))]
    ppermute x14, starting transfers between devices: 16.4 us -> 19.3 us  [sum_over(): lax.ppermute(value, axes, flip(total, m))]
    ppermute x14, waiting for transfers between devices: 13.5 us -> 16.1 us  [sum_over(): lax.ppermute(value, axes, flip(total, m))]
    unnamed x20 -> x22, local copies, waits for them, and re-layouts: 2.49 us -> 0.67 us
    pallas_call x1, Pallas kernels: 1.85 us -> 3.4 us  [tile_layouts(): pl.pallas_call(tiles_kernel, out_shape=jax.ShapeDtypeStruct((elements * s...]
  transfers between devices with their start and end apart: 28 -> 28, of which waited for: 20 -> 18; matrix products, arithmetic and copies ran while one was open for 0% -> 0% of each run, Pallas kernels for 7% -> 7%
where the time goes in v2:
time: 97.2 us; the launch traced here: 97 us
  starting transfers between devices  34.8 us (36%)
  waiting for transfers between devices  31.6 us (33%)
  Pallas kernels  28.8 us (30%)
    ppermute x14, starting transfers between devices, sum_over(): lax.ppermute(value, axes, flip(total, m))  19.3 us
    ppermute x14, waiting for transfers between devices, sum_over(): lax.ppermute(value, axes, flip(total, m))  16.1 us
    ppermute x3, starting transfers between devices, finish_solve(): got_a = lax.ppermute(sent, 'dom', flip(doms, 1))  10.4 us
    ppermute x3, waiting for transfers between devices, finish_solve(): pair_far = lax.ppermute(pair_own, 'line', flip(lines, 2))  9.43 us
    pallas_call x1, Pallas kernels, chain_products(): pl.pallas_call(functools.partial(chain_kernel, width, size), out_shape=(s...  7.57 us
    pallas_call x2, Pallas kernels, advance(): pl.pallas_call(functools.partial(advance_kernel, width, rounded), out_sha...  6.29 us
    pallas_call x1, Pallas kernels, tile_layouts(): pl.pallas_call(tiles_kernel, out_shape=jax.ShapeDtypeStruct((elements * s...  3.4 us
    ppermute x3, waiting for transfers between devices, finish_solve(): ends_other = lax.ppermute(ends_own, 'line', flip(lines, 1))  3.33 us
  transfers between devices with their start and end apart: 28, of which 18 were waited for; matrix products, arithmetic and copies ran while one was open for 0% of the time, Pallas kernels for 7%

profile of v2, /device:TPU:0, one launch (start us, length us, event | category | flops | bytes accessed | tf_op | source)
XLA Modules:
  0.0 97.0 jit_solution(10893447602458214557)
XLA Ops:
  0.6 3.4 %tile_layouts.3.tiles = f32[8192,128]{1,0:T(8,128)S(1)} custom-call(bf16[64,64,128]{2,1,0:T(8,128)(2,1)} %fwd.1, bf16[64,64,128]{2,1,0:T(8,128)(2,1)} %bwd.1), custom_call_target="tpu_custom_call" | custom-call | flops 4000000 | bytes 10485760 | tf_op jit(solution)/shard_map/tile_layouts/pallas_call | solution.py:141
  4.0 7.6 %chain_products.3 = (bf16[8,8,64,128]{3,2,1,0:T(8,128)(2,1)S(1)}, bf16[8,8,64,128]{3,2,1,0:T(8,128)(2,1)S(1)}, f32[64,128,128]{2,1,0:T(8,128)S(1)}, f32[32,64,128]{2,1,0:T(8,128)S(1)}) custom-call(f32[8192,128]{1,0:T(8,128)S(1)} %tile_layouts.3.tiles), custom_call_target="tpu_custom_call" | custom-call | flops 40000000 | bytes 12582912 | tf_op jit(solution)/shard_map/chain_products/pallas_call | solution.py:254
  12.2 2.6 %collective-permute-start.66 = (f32[8,128]{1,0:T(8,128)S(1)}, f32[8,128]{1,0:T(8,128)S(1)}, u32[]{:S(2)}, u32[]{:S(2)}) collective-permute-start(f32[8,128]{1,0:T(8,128)S(1)} %sum_squares.3), channel_id=1, source_target_pairs={{0,2},{1,3},{2,0},{3,1},{4,6},{5,7},{6,4},{7,5},{8,10},{9,11},{10,... | collective-permute-start | bytes 12296 | tf_op jit(solution)/shard_map/ppermute | solution.py:706
  14.8 1.5 %collective-permute-start.67 = (f32[8,128]{1,0:T(8,128)S(1)}, f32[8,128]{1,0:T(8,128)S(1)}, u32[]{:S(2)}, u32[]{:S(2)}) collective-permute-start(f32[8,128]{1,0:T(8,128)S(1)} %sum_squares.3), channel_id=1, source_target_pairs={{0,4},{1,5},{2,6},{3,7},{4,0},{5,1},{6,2},{7,3},{8,12},{9,13},{10,... | collective-permute-start | bytes 12296 | tf_op jit(solution)/shard_map/ppermute | solution.py:706
  16.4 2.0 %collective-permute-done.67 = f32[8,128]{1,0:T(8,128)S(1)} collective-permute-done((f32[8,128]{1,0:T(8,128)S(1)}, f32[8,128]{1,0:T(8,128)S(1)}, u32[]{:S(2)}, u32[]{:S(2)}) %collective-permute-start.67) | collective-permute-done | bytes 4128 | tf_op jit(solution)/shard_map/ppermute | solution.py:706
  18.4 2.4 %collective-permute-done.68 = f32[8,128]{1,0:T(8,128)S(1)} collective-permute-done((f32[8,128]{1,0:T(8,128)S(1)}, f32[8,128]{1,0:T(8,128)S(1)}, u32[]{:S(2)}, u32[]{:S(2)}) %collective-permute-start.68) | collective-permute-done | bytes 4128 | tf_op jit(solution)/shard_map/ppermute | solution.py:706
  20.8 1.6 %collective-permute-start.69 = (f32[8,128]{1,0:T(8,128)S(1)}, f32[8,128]{1,0:T(8,128)S(1)}, u32[]{:S(2)}, u32[]{:S(2)}) collective-permute-start(f32[8,128]{1,0:T(8,128)S(1)} %add_add_fusion.5), channel_id=1, source_target_pairs={{0,8},{1,9},{2,10},{3,11},{4,12},{5,13},{6,14},{7,15},{8,0},{9,1},... | collective-permute-start | bytes 12296 | tf_op jit(solution)/shard_map/ppermute | solution.py:706
  22.4 2.6 %collective-permute-start.70 = (f32[8,128]{1,0:T(8,128)S(1)}, f32[8,128]{1,0:T(8,128)S(1)}, u32[]{:S(2)}, u32[]{:S(2)}) collective-permute-start(f32[8,128]{1,0:T(8,128)S(1)} %add_add_fusion.5), channel_id=1, source_target_pairs={{0,16},{1,17},{2,18},{3,19},{4,20},{5,21},{6,22},{7,23},{8,24},{9,... | collective-permute-start | bytes 12296 | tf_op jit(solution)/shard_map/ppermute | solution.py:706
  25.2 1.7 %line_maps.3 = (f32[8,64,128]{2,1,0:T(8,128)S(1)}, f32[8,64,128]{2,1,0:T(8,128)S(1)}, f32[8,64,128]{2,1,0:T(8,128)S(1)}, f32[8,64,128]{2,1,0:T(8,128)S(1)}, f32[...) custom-call(f32[32,64,128]{2,1,0:T(8,128)S(1)} %get-tuple-element.103.own, ...), custom_call_target="tpu_custom_call" | custom-call | tf_op jit(solution)/shard_map/line_maps/pallas_call | solution.py:331
  27.5 2.9 %collective-permute-done.71 = f32[8,128]{1,0:T(8,128)S(1)} collective-permute-done((f32[8,128]{1,0:T(8,128)S(1)}, f32[8,128]{1,0:T(8,128)S(1)}, u32[]{:S(2)}, u32[]{:S(2)}) %collective-permute-start.71) | collective-permute-done | bytes 4128 | tf_op jit(solution)/shard_map/ppermute | solution.py:706
  30.4 1.2 %collective-permute-done.72 = f32[8,128]{1,0:T(8,128)S(1)} collective-permute-done((f32[8,128]{1,0:T(8,128)S(1)}, f32[8,128]{1,0:T(8,128)S(1)}, u32[]{:S(2)}, u32[]{:S(2)}) %collective-permute-start.72) | collective-permute-done | bytes 4128 | tf_op jit(solution)/shard_map/ppermute | solution.py:706
  31.6 2.0 %line_sweep.7 = (f32[64,128]{1,0:T(8,128)S(1)}, f32[16,128]{1,0:T(8,128)S(1)}, f32[64,128]{1,0:T(8,128)S(1)}) custom-call(f32[64,128]{1,0:T(8,128)S(1)} %copy-done.7, f32[8,128]{1,0:T(8,128)S(1)} %add_sqrt_fusion.4.norm, bf16[64,64,128]{2,1,0:T(8,128)(2,1)S(1)} %copy-done.1, bf16[8,8,64,128]{3,2,1,0:T(8,128)(2,1)S(1)} %get-tuple-element.100.fwd_steps, ...), custom_call_target="tpu_custom_call" | custom-call | tf_op jit(solution)/shard_map/line_sweep/pallas_call | solution.py:376
  33.9 1.0 %collective-permute-done.73.other = f32[16,128]{1,0:T(8,128)S(1)} collective-permute-done((f32[16,128]{1,0:T(8,128)S(1)}, f32[16,128]{1,0:T(8,128)S(1)}, u32[]{:S(2)}, u32[]{:S(2)}) %collective-permute-start.73) | collective-permute-done | bytes 8224 | tf_op jit(solution)/shard_map/ppermute | solution.py:738
  35.7 3.1 %collective-permute-done.75.far = f32[16,128]{1,0:T(8,128)S(1)} collective-permute-done((f32[16,128]{1,0:T(8,128)S(1)}, f32[16,128]{1,0:T(8,128)S(1)}, u32[]{:S(2)}, u32[]{:S(2)}) %collective-permute-start.75) | collective-permute-done | bytes 8224 | tf_op jit(solution)/shard_map/ppermute | solution.py:740
  41.8 1.9 %collective-permute-done.77.got_a = f32[64,32]{1,0:T(8,128)S(1)} collective-permute-done((f32[64,32]{1,0:T(8,128)S(1)}, f32[64,32]{1,0:T(8,128)S(1)}, u32[]{:S(2)}, u32[]{:S(2)}) %collective-permute-start.77) | collective-permute-done | bytes 8224 | tf_op jit(solution)/shard_map/ppermute | solution.py:744
  43.7 3.1 %faces_and_sweep.8 = (f32[64,128]{1,0:T(8,128)S(1)}, f32[16,128]{1,0:T(8,128)S(1)}, f32[64,128]{1,0:T(8,128)S(1)}) custom-call(f32[64,128]{1,0:T(8,128)S(1)} %get-tuple-element.113.vector.rest_0_, f32[64,32]{1,0:T(8,128)S(1)} %collective-permute-done.77.got_a, f32[64,32]{1,0:T(8,128)S(1)} %collective-permute-done.78.got_b, s32[4,128]{1,0:T(4,128)S(1)} %copy-done.8, ...), custom_call_target="tpu_custom_call" | custom-call | tf_op jit(solution)/shard_map/faces_and_sweep/pallas_call | solution.py:557
  46.9 1.2 %collective-permute-done.79.other = f32[16,128]{1,0:T(8,128)S(1)} collective-permute-done((f32[16,128]{1,0:T(8,128)S(1)}, f32[16,128]{1,0:T(8,128)S(1)}, u32[]{:S(2)}, u32[]{:S(2)}) %collective-permute-start.79) | collective-permute-done | bytes 8224 | tf_op jit(solution)/shard_map/ppermute | solution.py:738
  48.9 3.1 %collective-permute-done.80.far = f32[16,128]{1,0:T(8,128)S(1)} collective-permute-done((f32[16,128]{1,0:T(8,128)S(1)}, f32[16,128]{1,0:T(8,128)S(1)}, u32[]{:S(2)}, u32[]{:S(2)}) %collective-permute-start.80) | collective-permute-done | bytes 8224 | tf_op jit(solution)/shard_map/ppermute | solution.py:740
  52.9 4.9 %collective-permute-start.81 = (f32[64,32]{1,0:T(8,128)S(1)}, f32[64,32]{1,0:T(8,128)S(1)}, u32[]{:S(2)}, u32[]{:S(2)}) collective-permute-start(f32[64,32]{1,0:T(8,128)S(1)} %get-tuple-element.119), channel_id=1, source_target_pairs={{0,4},{4,0},{8,12},{12,8},{16,20},{20,16},{24,28},{28,24},{1,5},{5... | collective-permute-start | bytes 24584 | tf_op jit(solution)/shard_map/ppermute | solution.py:744
  59.7 3.2 %faces_and_sweep.9 = (f32[64,128]{1,0:T(8,128)S(1)}, f32[16,128]{1,0:T(8,128)S(1)}, f32[64,128]{1,0:T(8,128)S(1)}) custom-call(f32[64,128]{1,0:T(8,128)S(1)} %get-tuple-element.118.vector.rest_1_, f32[64,32]{1,0:T(8,128)S(1)} %collective-permute-done.81.got_a, f32[64,32]{1,0:T(8,128)S(1)} %collective-permute-done.82.got_b, s32[4,128]{1,0:T(4,128)S(1)} %copy-done.8, ...), custom_call_target="tpu_custom_call" | custom-call | tf_op jit(solution)/shard_map/faces_and_sweep/pallas_call | solution.py:557
  62.9 1.2 %collective-permute-done.83.other = f32[16,128]{1,0:T(8,128)S(1)} collective-permute-done((f32[16,128]{1,0:T(8,128)S(1)}, f32[16,128]{1,0:T(8,128)S(1)}, u32[]{:S(2)}, u32[]{:S(2)}) %collective-permute-start.83) | collective-permute-done | bytes 8224 | tf_op jit(solution)/shard_map/ppermute | solution.py:738
  64.8 3.1 %collective-permute-done.84.far = f32[16,128]{1,0:T(8,128)S(1)} collective-permute-done((f32[16,128]{1,0:T(8,128)S(1)}, f32[16,128]{1,0:T(8,128)S(1)}, u32[]{:S(2)}, u32[]{:S(2)}) %collective-permute-start.84) | collective-permute-done | bytes 8224 | tf_op jit(solution)/shard_map/ppermute | solution.py:740
  68.9 4.9 %collective-permute-start.85 = (f32[64,32]{1,0:T(8,128)S(1)}, f32[64,32]{1,0:T(8,128)S(1)}, u32[]{:S(2)}, u32[]{:S(2)}) collective-permute-start(f32[64,32]{1,0:T(8,128)S(1)} %get-tuple-element.124), channel_id=1, source_target_pairs={{0,4},{4,0},{8,12},{12,8},{16,20},{20,16},{24,28},{28,24},{1,5},{5... | collective-permute-start | bytes 24584 | tf_op jit(solution)/shard_map/ppermute | solution.py:744
  75.7 1.2 %faces_and_sums.1 = f32[16,128]{1,0:T(8,128)S(1)} custom-call(f32[64,128]{1,0:T(8,128)S(1)} %get-tuple-element.123.vector.rest_2_, f32[64,32]{1,0:T(8,128)S(1)} %collective-permute-done.85.got_a, f32[64,32]{1,0:T(8,128)S(1)} %collective-permute-done.86.got_b, s32[4,128]{1,0:T(4,128)S(1)} %copy-done.8, f32[64,128]{1,0:T(8,128)S(1)} %near_faces.11.partial, ...), custom_call_target="tpu_custom_call" | custom-call | tf_op jit(solution)/shard_map/faces_and_sums/pallas_call | solution.py:590
  77.4 5.0 %collective-permute-start.88 = (f32[16,128]{1,0:T(8,128)S(1)}, f32[16,128]{1,0:T(8,128)S(1)}, u32[]{:S(2)}, u32[]{:S(2)}) collective-permute-start(f32[16,128]{1,0:T(8,128)S(1)} %faces_and_sums.1), channel_id=1, source_target_pairs={{0,4},{1,5},{2,6},{3,7},{4,0},{5,1},{6,2},{7,3},{8,12},{9,13},{10,... | collective-permute-start | bytes 24584 | tf_op jit(solution)/shard_map/ppermute | solution.py:706
  82.4 1.0 collective-permute-start.89
  84.0 2.9 %collective-permute-done.89 = f32[16,128]{1,0:T(8,128)S(1)} collective-permute-done((f32[16,128]{1,0:T(8,128)S(1)}, f32[16,128]{1,0:T(8,128)S(1)}, u32[]{:S(2)}, u32[]{:S(2)}) %collective-permute-start.89) | collective-permute-done | bytes 8224 | tf_op jit(solution)/shard_map/ppermute | solution.py:706
  87.8 0.9 collective-permute-start.91
  88.8 2.6 %collective-permute-start.92 = (f32[16,128]{1,0:T(8,128)S(1)}, f32[16,128]{1,0:T(8,128)S(1)}, u32[]{:S(2)}, u32[]{:S(2)}) collective-permute-start(f32[16,128]{1,0:T(8,128)S(1)} %add_add_fusion.3), channel_id=1, source_target_pairs={{0,24},{1,25},{2,26},{3,27},{4,28},{5,29},{6,30},{7,31},{8,16},{9,... | collective-permute-start | bytes 24584 | tf_op jit(solution)/shard_map/ppermute | solution.py:706
  91.3 1.0 %collective-permute-done.91 = f32[16,128]{1,0:T(8,128)S(1)} collective-permute-done((f32[16,128]{1,0:T(8,128)S(1)}, f32[16,128]{1,0:T(8,128)S(1)}, u32[]{:S(2)}, u32[]{:S(2)}) %collective-permute-start.91) | collective-permute-done | bytes 8224 | tf_op jit(solution)/shard_map/ppermute | solution.py:706
  92.4 1.8 %collective-permute-done.92 = f32[16,128]{1,0:T(8,128)S(1)} collective-permute-done((f32[16,128]{1,0:T(8,128)S(1)}, f32[16,128]{1,0:T(8,128)S(1)}, u32[]{:S(2)}, u32[]{:S(2)}) %collective-permute-start.92) | collective-permute-done | bytes 8224 | tf_op jit(solution)/shard_map/ppermute | solution.py:706
  94.2 1.2 %collective-permute-done.93 = f32[16,128]{1,0:T(8,128)S(1)} collective-permute-done((f32[16,128]{1,0:T(8,128)S(1)}, f32[16,128]{1,0:T(8,128)S(1)}, u32[]{:S(2)}, u32[]{:S(2)}) %collective-permute-start.93) | collective-permute-done | bytes 8224 | tf_op jit(solution)/shard_map/ppermute | solution.py:706
  (71 shorter events, 16.3 us)
Async XLA Ops:
  11.6 19.9 %copy-start.1 = (bf16[64,64,128]{2,1,0:T(8,128)(2,1)S(1)}, bf16[64,64,128]{2,1,0:T(8,128)(2,1)}, u32[]{:S(2)}) copy-start(bf16[64,64,128]{2,1,0:T(8,128)(2,1)} %inv.5) | copy-start | bytes 3145732
  11.6 13.6 %collective-permute-start.74 = (f32[32,64,128]{2,1,0:T(8,128)S(1)}, f32[32,64,128]{2,1,0:T(8,128)S(1)}, u32[]{:S(2)}, u32[]{:S(2)}) collective-permute-start(f32[32,64,128]{2,1,0:T(8,128)S(1)} %get-tuple-element.103.own), channel_id=1, source_target_pairs={{0,1},{1,0},{2,3},{3,2},{4,5},{5,4},{6,7},{7,6},{8,9},{9,8},{10,11... | collective-permute-start | bytes 3145736 | tf_op jit(solution)/shard_map/ppermute | solution.py:724
  12.2 26.6 %copy-start.9 = (s32[2,16]{1,0:T(2,128)S(1)}, s32[2,16]{1,0:T(2,128)}, u32[]{:S(2)}) copy-start(s32[2,16]{1,0:T(2,128)} %send_list.5) | copy-start | bytes 388
  12.2 4.2 %collective-permute-start.66 = (f32[8,128]{1,0:T(8,128)S(1)}, f32[8,128]{1,0:T(8,128)S(1)}, u32[]{:S(2)}, u32[]{:S(2)}) collective-permute-start(f32[8,128]{1,0:T(8,128)S(1)} %sum_squares.3), channel_id=1, source_target_pairs={{0,2},{1,3},{2,0},{3,1},{4,6},{5,7},{6,4},{7,5},{8,10},{9,11},{10,... | collective-permute-start | bytes 12296 | tf_op jit(solution)/shard_map/ppermute | solution.py:706
  14.8 3.6 %collective-permute-start.67 = (f32[8,128]{1,0:T(8,128)S(1)}, f32[8,128]{1,0:T(8,128)S(1)}, u32[]{:S(2)}, u32[]{:S(2)}) collective-permute-start(f32[8,128]{1,0:T(8,128)S(1)} %sum_squares.3), channel_id=1, source_target_pairs={{0,4},{1,5},{2,6},{3,7},{4,0},{5,1},{6,2},{7,3},{8,12},{9,13},{10,... | collective-permute-start | bytes 12296 | tf_op jit(solution)/shard_map/ppermute | solution.py:706
  16.3 4.5 %collective-permute-start.68 = (f32[8,128]{1,0:T(8,128)S(1)}, f32[8,128]{1,0:T(8,128)S(1)}, u32[]{:S(2)}, u32[]{:S(2)}) collective-permute-start(f32[8,128]{1,0:T(8,128)S(1)} %sum_squares.3), channel_id=1, source_target_pairs={{0,6},{1,7},{2,4},{3,5},{4,2},{5,3},{6,0},{7,1},{8,14},{9,15},{10,... | collective-permute-start | bytes 12296 | tf_op jit(solution)/shard_map/ppermute | solution.py:706
  20.8 6.7 %collective-permute-start.69 = (f32[8,128]{1,0:T(8,128)S(1)}, f32[8,128]{1,0:T(8,128)S(1)}, u32[]{:S(2)}, u32[]{:S(2)}) collective-permute-start(f32[8,128]{1,0:T(8,128)S(1)} %add_add_fusion.5), channel_id=1, source_target_pairs={{0,8},{1,9},{2,10},{3,11},{4,12},{5,13},{6,14},{7,15},{8,0},{9,1},... | collective-permute-start | bytes 12296 | tf_op jit(solution)/shard_map/ppermute | solution.py:706
  22.4 5.1 %collective-permute-start.70 = (f32[8,128]{1,0:T(8,128)S(1)}, f32[8,128]{1,0:T(8,128)S(1)}, u32[]{:S(2)}, u32[]{:S(2)}) collective-permute-start(f32[8,128]{1,0:T(8,128)S(1)} %add_add_fusion.5), channel_id=1, source_target_pairs={{0,16},{1,17},{2,18},{3,19},{4,20},{5,21},{6,22},{7,23},{8,24},{9,... | collective-permute-start | bytes 12296 | tf_op jit(solution)/shard_map/ppermute | solution.py:706
  25.0 5.4 %collective-permute-start.71 = (f32[8,128]{1,0:T(8,128)S(1)}, f32[8,128]{1,0:T(8,128)S(1)}, u32[]{:S(2)}, u32[]{:S(2)}) collective-permute-start(f32[8,128]{1,0:T(8,128)S(1)} %add_add_fusion.5), channel_id=1, source_target_pairs={{0,24},{1,25},{2,26},{3,27},{4,28},{5,29},{6,30},{7,31},{8,16},{9,... | collective-permute-start | bytes 12296 | tf_op jit(solution)/shard_map/ppermute | solution.py:706
  26.9 11.9 %collective-permute-start.76 = (bf16[24,64,128]{2,1,0:T(8,128)(2,1)S(1)}, bf16[24,64,128]{2,1,0:T(8,128)(2,1)S(1)}, u32[]{:S(2)}, u32[]{:S(2)}) collective-permute-start(bf16[24,64,128]{2,1,0:T(8,128)(2,1)S(1)} %get-tuple-element.111), channel_id=1, source_target_pairs={{0,2},{1,3},{2,0},{3,1},{4,6},{5,7},{6,4},{7,5},{8,10},{9,11},{10,... | collective-permute-start | bytes 1179656 | tf_op jit(solution)/shard_map/ppermute | solution.py:729
  30.4 1.2 %collective-permute-start.72 = (f32[8,128]{1,0:T(8,128)S(1)}, f32[8,128]{1,0:T(8,128)S(1)}, u32[]{:S(2)}, u32[]{:S(2)}) collective-permute-start(f32[8,128]{1,0:T(8,128)S(1)} %add_add_fusion.4), channel_id=1, source_target_pairs={{0,1},{1,0},{2,3},{3,2},{4,5},{5,4},{6,7},{7,6},{8,9},{9,8},{10,11... | collective-permute-start | bytes 12296 | tf_op jit(solution)/shard_map/ppermute | solution.py:706
  33.6 1.2 %collective-permute-start.73 = (f32[16,128]{1,0:T(8,128)S(1)}, f32[16,128]{1,0:T(8,128)S(1)}, u32[]{:S(2)}, u32[]{:S(2)}) collective-permute-start(f32[16,128]{1,0:T(8,128)S(1)} %get-tuple-element.102.own), channel_id=1, source_target_pairs={{0,1},{1,0},{2,3},{3,2},{4,5},{5,4},{6,7},{7,6},{8,9},{9,8},{10,11... | collective-permute-start | bytes 24584 | tf_op jit(solution)/shard_map/ppermute | solution.py:738
  35.1 3.7 %collective-permute-start.75 = (f32[16,128]{1,0:T(8,128)S(1)}, f32[16,128]{1,0:T(8,128)S(1)}, u32[]{:S(2)}, u32[]{:S(2)}) collective-permute-start(f32[16,128]{1,0:T(8,128)S(1)} %line_pair.9.pair), channel_id=1, source_target_pairs={{0,2},{1,3},{2,0},{3,1},{4,6},{5,7},{6,4},{7,5},{8,10},{9,11},{10,... | collective-permute-start | bytes 24584 | tf_op jit(solution)/shard_map/ppermute | solution.py:740
  39.7 4.0 %collective-permute-start.77 = (f32[64,32]{1,0:T(8,128)S(1)}, f32[64,32]{1,0:T(8,128)S(1)}, u32[]{:S(2)}, u32[]{:S(2)}) collective-permute-start(f32[64,32]{1,0:T(8,128)S(1)} %get-tuple-element.114), channel_id=1, source_target_pairs={{0,4},{4,0},{8,12},{12,8},{16,20},{20,16},{24,28},{28,24},{1,5},{5... | collective-permute-start | bytes 24584 | tf_op jit(solution)/shard_map/ppermute | solution.py:744
  40.3 3.4 %collective-permute-start.78 = (f32[64,32]{1,0:T(8,128)S(1)}, f32[64,32]{1,0:T(8,128)S(1)}, u32[]{:S(2)}, u32[]{:S(2)}) collective-permute-start(f32[64,32]{1,0:T(8,128)S(1)} %get-tuple-element.114), channel_id=1, source_target_pairs={{0,0},{4,8},{8,4},{12,16},{16,12},{20,24},{24,20},{28,28},{1,1},{5... | collective-permute-start | bytes 24584 | tf_op jit(solution)/shard_map/ppermute | solution.py:745
  46.8 1.2 %collective-permute-start.79 = (f32[16,128]{1,0:T(8,128)S(1)}, f32[16,128]{1,0:T(8,128)S(1)}, u32[]{:S(2)}, u32[]{:S(2)}) collective-permute-start(f32[16,128]{1,0:T(8,128)S(1)} %get-tuple-element.116.own), channel_id=1, source_target_pairs={{0,1},{1,0},{2,3},{3,2},{4,5},{5,4},{6,7},{7,6},{8,9},{9,8},{10,11... | collective-permute-start | bytes 24584 | tf_op jit(solution)/shard_map/ppermute | solution.py:738
  48.3 3.7 %collective-permute-start.80 = (f32[16,128]{1,0:T(8,128)S(1)}, f32[16,128]{1,0:T(8,128)S(1)}, u32[]{:S(2)}, u32[]{:S(2)}) collective-permute-start(f32[16,128]{1,0:T(8,128)S(1)} %line_pair.10.pair), channel_id=1, source_target_pairs={{0,2},{1,3},{2,0},{3,1},{4,6},{5,7},{6,4},{7,5},{8,10},{9,11},{10,... | collective-permute-start | bytes 24584 | tf_op jit(solution)/shard_map/ppermute | solution.py:740
  52.9 6.8 %collective-permute-start.81 = (f32[64,32]{1,0:T(8,128)S(1)}, f32[64,32]{1,0:T(8,128)S(1)}, u32[]{:S(2)}, u32[]{:S(2)}) collective-permute-start(f32[64,32]{1,0:T(8,128)S(1)} %get-tuple-element.119), channel_id=1, source_target_pairs={{0,4},{4,0},{8,12},{12,8},{16,20},{20,16},{24,28},{28,24},{1,5},{5... | collective-permute-start | bytes 24584 | tf_op jit(solution)/shard_map/ppermute | solution.py:744
  57.8 1.9 %collective-permute-start.82 = (f32[64,32]{1,0:T(8,128)S(1)}, f32[64,32]{1,0:T(8,128)S(1)}, u32[]{:S(2)}, u32[]{:S(2)}) collective-permute-start(f32[64,32]{1,0:T(8,128)S(1)} %get-tuple-element.119), channel_id=1, source_target_pairs={{0,0},{4,8},{8,4},{12,16},{16,12},{20,24},{24,20},{28,28},{1,1},{5... | collective-permute-start | bytes 24584 | tf_op jit(solution)/shard_map/ppermute | solution.py:745
  62.8 1.2 %collective-permute-start.83 = (f32[16,128]{1,0:T(8,128)S(1)}, f32[16,128]{1,0:T(8,128)S(1)}, u32[]{:S(2)}, u32[]{:S(2)}) collective-permute-start(f32[16,128]{1,0:T(8,128)S(1)} %get-tuple-element.121.own), channel_id=1, source_target_pairs={{0,1},{1,0},{2,3},{3,2},{4,5},{5,4},{6,7},{7,6},{8,9},{9,8},{10,11... | collective-permute-start | bytes 24584 | tf_op jit(solution)/shard_map/ppermute | solution.py:738
  64.3 3.7 %collective-permute-start.84 = (f32[16,128]{1,0:T(8,128)S(1)}, f32[16,128]{1,0:T(8,128)S(1)}, u32[]{:S(2)}, u32[]{:S(2)}) collective-permute-start(f32[16,128]{1,0:T(8,128)S(1)} %line_pair.11.pair), channel_id=1, source_target_pairs={{0,2},{1,3},{2,0},{3,1},{4,6},{5,7},{6,4},{7,5},{8,10},{9,11},{10,... | collective-permute-start | bytes 24584 | tf_op jit(solution)/shard_map/ppermute | solution.py:740
  68.9 27.2 %copy-start.5 = (bf16[64,64,128]{2,1,0:T(8,128)(2,1)S(1)}, bf16[64,64,128]{2,1,0:T(8,128)(2,1)}, u32[]{:S(2)}) copy-start(bf16[64,64,128]{2,1,0:T(8,128)(2,1)} %fwd.1) | copy-start | bytes 3145732
  68.9 27.2 %copy-start.6 = (bf16[64,64,128]{2,1,0:T(8,128)(2,1)S(1)}, bf16[64,64,128]{2,1,0:T(8,128)(2,1)}, u32[]{:S(2)}) copy-start(bf16[64,64,128]{2,1,0:T(8,128)(2,1)} %bwd.1) | copy-start | bytes 3145732
  68.9 6.8 %collective-permute-start.85 = (f32[64,32]{1,0:T(8,128)S(1)}, f32[64,32]{1,0:T(8,128)S(1)}, u32[]{:S(2)}, u32[]{:S(2)}) collective-permute-start(f32[64,32]{1,0:T(8,128)S(1)} %get-tuple-element.124), channel_id=1, source_target_pairs={{0,4},{4,0},{8,12},{12,8},{16,20},{20,16},{24,28},{28,24},{1,5},{5... | collective-permute-start | bytes 24584 | tf_op jit(solution)/shard_map/ppermute | solution.py:744
  73.8 1.9 %collective-permute-start.86 = (f32[64,32]{1,0:T(8,128)S(1)}, f32[64,32]{1,0:T(8,128)S(1)}, u32[]{:S(2)}, u32[]{:S(2)}) collective-permute-start(f32[64,32]{1,0:T(8,128)S(1)} %get-tuple-element.124), channel_id=1, source_target_pairs={{0,0},{4,8},{8,4},{12,16},{16,12},{20,24},{24,20},{28,28},{1,1},{5... | collective-permute-start | bytes 24584 | tf_op jit(solution)/shard_map/ppermute | solution.py:745
  76.9 6.4 %collective-permute-start.87 = (f32[16,128]{1,0:T(8,128)S(1)}, f32[16,128]{1,0:T(8,128)S(1)}, u32[]{:S(2)}, u32[]{:S(2)}) collective-permute-start(f32[16,128]{1,0:T(8,128)S(1)} %faces_and_sums.1), channel_id=1, source_target_pairs={{0,2},{1,3},{2,0},{3,1},{4,6},{5,7},{6,4},{7,5},{8,10},{9,11},{10,... | collective-permute-start | bytes 24584 | tf_op jit(solution)/shard_map/ppermute | solution.py:706
  77.4 6.6 %collective-permute-start.88 = (f32[16,128]{1,0:T(8,128)S(1)}, f32[16,128]{1,0:T(8,128)S(1)}, u32[]{:S(2)}, u32[]{:S(2)}) collective-permute-start(f32[16,128]{1,0:T(8,128)S(1)} %faces_and_sums.1), channel_id=1, source_target_pairs={{0,4},{1,5},{2,6},{3,7},{4,0},{5,1},{6,2},{7,3},{8,12},{9,13},{10,... | collective-permute-start | bytes 24584 | tf_op jit(solution)/shard_map/ppermute | solution.py:706
  82.4 4.5 %collective-permute-start.89 = (f32[16,128]{1,0:T(8,128)S(1)}, f32[16,128]{1,0:T(8,128)S(1)}, u32[]{:S(2)}, u32[]{:S(2)}) collective-permute-start(f32[16,128]{1,0:T(8,128)S(1)} %faces_and_sums.1), channel_id=1, source_target_pairs={{0,6},{1,7},{2,4},{3,5},{4,2},{5,3},{6,0},{7,1},{8,14},{9,15},{10,... | collective-permute-start | bytes 24584 | tf_op jit(solution)/shard_map/ppermute | solution.py:706
  86.9 4.4 %collective-permute-start.90 = (f32[16,128]{1,0:T(8,128)S(1)}, f32[16,128]{1,0:T(8,128)S(1)}, u32[]{:S(2)}, u32[]{:S(2)}) collective-permute-start(f32[16,128]{1,0:T(8,128)S(1)} %add_add_fusion.3), channel_id=1, source_target_pairs={{0,8},{1,9},{2,10},{3,11},{4,12},{5,13},{6,14},{7,15},{8,0},{9,1},... | collective-permute-start | bytes 24584 | tf_op jit(solution)/shard_map/ppermute | solution.py:706
  87.8 4.5 %collective-permute-start.91 = (f32[16,128]{1,0:T(8,128)S(1)}, f32[16,128]{1,0:T(8,128)S(1)}, u32[]{:S(2)}, u32[]{:S(2)}) collective-permute-start(f32[16,128]{1,0:T(8,128)S(1)} %add_add_fusion.3), channel_id=1, source_target_pairs={{0,16},{1,17},{2,18},{3,19},{4,20},{5,21},{6,22},{7,23},{8,24},{9,... | collective-permute-start | bytes 24584 | tf_op jit(solution)/shard_map/ppermute | solution.py:706
  88.8 5.4 %collective-permute-start.92 = (f32[16,128]{1,0:T(8,128)S(1)}, f32[16,128]{1,0:T(8,128)S(1)}, u32[]{:S(2)}, u32[]{:S(2)}) collective-permute-start(f32[16,128]{1,0:T(8,128)S(1)} %add_add_fusion.3), channel_id=1, source_target_pairs={{0,24},{1,25},{2,26},{3,27},{4,28},{5,29},{6,30},{7,31},{8,16},{9,... | collective-permute-start | bytes 24584 | tf_op jit(solution)/shard_map/ppermute | solution.py:706
  94.2 1.2 %collective-permute-start.93 = (f32[16,128]{1,0:T(8,128)S(1)}, f32[16,128]{1,0:T(8,128)S(1)}, u32[]{:S(2)}, u32[]{:S(2)}) collective-permute-start(f32[16,128]{1,0:T(8,128)S(1)} %add_add_fusion.2), channel_id=1, source_target_pairs={{0,1},{1,0},{2,3},{3,2},{4,5},{5,4},{6,7},{7,6},{8,9},{9,8},{10,11... | collective-permute-start | bytes 24584 | tf_op jit(solution)/shard_map/ppermute | solution.py:706
  (7 other events, 50.1 us)

commit v3 on v2

--- a/solution.py
+++ b/solution.py
@@ -163,7 +163,7 @@
     )(vector)
 
 
-def chain_kernel(width, size, tiles, fwd_steps, bwd_steps, response, ends, chain):
+def chain_kernel(width, size, tiles, fwd_steps, bwd_steps, chain, ends):
     elements = tiles.shape[0] // size
     positions = elements // width
     half = lanes_of((size, elements)) < size
@@ -234,6 +234,10 @@
         ends[paired + line] = chain[pl.ds(line * size, size), :]
     ends[paired + width :] = bwd_steps[last].astype(F32)
 
+
+def response_kernel(chain, response):
+    size, _, elements = response.shape
+
     @pl.loop(0, size // SUB)
     def _(n):
         groups = []
@@ -247,6 +251,17 @@
             response[n * SUB + il] = jnp.concatenate([rows[il] for rows in groups], axis=0).T
 
 
+def response_layout(chain, size):
+    elements = chain.shape[0] // size
+    return pl.pallas_call(
+        response_kernel,
+        out_shape=jax.ShapeDtypeStruct((size, 2 * size, elements), F32),
+        name="response_layout",
+        compiler_params=pltpu.CompilerParams(vmem_limit_bytes=12 * MIB),
+        cost_estimate=pl.CostEstimate(flops=4000000, bytes_accessed=8 * MIB, transcendentals=0),
+    )(chain)
+
+
 def chain_products(tiles, width):
     elements = tiles.shape[1]
     size = tiles.shape[0] // elements
@@ -256,10 +271,9 @@
         out_shape=(
             steps,
             steps,
-            jax.ShapeDtypeStruct((size, 2 * size, elements), F32),
+            jax.ShapeDtypeStruct((elements * size, 2 * size), F32),
             jax.ShapeDtypeStruct((width + width // 2 + SUB, size, elements), F32),
         ),
-        scratch_shapes=[pltpu.VMEM((elements * size, elements), F32)],
         name="chain_products",
         compiler_params=pltpu.CompilerParams(vmem_limit_bytes=16 * MIB),
         cost_estimate=pl.CostEstimate(flops=40000000, bytes_accessed=12 * MIB, transcendentals=0),
@@ -719,7 +733,7 @@
     bits = index_bits(doms * lines)
     squares = sum_over(sum_squares(right_side), [bits[1:3]])
     tiles = tile_layouts(fwd_blocks, bwd_blocks)
-    fwd_steps, bwd_steps, response, ends = chain_products(tiles, width)
+    fwd_steps, bwd_steps, chain, ends = chain_products(tiles, width)
     squares = sum_over(squares, [bits[n : n + 2] for n in range(3, len(bits), 2)])
     other_ends = lax.ppermute(ends, "line", flip(lines, 1))
     norm = jnp.sqrt(sum_over(squares, [bits[:1]]))
@@ -727,6 +741,7 @@
         ends, other_ends, width
     )
     far_maps = lax.ppermute(message, "line", flip(lines, 2))
+    response = response_layout(chain, right_side.shape[0])
     sweeps = (fwd_steps, bwd_steps)
     pairs = (through_high, reach_high, back_low)
     rest = (through_low, reach_high, back_high, before, far_maps, response)

time: 97.2 us -> 93.5 us (0.962)
  waiting for transfers between devices: 31.6 us -> 26.7 us
  starting transfers between devices: 34.8 us -> 35.9 us
    ppermute x3, starting transfers between devices: 10.4 us -> 13.5 us  [finish_solve(): got_a = lax.ppermute(sent, 'dom', flip(doms, 1))]
    ppermute x3, waiting for transfers between devices: 9.43 us -> 6.61 us  [finish_solve(): pair_far = lax.ppermute(pair_own, 'line', flip(lines, 2))]
    ppermute x14, starting transfers between devices: 19.3 us -> 16.5 us  [sum_over(): lax.ppermute(value, axes, flip(total, m))]
    ppermute x14, waiting for transfers between devices: 16.1 us -> 13.6 us  [sum_over(): lax.ppermute(value, axes, flip(total, m))]
    pallas_call x0 -> x1, Pallas kernels: none -> 2.15 us  [response_layout(): pl.pallas_call(response_kernel, out_shape=jax.ShapeDtypeStruct((size, 2 *...]
    pallas_call x1, Pallas kernels: 7.57 us -> 5.46 us  [chain_products(): pl.pallas_call(functools.partial(chain_kernel, width, size), out_shape=(s...]
  transfers between devices with their start and end apart: 28 -> 28, of which waited for: 18 -> 19; matrix products, arithmetic and copies ran while one was open for 0% -> 0% of each run, Pallas kernels for 7% -> 9%
where the time goes in v3:
time: 93.5 us; the launch traced here: 93.4 us
  starting transfers between devices  35.9 us (38%)
  Pallas kernels  28.8 us (31%)
  waiting for transfers between devices  26.7 us (29%)
  between operations  0.97 us (1%)
    ppermute x14, starting transfers between devices, sum_over(): lax.ppermute(value, axes, flip(total, m))  16.5 us
    ppermute x14, waiting for transfers between devices, sum_over(): lax.ppermute(value, axes, flip(total, m))  13.6 us
    ppermute x3, starting transfers between devices, finish_solve(): got_a = lax.ppermute(sent, 'dom', flip(doms, 1))  13.5 us
    ppermute x3, waiting for transfers between devices, finish_solve(): pair_far = lax.ppermute(pair_own, 'line', flip(lines, 2))  6.61 us
    pallas_call x2, Pallas kernels, advance(): pl.pallas_call(functools.partial(advance_kernel, width, rounded), out_sha...  6.29 us
    pallas_call x1, Pallas kernels, chain_products(): pl.pallas_call(functools.partial(chain_kernel, width, size), out_shape=(s...  5.46 us
    pallas_call x1, Pallas kernels, tile_layouts(): pl.pallas_call(tiles_kernel, out_shape=jax.ShapeDtypeStruct((elements * s...  3.4 us
    ppermute x3, waiting for transfers between devices, finish_solve(): ends_other = lax.ppermute(ends_own, 'line', flip(lines, 1))  3.32 us
  transfers between devices with their start and end apart: 28, of which 19 were waited for; matrix products, arithmetic and copies ran while one was open for 0% of the time, Pallas kernels for 9%

profile of v3, /device:TPU:0, one launch (start us, length us, event | category | flops | bytes accessed | tf_op | source)
XLA Modules:
  0.0 93.4 jit_solution(8729926243205760052)
XLA Ops:
  0.6 3.4 %tile_layouts.3.tiles = f32[8192,128]{1,0:T(8,128)S(1)} custom-call(bf16[64,64,128]{2,1,0:T(8,128)(2,1)} %fwd.1, bf16[64,64,128]{2,1,0:T(8,128)(2,1)} %bwd.1), custom_call_target="tpu_custom_call" | custom-call | flops 4000000 | bytes 10485760 | tf_op jit(solution)/shard_map/tile_layouts/pallas_call | solution.py:141
  4.0 5.5 %chain_products.3 = (bf16[8,8,64,128]{3,2,1,0:T(8,128)(2,1)S(1)}, bf16[8,8,64,128]{3,2,1,0:T(8,128)(2,1)S(1)}, f32[8192,128]{1,0:T(8,128)S(1)}, f32[32,64,128]{2,1,0:T(8,128)S(1)}) custom-call(f32[8192,128]{1,0:T(8,128)S(1)} %tile_layouts.3.tiles), custom_call_target="tpu_custom_call" | custom-call | flops 40000000 | bytes 12582912 | tf_op jit(solution)/shard_map/chain_products/pallas_call | solution.py:269
  10.2 3.4 %collective-permute-start.68 = (f32[8,128]{1,0:T(8,128)S(1)}, f32[8,128]{1,0:T(8,128)S(1)}, u32[]{:S(2)}, u32[]{:S(2)}) collective-permute-start(f32[8,128]{1,0:T(8,128)S(1)} %sum_squares.3), channel_id=1, source_target_pairs={{0,6},{1,7},{2,4},{3,5},{4,2},{5,3},{6,0},{7,1},{8,14},{9,15},{10,... | collective-permute-start | bytes 12296 | tf_op jit(solution)/shard_map/ppermute | solution.py:720
  15.2 2.0 %collective-permute-done.67 = f32[8,128]{1,0:T(8,128)S(1)} collective-permute-done((f32[8,128]{1,0:T(8,128)S(1)}, f32[8,128]{1,0:T(8,128)S(1)}, u32[]{:S(2)}, u32[]{:S(2)}) %collective-permute-start.67) | collective-permute-done | bytes 4128 | tf_op jit(solution)/shard_map/ppermute | solution.py:720
  17.8 3.6 %collective-permute-start.71 = (f32[8,128]{1,0:T(8,128)S(1)}, f32[8,128]{1,0:T(8,128)S(1)}, u32[]{:S(2)}, u32[]{:S(2)}) collective-permute-start(f32[8,128]{1,0:T(8,128)S(1)} %add_add_fusion.5), channel_id=1, source_target_pairs={{0,24},{1,25},{2,26},{3,27},{4,28},{5,29},{6,30},{7,31},{8,16},{9,... | collective-permute-start | bytes 12296 | tf_op jit(solution)/shard_map/ppermute | solution.py:720
  22.2 1.7 %line_maps.3 = (f32[8,64,128]{2,1,0:T(8,128)S(1)}, f32[8,64,128]{2,1,0:T(8,128)S(1)}, f32[8,64,128]{2,1,0:T(8,128)S(1)}, f32[8,64,128]{2,1,0:T(8,128)S(1)}, f32[...) custom-call(f32[32,64,128]{2,1,0:T(8,128)S(1)} %get-tuple-element.103.own, ...), custom_call_target="tpu_custom_call" | custom-call | tf_op jit(solution)/shard_map/line_maps/pallas_call | solution.py:345
  24.3 1.6 %collective-permute-done.70 = f32[8,128]{1,0:T(8,128)S(1)} collective-permute-done((f32[8,128]{1,0:T(8,128)S(1)}, f32[8,128]{1,0:T(8,128)S(1)}, u32[]{:S(2)}, u32[]{:S(2)}) %collective-permute-start.70) | collective-permute-done | bytes 4128 | tf_op jit(solution)/shard_map/ppermute | solution.py:720
  26.0 1.2 %collective-permute-done.72 = f32[8,128]{1,0:T(8,128)S(1)} collective-permute-done((f32[8,128]{1,0:T(8,128)S(1)}, f32[8,128]{1,0:T(8,128)S(1)}, u32[]{:S(2)}, u32[]{:S(2)}) %collective-permute-start.72) | collective-permute-done | bytes 4128 | tf_op jit(solution)/shard_map/ppermute | solution.py:720
  27.1 2.0 %line_sweep.7 = (f32[64,128]{1,0:T(8,128)S(1)}, f32[16,128]{1,0:T(8,128)S(1)}, f32[64,128]{1,0:T(8,128)S(1)}) custom-call(f32[64,128]{1,0:T(8,128)S(1)} %copy-done.7, f32[8,128]{1,0:T(8,128)S(1)} %add_sqrt_fusion.4.norm, bf16[64,64,128]{2,1,0:T(8,128)(2,1)S(1)} %copy-done.1, bf16[8,8,64,128]{3,2,1,0:T(8,128)(2,1)S(1)} %get-tuple-element.100.fwd_steps, ...), custom_call_target="tpu_custom_call" | custom-call | tf_op jit(solution)/shard_map/line_sweep/pallas_call | solution.py:390
  31.2 2.1 %response_layout.3.response = f32[64,128,128]{2,1,0:T(8,128)S(1)} custom-call(f32[8192,128]{1,0:T(8,128)S(1)} %get-tuple-element.112.chain), custom_call_target="tpu_custom_call" | custom-call | flops 4000000 | bytes 8388608 | tf_op jit(solution)/shard_map/response_layout/pallas_call | solution.py:256
  36.1 3.2 %collective-permute-start.77 = (f32[64,32]{1,0:T(8,128)S(1)}, f32[64,32]{1,0:T(8,128)S(1)}, u32[]{:S(2)}, u32[]{:S(2)}) collective-permute-start(f32[64,32]{1,0:T(8,128)S(1)} %get-tuple-element.114), channel_id=1, source_target_pairs={{0,4},{4,0},{8,12},{12,8},{16,20},{20,16},{24,28},{28,24},{1,5},{5... | collective-permute-start | bytes 24584 | tf_op jit(solution)/shard_map/ppermute | solution.py:759
  40.1 1.1 %collective-permute-done.77.got_a = f32[64,32]{1,0:T(8,128)S(1)} collective-permute-done((f32[64,32]{1,0:T(8,128)S(1)}, f32[64,32]{1,0:T(8,128)S(1)}, u32[]{:S(2)}, u32[]{:S(2)}) %collective-permute-start.77) | collective-permute-done | bytes 8224 | tf_op jit(solution)/shard_map/ppermute | solution.py:759
  41.1 3.1 %faces_and_sweep.8 = (f32[64,128]{1,0:T(8,128)S(1)}, f32[16,128]{1,0:T(8,128)S(1)}, f32[64,128]{1,0:T(8,128)S(1)}) custom-call(f32[64,128]{1,0:T(8,128)S(1)} %get-tuple-element.113.vector.rest_0_, f32[64,32]{1,0:T(8,128)S(1)} %collective-permute-done.77.got_a, f32[64,32]{1,0:T(8,128)S(1)} %collective-permute-done.78.got_b, s32[4,128]{1,0:T(4,128)S(1)} %copy-done.8, ...), custom_call_target="tpu_custom_call" | custom-call | tf_op jit(solution)/shard_map/faces_and_sweep/pallas_call | solution.py:571
  44.3 1.2 %collective-permute-done.79.other = f32[16,128]{1,0:T(8,128)S(1)} collective-permute-done((f32[16,128]{1,0:T(8,128)S(1)}, f32[16,128]{1,0:T(8,128)S(1)}, u32[]{:S(2)}, u32[]{:S(2)}) %collective-permute-start.79) | collective-permute-done | bytes 8224 | tf_op jit(solution)/shard_map/ppermute | solution.py:753
  45.7 1.0 %collective-permute-start.80 = (f32[16,128]{1,0:T(8,128)S(1)}, f32[16,128]{1,0:T(8,128)S(1)}, u32[]{:S(2)}, u32[]{:S(2)}) collective-permute-start(f32[16,128]{1,0:T(8,128)S(1)} %line_pair.10.pair), channel_id=1, source_target_pairs={{0,2},{1,3},{2,0},{3,1},{4,6},{5,7},{6,4},{7,5},{8,10},{9,11},{10,... | collective-permute-start | bytes 24584 | tf_op jit(solution)/shard_map/ppermute | solution.py:755
  46.8 2.7 %collective-permute-done.80.far = f32[16,128]{1,0:T(8,128)S(1)} collective-permute-done((f32[16,128]{1,0:T(8,128)S(1)}, f32[16,128]{1,0:T(8,128)S(1)}, u32[]{:S(2)}, u32[]{:S(2)}) %collective-permute-start.80) | collective-permute-done | bytes 8224 | tf_op jit(solution)/shard_map/ppermute | solution.py:755
  51.0 5.9 %collective-permute-start.81 = (f32[64,32]{1,0:T(8,128)S(1)}, f32[64,32]{1,0:T(8,128)S(1)}, u32[]{:S(2)}, u32[]{:S(2)}) collective-permute-start(f32[64,32]{1,0:T(8,128)S(1)} %get-tuple-element.119), channel_id=1, source_target_pairs={{0,4},{4,0},{8,12},{12,8},{16,20},{20,16},{24,28},{28,24},{1,5},{5... | collective-permute-start | bytes 24584 | tf_op jit(solution)/shard_map/ppermute | solution.py:759
  57.7 1.1 %collective-permute-done.81.got_a = f32[64,32]{1,0:T(8,128)S(1)} collective-permute-done((f32[64,32]{1,0:T(8,128)S(1)}, f32[64,32]{1,0:T(8,128)S(1)}, u32[]{:S(2)}, u32[]{:S(2)}) %collective-permute-start.81) | collective-permute-done | bytes 8224 | tf_op jit(solution)/shard_map/ppermute | solution.py:759
  58.8 3.2 %faces_and_sweep.9 = (f32[64,128]{1,0:T(8,128)S(1)}, f32[16,128]{1,0:T(8,128)S(1)}, f32[64,128]{1,0:T(8,128)S(1)}) custom-call(f32[64,128]{1,0:T(8,128)S(1)} %get-tuple-element.118.vector.rest_1_, f32[64,32]{1,0:T(8,128)S(1)} %collective-permute-done.81.got_a, f32[64,32]{1,0:T(8,128)S(1)} %collective-permute-done.82.got_b, s32[4,128]{1,0:T(4,128)S(1)} %copy-done.8, ...), custom_call_target="tpu_custom_call" | custom-call | tf_op jit(solution)/shard_map/faces_and_sweep/pallas_call | solution.py:571
  62.0 1.2 %collective-permute-done.83.other = f32[16,128]{1,0:T(8,128)S(1)} collective-permute-done((f32[16,128]{1,0:T(8,128)S(1)}, f32[16,128]{1,0:T(8,128)S(1)}, u32[]{:S(2)}, u32[]{:S(2)}) %collective-permute-start.83) | collective-permute-done | bytes 8224 | tf_op jit(solution)/shard_map/ppermute | solution.py:753
  64.2 2.9 %collective-permute-done.84.far = f32[16,128]{1,0:T(8,128)S(1)} collective-permute-done((f32[16,128]{1,0:T(8,128)S(1)}, f32[16,128]{1,0:T(8,128)S(1)}, u32[]{:S(2)}, u32[]{:S(2)}) %collective-permute-start.84) | collective-permute-done | bytes 8224 | tf_op jit(solution)/shard_map/ppermute | solution.py:755
  68.8 4.5 %collective-permute-start.85 = (f32[64,32]{1,0:T(8,128)S(1)}, f32[64,32]{1,0:T(8,128)S(1)}, u32[]{:S(2)}, u32[]{:S(2)}) collective-permute-start(f32[64,32]{1,0:T(8,128)S(1)} %get-tuple-element.124), channel_id=1, source_target_pairs={{0,4},{4,0},{8,12},{12,8},{16,20},{20,16},{24,28},{28,24},{1,5},{5... | collective-permute-start | bytes 24584 | tf_op jit(solution)/shard_map/ppermute | solution.py:759
  74.1 1.1 %collective-permute-done.85.got_a = f32[64,32]{1,0:T(8,128)S(1)} collective-permute-done((f32[64,32]{1,0:T(8,128)S(1)}, f32[64,32]{1,0:T(8,128)S(1)}, u32[]{:S(2)}, u32[]{:S(2)}) %collective-permute-start.85) | collective-permute-done | bytes 8224 | tf_op jit(solution)/shard_map/ppermute | solution.py:759
  75.2 1.2 %faces_and_sums.1 = f32[16,128]{1,0:T(8,128)S(1)} custom-call(f32[64,128]{1,0:T(8,128)S(1)} %get-tuple-element.123.vector.rest_2_, f32[64,32]{1,0:T(8,128)S(1)} %collective-permute-done.85.got_a, f32[64,32]{1,0:T(8,128)S(1)} %collective-permute-done.86.got_b, s32[4,128]{1,0:T(4,128)S(1)} %copy-done.8, f32[64,128]{1,0:T(8,128)S(1)} %near_faces.11.partial, ...), custom_call_target="tpu_custom_call" | custom-call | tf_op jit(solution)/shard_map/faces_and_sums/pallas_call | solution.py:604
  76.4 2.2 %collective-permute-start.89 = (f32[16,128]{1,0:T(8,128)S(1)}, f32[16,128]{1,0:T(8,128)S(1)}, u32[]{:S(2)}, u32[]{:S(2)}) collective-permute-start(f32[16,128]{1,0:T(8,128)S(1)} %faces_and_sums.1), channel_id=1, source_target_pairs={{0,6},{1,7},{2,4},{3,5},{4,2},{5,3},{6,0},{7,1},{8,14},{9,15},{10,... | collective-permute-start | bytes 24584 | tf_op jit(solution)/shard_map/ppermute | solution.py:720
  78.6 1.3 %collective-permute-start.87 = (f32[16,128]{1,0:T(8,128)S(1)}, f32[16,128]{1,0:T(8,128)S(1)}, u32[]{:S(2)}, u32[]{:S(2)}) collective-permute-start(f32[16,128]{1,0:T(8,128)S(1)} %faces_and_sums.1), channel_id=1, source_target_pairs={{0,2},{1,3},{2,0},{3,1},{4,6},{5,7},{6,4},{7,5},{8,10},{9,11},{10,... | collective-permute-start | bytes 24584 | tf_op jit(solution)/shard_map/ppermute | solution.py:720
  79.9 1.1 %collective-permute-done.89 = f32[16,128]{1,0:T(8,128)S(1)} collective-permute-done((f32[16,128]{1,0:T(8,128)S(1)}, f32[16,128]{1,0:T(8,128)S(1)}, u32[]{:S(2)}, u32[]{:S(2)}) %collective-permute-start.89) | collective-permute-done | bytes 8224 | tf_op jit(solution)/shard_map/ppermute | solution.py:720
  81.0 1.3 %collective-permute-done.88 = f32[16,128]{1,0:T(8,128)S(1)} collective-permute-done((f32[16,128]{1,0:T(8,128)S(1)}, f32[16,128]{1,0:T(8,128)S(1)}, u32[]{:S(2)}, u32[]{:S(2)}) %collective-permute-start.88) | collective-permute-done | bytes 8224 | tf_op jit(solution)/shard_map/ppermute | solution.py:720
  82.3 3.7 %collective-permute-start.92 = (f32[16,128]{1,0:T(8,128)S(1)}, f32[16,128]{1,0:T(8,128)S(1)}, u32[]{:S(2)}, u32[]{:S(2)}) collective-permute-start(f32[16,128]{1,0:T(8,128)S(1)} %add_add_fusion.3), channel_id=1, source_target_pairs={{0,24},{1,25},{2,26},{3,27},{4,28},{5,29},{6,30},{7,31},{8,16},{9,... | collective-permute-start | bytes 24584 | tf_op jit(solution)/shard_map/ppermute | solution.py:720
  86.7 1.1 %collective-permute-done.92 = f32[16,128]{1,0:T(8,128)S(1)} collective-permute-done((f32[16,128]{1,0:T(8,128)S(1)}, f32[16,128]{1,0:T(8,128)S(1)}, u32[]{:S(2)}, u32[]{:S(2)}) %collective-permute-start.92) | collective-permute-done | bytes 8224 | tf_op jit(solution)/shard_map/ppermute | solution.py:720
  87.8 2.8 %collective-permute-done.91 = f32[16,128]{1,0:T(8,128)S(1)} collective-permute-done((f32[16,128]{1,0:T(8,128)S(1)}, f32[16,128]{1,0:T(8,128)S(1)}, u32[]{:S(2)}, u32[]{:S(2)}) %collective-permute-start.91) | collective-permute-done | bytes 8224 | tf_op jit(solution)/shard_map/ppermute | solution.py:720
  90.6 1.2 %collective-permute-done.93 = f32[16,128]{1,0:T(8,128)S(1)} collective-permute-done((f32[16,128]{1,0:T(8,128)S(1)}, f32[16,128]{1,0:T(8,128)S(1)}, u32[]{:S(2)}, u32[]{:S(2)}) %collective-permute-start.93) | collective-permute-done | bytes 8224 | tf_op jit(solution)/shard_map/ppermute | solution.py:720
  (72 shorter events, 18.1 us)
Async XLA Ops:
  0.6 9.5 %copy-start.7 = (f32[64,128]{1,0:T(8,128)S(1)}, f32[64,128]{1,0:T(8,128)}, u32[]{:S(2)}) copy-start(f32[64,128]{1,0:T(8,128)} %right_side.1) | copy-start | bytes 98308
  9.5 17.6 %copy-start.1 = (bf16[64,64,128]{2,1,0:T(8,128)(2,1)S(1)}, bf16[64,64,128]{2,1,0:T(8,128)(2,1)}, u32[]{:S(2)}) copy-start(bf16[64,64,128]{2,1,0:T(8,128)(2,1)} %inv.5) | copy-start | bytes 3145732
  9.5 12.6 %collective-permute-start.74 = (f32[32,64,128]{2,1,0:T(8,128)S(1)}, f32[32,64,128]{2,1,0:T(8,128)S(1)}, u32[]{:S(2)}, u32[]{:S(2)}) collective-permute-start(f32[32,64,128]{2,1,0:T(8,128)S(1)} %get-tuple-element.103.own), channel_id=1, source_target_pairs={{0,1},{1,0},{2,3},{3,2},{4,5},{5,4},{6,7},{7,6},{8,9},{9,8},{10,11... | collective-permute-start | bytes 3145736 | tf_op jit(solution)/shard_map/ppermute | solution.py:738
  10.2 5.0 %collective-permute-start.68 = (f32[8,128]{1,0:T(8,128)S(1)}, f32[8,128]{1,0:T(8,128)S(1)}, u32[]{:S(2)}, u32[]{:S(2)}) collective-permute-start(f32[8,128]{1,0:T(8,128)S(1)} %sum_squares.3), channel_id=1, source_target_pairs={{0,6},{1,7},{2,4},{3,5},{4,2},{5,3},{6,0},{7,1},{8,14},{9,15},{10,... | collective-permute-start | bytes 12296 | tf_op jit(solution)/shard_map/ppermute | solution.py:720
  13.6 3.6 %collective-permute-start.67 = (f32[8,128]{1,0:T(8,128)S(1)}, f32[8,128]{1,0:T(8,128)S(1)}, u32[]{:S(2)}, u32[]{:S(2)}) collective-permute-start(f32[8,128]{1,0:T(8,128)S(1)} %sum_squares.3), channel_id=1, source_target_pairs={{0,4},{1,5},{2,6},{3,7},{4,0},{5,1},{6,2},{7,3},{8,12},{9,13},{10,... | collective-permute-start | bytes 12296 | tf_op jit(solution)/shard_map/ppermute | solution.py:720
  14.2 3.6 %collective-permute-start.66 = (f32[8,128]{1,0:T(8,128)S(1)}, f32[8,128]{1,0:T(8,128)S(1)}, u32[]{:S(2)}, u32[]{:S(2)}) collective-permute-start(f32[8,128]{1,0:T(8,128)S(1)} %sum_squares.3), channel_id=1, source_target_pairs={{0,2},{1,3},{2,0},{3,1},{4,6},{5,7},{6,4},{7,5},{8,10},{9,11},{10,... | collective-permute-start | bytes 12296 | tf_op jit(solution)/shard_map/ppermute | solution.py:720
  17.8 6.5 %collective-permute-start.71 = (f32[8,128]{1,0:T(8,128)S(1)}, f32[8,128]{1,0:T(8,128)S(1)}, u32[]{:S(2)}, u32[]{:S(2)}) collective-permute-start(f32[8,128]{1,0:T(8,128)S(1)} %add_add_fusion.5), channel_id=1, source_target_pairs={{0,24},{1,25},{2,26},{3,27},{4,28},{5,29},{6,30},{7,31},{8,16},{9,... | collective-permute-start | bytes 12296 | tf_op jit(solution)/shard_map/ppermute | solution.py:720
  21.4 4.5 %collective-permute-start.70 = (f32[8,128]{1,0:T(8,128)S(1)}, f32[8,128]{1,0:T(8,128)S(1)}, u32[]{:S(2)}, u32[]{:S(2)}) collective-permute-start(f32[8,128]{1,0:T(8,128)S(1)} %add_add_fusion.5), channel_id=1, source_target_pairs={{0,16},{1,17},{2,18},{3,19},{4,20},{5,21},{6,22},{7,23},{8,24},{9,... | collective-permute-start | bytes 12296 | tf_op jit(solution)/shard_map/ppermute | solution.py:720
  21.4 4.5 %collective-permute-start.69 = (f32[8,128]{1,0:T(8,128)S(1)}, f32[8,128]{1,0:T(8,128)S(1)}, u32[]{:S(2)}, u32[]{:S(2)}) collective-permute-start(f32[8,128]{1,0:T(8,128)S(1)} %add_add_fusion.5), channel_id=1, source_target_pairs={{0,8},{1,9},{2,10},{3,11},{4,12},{5,13},{6,14},{7,15},{8,0},{9,1},... | collective-permute-start | bytes 12296 | tf_op jit(solution)/shard_map/ppermute | solution.py:720
  23.9 10.5 %collective-permute-start.76 = (bf16[24,64,128]{2,1,0:T(8,128)(2,1)S(1)}, bf16[24,64,128]{2,1,0:T(8,128)(2,1)S(1)}, u32[]{:S(2)}, u32[]{:S(2)}) collective-permute-start(bf16[24,64,128]{2,1,0:T(8,128)(2,1)S(1)} %get-tuple-element.111), channel_id=1, source_target_pairs={{0,2},{1,3},{2,0},{3,1},{4,6},{5,7},{6,4},{7,5},{8,10},{9,11},{10,... | collective-permute-start | bytes 1179656 | tf_op jit(solution)/shard_map/ppermute | solution.py:743
  25.9 1.2 %collective-permute-start.72 = (f32[8,128]{1,0:T(8,128)S(1)}, f32[8,128]{1,0:T(8,128)S(1)}, u32[]{:S(2)}, u32[]{:S(2)}) collective-permute-start(f32[8,128]{1,0:T(8,128)S(1)} %add_add_fusion.4), channel_id=1, source_target_pairs={{0,1},{1,0},{2,3},{3,2},{4,5},{5,4},{6,7},{7,6},{8,9},{9,8},{10,11... | collective-permute-start | bytes 12296 | tf_op jit(solution)/shard_map/ppermute | solution.py:720
  29.2 1.2 %collective-permute-start.73 = (f32[16,128]{1,0:T(8,128)S(1)}, f32[16,128]{1,0:T(8,128)S(1)}, u32[]{:S(2)}, u32[]{:S(2)}) collective-permute-start(f32[16,128]{1,0:T(8,128)S(1)} %get-tuple-element.102.own), channel_id=1, source_target_pairs={{0,1},{1,0},{2,3},{3,2},{4,5},{5,4},{6,7},{7,6},{8,9},{9,8},{10,11... | collective-permute-start | bytes 24584 | tf_op jit(solution)/shard_map/ppermute | solution.py:753
  30.6 3.7 %collective-permute-start.75 = (f32[16,128]{1,0:T(8,128)S(1)}, f32[16,128]{1,0:T(8,128)S(1)}, u32[]{:S(2)}, u32[]{:S(2)}) collective-permute-start(f32[16,128]{1,0:T(8,128)S(1)} %line_pair.9.pair), channel_id=1, source_target_pairs={{0,2},{1,3},{2,0},{3,1},{4,6},{5,7},{6,4},{7,5},{8,10},{9,11},{10,... | collective-permute-start | bytes 24584 | tf_op jit(solution)/shard_map/ppermute | solution.py:755
  35.2 4.8 %collective-permute-start.78 = (f32[64,32]{1,0:T(8,128)S(1)}, f32[64,32]{1,0:T(8,128)S(1)}, u32[]{:S(2)}, u32[]{:S(2)}) collective-permute-start(f32[64,32]{1,0:T(8,128)S(1)} %get-tuple-element.114), channel_id=1, source_target_pairs={{0,0},{4,8},{8,4},{12,16},{16,12},{20,24},{24,20},{28,28},{1,1},{5... | collective-permute-start | bytes 24584 | tf_op jit(solution)/shard_map/ppermute | solution.py:760
  36.1 5.1 %collective-permute-start.77 = (f32[64,32]{1,0:T(8,128)S(1)}, f32[64,32]{1,0:T(8,128)S(1)}, u32[]{:S(2)}, u32[]{:S(2)}) collective-permute-start(f32[64,32]{1,0:T(8,128)S(1)} %get-tuple-element.114), channel_id=1, source_target_pairs={{0,4},{4,0},{8,12},{12,8},{16,20},{20,16},{24,28},{28,24},{1,5},{5... | collective-permute-start | bytes 24584 | tf_op jit(solution)/shard_map/ppermute | solution.py:759
  44.3 1.2 %collective-permute-start.79 = (f32[16,128]{1,0:T(8,128)S(1)}, f32[16,128]{1,0:T(8,128)S(1)}, u32[]{:S(2)}, u32[]{:S(2)}) collective-permute-start(f32[16,128]{1,0:T(8,128)S(1)} %get-tuple-element.116.own), channel_id=1, source_target_pairs={{0,1},{1,0},{2,3},{3,2},{4,5},{5,4},{6,7},{7,6},{8,9},{9,8},{10,11... | collective-permute-start | bytes 24584 | tf_op jit(solution)/shard_map/ppermute | solution.py:753
  45.7 3.7 %collective-permute-start.80 = (f32[16,128]{1,0:T(8,128)S(1)}, f32[16,128]{1,0:T(8,128)S(1)}, u32[]{:S(2)}, u32[]{:S(2)}) collective-permute-start(f32[16,128]{1,0:T(8,128)S(1)} %line_pair.10.pair), channel_id=1, source_target_pairs={{0,2},{1,3},{2,0},{3,1},{4,6},{5,7},{6,4},{7,5},{8,10},{9,11},{10,... | collective-permute-start | bytes 24584 | tf_op jit(solution)/shard_map/ppermute | solution.py:755
  50.3 7.4 %collective-permute-start.82 = (f32[64,32]{1,0:T(8,128)S(1)}, f32[64,32]{1,0:T(8,128)S(1)}, u32[]{:S(2)}, u32[]{:S(2)}) collective-permute-start(f32[64,32]{1,0:T(8,128)S(1)} %get-tuple-element.119), channel_id=1, source_target_pairs={{0,0},{4,8},{8,4},{12,16},{16,12},{20,24},{24,20},{28,28},{1,1},{5... | collective-permute-start | bytes 24584 | tf_op jit(solution)/shard_map/ppermute | solution.py:760
  51.0 7.8 %collective-permute-start.81 = (f32[64,32]{1,0:T(8,128)S(1)}, f32[64,32]{1,0:T(8,128)S(1)}, u32[]{:S(2)}, u32[]{:S(2)}) collective-permute-start(f32[64,32]{1,0:T(8,128)S(1)} %get-tuple-element.119), channel_id=1, source_target_pairs={{0,4},{4,0},{8,12},{12,8},{16,20},{20,16},{24,28},{28,24},{1,5},{5... | collective-permute-start | bytes 24584 | tf_op jit(solution)/shard_map/ppermute | solution.py:759
  61.9 1.2 %collective-permute-start.83 = (f32[16,128]{1,0:T(8,128)S(1)}, f32[16,128]{1,0:T(8,128)S(1)}, u32[]{:S(2)}, u32[]{:S(2)}) collective-permute-start(f32[16,128]{1,0:T(8,128)S(1)} %get-tuple-element.121.own), channel_id=1, source_target_pairs={{0,1},{1,0},{2,3},{3,2},{4,5},{5,4},{6,7},{7,6},{8,9},{9,8},{10,11... | collective-permute-start | bytes 24584 | tf_op jit(solution)/shard_map/ppermute | solution.py:753
  63.4 3.7 %collective-permute-start.84 = (f32[16,128]{1,0:T(8,128)S(1)}, f32[16,128]{1,0:T(8,128)S(1)}, u32[]{:S(2)}, u32[]{:S(2)}) collective-permute-start(f32[16,128]{1,0:T(8,128)S(1)} %line_pair.11.pair), channel_id=1, source_target_pairs={{0,2},{1,3},{2,0},{3,1},{4,6},{5,7},{6,4},{7,5},{8,10},{9,11},{10,... | collective-permute-start | bytes 24584 | tf_op jit(solution)/shard_map/ppermute | solution.py:755
  68.0 24.5 %copy-start.5 = (bf16[64,64,128]{2,1,0:T(8,128)(2,1)S(1)}, bf16[64,64,128]{2,1,0:T(8,128)(2,1)}, u32[]{:S(2)}) copy-start(bf16[64,64,128]{2,1,0:T(8,128)(2,1)} %fwd.1) | copy-start | bytes 3145732
  68.0 24.5 %copy-start.6 = (bf16[64,64,128]{2,1,0:T(8,128)(2,1)S(1)}, bf16[64,64,128]{2,1,0:T(8,128)(2,1)}, u32[]{:S(2)}) copy-start(bf16[64,64,128]{2,1,0:T(8,128)(2,1)} %bwd.1) | copy-start | bytes 3145732
  68.0 6.1 %collective-permute-start.86 = (f32[64,32]{1,0:T(8,128)S(1)}, f32[64,32]{1,0:T(8,128)S(1)}, u32[]{:S(2)}, u32[]{:S(2)}) collective-permute-start(f32[64,32]{1,0:T(8,128)S(1)} %get-tuple-element.124), channel_id=1, source_target_pairs={{0,0},{4,8},{8,4},{12,16},{16,12},{20,24},{24,20},{28,28},{1,1},{5... | collective-permute-start | bytes 24584 | tf_op jit(solution)/shard_map/ppermute | solution.py:760
  68.8 6.4 %collective-permute-start.85 = (f32[64,32]{1,0:T(8,128)S(1)}, f32[64,32]{1,0:T(8,128)S(1)}, u32[]{:S(2)}, u32[]{:S(2)}) collective-permute-start(f32[64,32]{1,0:T(8,128)S(1)} %get-tuple-element.124), channel_id=1, source_target_pairs={{0,4},{4,0},{8,12},{12,8},{16,20},{20,16},{24,28},{28,24},{1,5},{5... | collective-permute-start | bytes 24584 | tf_op jit(solution)/shard_map/ppermute | solution.py:759
  76.4 4.6 %collective-permute-start.89 = (f32[16,128]{1,0:T(8,128)S(1)}, f32[16,128]{1,0:T(8,128)S(1)}, u32[]{:S(2)}, u32[]{:S(2)}) collective-permute-start(f32[16,128]{1,0:T(8,128)S(1)} %faces_and_sums.1), channel_id=1, source_target_pairs={{0,6},{1,7},{2,4},{3,5},{4,2},{5,3},{6,0},{7,1},{8,14},{9,15},{10,... | collective-permute-start | bytes 24584 | tf_op jit(solution)/shard_map/ppermute | solution.py:720
  78.6 3.7 %collective-permute-start.88 = (f32[16,128]{1,0:T(8,128)S(1)}, f32[16,128]{1,0:T(8,128)S(1)}, u32[]{:S(2)}, u32[]{:S(2)}) collective-permute-start(f32[16,128]{1,0:T(8,128)S(1)} %faces_and_sums.1), channel_id=1, source_target_pairs={{0,4},{1,5},{2,6},{3,7},{4,0},{5,1},{6,2},{7,3},{8,12},{9,13},{10,... | collective-permute-start | bytes 24584 | tf_op jit(solution)/shard_map/ppermute | solution.py:720
  78.6 3.7 %collective-permute-start.87 = (f32[16,128]{1,0:T(8,128)S(1)}, f32[16,128]{1,0:T(8,128)S(1)}, u32[]{:S(2)}, u32[]{:S(2)}) collective-permute-start(f32[16,128]{1,0:T(8,128)S(1)} %faces_and_sums.1), channel_id=1, source_target_pairs={{0,2},{1,3},{2,0},{3,1},{4,6},{5,7},{6,4},{7,5},{8,10},{9,11},{10,... | collective-permute-start | bytes 24584 | tf_op jit(solution)/shard_map/ppermute | solution.py:720
  82.3 5.5 %collective-permute-start.92 = (f32[16,128]{1,0:T(8,128)S(1)}, f32[16,128]{1,0:T(8,128)S(1)}, u32[]{:S(2)}, u32[]{:S(2)}) collective-permute-start(f32[16,128]{1,0:T(8,128)S(1)} %add_add_fusion.3), channel_id=1, source_target_pairs={{0,24},{1,25},{2,26},{3,27},{4,28},{5,29},{6,30},{7,31},{8,16},{9,... | collective-permute-start | bytes 24584 | tf_op jit(solution)/shard_map/ppermute | solution.py:720
  86.0 4.5 %collective-permute-start.91 = (f32[16,128]{1,0:T(8,128)S(1)}, f32[16,128]{1,0:T(8,128)S(1)}, u32[]{:S(2)}, u32[]{:S(2)}) collective-permute-start(f32[16,128]{1,0:T(8,128)S(1)} %add_add_fusion.3), channel_id=1, source_target_pairs={{0,16},{1,17},{2,18},{3,19},{4,20},{5,21},{6,22},{7,23},{8,24},{9,... | collective-permute-start | bytes 24584 | tf_op jit(solution)/shard_map/ppermute | solution.py:720
  86.1 4.5 %collective-permute-start.90 = (f32[16,128]{1,0:T(8,128)S(1)}, f32[16,128]{1,0:T(8,128)S(1)}, u32[]{:S(2)}, u32[]{:S(2)}) collective-permute-start(f32[16,128]{1,0:T(8,128)S(1)} %add_add_fusion.3), channel_id=1, source_target_pairs={{0,8},{1,9},{2,10},{3,11},{4,12},{5,13},{6,14},{7,15},{8,0},{9,1},... | collective-permute-start | bytes 24584 | tf_op jit(solution)/shard_map/ppermute | solution.py:720
  90.6 1.2 %collective-permute-start.93 = (f32[16,128]{1,0:T(8,128)S(1)}, f32[16,128]{1,0:T(8,128)S(1)}, u32[]{:S(2)}, u32[]{:S(2)}) collective-permute-start(f32[16,128]{1,0:T(8,128)S(1)} %add_add_fusion.2), channel_id=1, source_target_pairs={{0,1},{1,0},{2,3},{3,2},{4,5},{5,4},{6,7},{7,6},{8,9},{9,8},{10,11... | collective-permute-start | bytes 24584 | tf_op jit(solution)/shard_map/ppermute | solution.py:720
  (7 other events, 35.1 us)
